TPU v7x, 256 devices: a whole 4x4x8 slice. The times are simulated.
256 devices in a mesh: section: 16 (over z_lo, y), ctx: 4 (over x), tensor: 4 (over z_hi, core).
Axes of the slice: x: 4, y: 4, z: 8 (z_hi: 2, z_lo: 4; z = z_hi * 4 + z_lo), core: 2. Of those that a mesh axis runs over, the one named last changes fastest.
Arguments:
- arriving: bfloat16 [16, 1024, 4096], P('section', 'ctx', 'tensor')
- stored: bfloat16 [16, 1024, 4096], P('section', 'ctx', 'tensor')
- docs_forward: int32 [16, 1024], P('section', 'ctx'), may hold values from 0 to 3, never falling along the last dimension, each value on 1 to 512 neighbouring positions
- docs_backward: int32 [16, 1024], P('section', 'ctx'), may hold values from 0 to 3, never falling along the last dimension, each value on 1 to 512 neighbouring positions
- norm_gain: bfloat16 [16, 4096], P('section')
- query_weight: bfloat16 [16, 4096, 4096], P('section', 'ctx', 'tensor')
- key_weight: bfloat16 [16, 4096, 512], P('section', 'ctx', 'tensor')
- value_projection_weight: bfloat16 [16, 4096, 512], P('section', 'ctx', 'tensor'), may hold values from -0.09375 to 0.09375
- out_weight: bfloat16 [16, 4096, 4096], P('section', 'tensor', 'ctx'), may hold values from -0.375 to 0.375
Outputs:
- forward_output: bfloat16 [16, 1024, 4096], P('section', 'ctx', 'tensor')
- stashed: bfloat16 [16, 1024, 4096], P('section', 'ctx', 'tensor')
- rebuilt: bfloat16 [16, 1024, 4096], P('section', 'ctx', 'tensor')
Inputs may be any that keep to these rules, and one draw needn't show every extreme that they name: `docs_forward`: each row holds 4 packed documents: ids never fall, each document has 1 to 512 tokens, one exactly 512. `docs_backward`: each row holds 4 packed documents: ids never fall, each document has 1 to 512 tokens, one exactly 512.
All inputs are finite; a program needn't handle non-finite values.
Results may differ from a plain program's by a relative error of at most 0.0066.
Values may be sent and summed in bfloat16 or wider, within the bound.
No kernel may reach another device: no remote copies, remote signals or barrier semaphores. Data moves between devices by JAX's collectives and lax.ppermute only.
A program may use at most 128 MiB of HBM per device.

v0:
```python
import functools
import math

import jax
import jax.numpy as jnp
from jax import lax
from jax.experimental import pallas as pl
from jax.experimental.pallas import tpu as pltpu
from jax.sharding import PartitionSpec as P

HEAD = 128
norm_epsilon = 1e-05
rope_base = 500000.0
BF = jnp.bfloat16
F32 = jnp.float32
STRIPS = (5, 3)


def after(value, *earlier):
    return lax.optimization_barrier((value,) + earlier)[0]


def z_route(step, sections, tensors):
    low_count = 4
    rows = sections // low_count
    cores = 2
    high_count = tensors // cores
    depth = low_count * high_count
    route = []
    for z in range(depth):
        origin = (z + step) % depth
        for y in range(rows):
            for core in range(cores):
                source = ((origin % low_count) * rows + y) * tensors + (origin // low_count) * cores + core
                target = ((z % low_count) * rows + y) * tensors + (z // low_count) * cores + core
                route.append((source, target))
    return route


def from_z(block, step):
    route = z_route(step, lax.axis_size("section"), lax.axis_size("tensor"))
    return lax.ppermute(block, ("section", "tensor"), route)


def from_x(block, step):
    count = lax.axis_size("ctx")
    return lax.ppermute(block, "ctx", [((c + step) % count, c) for c in range(count)])


def from_before(block, step):
    count = lax.axis_size("ctx")
    return lax.ppermute(block, "ctx", [(c - step, c) for c in range(step, count)])


def from_tensor(block, flip):
    count = lax.axis_size("tensor")
    return lax.ppermute(block, "tensor", [(t, t ^ flip) for t in range(count)])


def first_hop(shard):
    return from_x(shard, 1), from_x(shard, -1)


def second_hop(ahead, behind):
    half = ahead.shape[0] // 2
    return from_x(ahead[:half], 1), from_x(behind[half:], -1)


def rope_tables(rows):
    half = HEAD // 2
    exponent = jnp.arange(half).astype(F32) * (2.0 / HEAD)
    inverse = jnp.exp(-exponent * math.log(rope_base))
    positions = lax.axis_index("ctx") * rows + jnp.arange(rows, dtype=jnp.int32)
    angles = positions.astype(F32)[:, None] * inverse[None, :]
    cosine = jnp.cos(angles)
    sine = jnp.sin(angles)
    return jnp.concatenate((cosine, cosine), axis=1), jnp.concatenate((-sine, sine), axis=1)


def normalize_kernel(*refs):
    block_refs, gain_ref, out_ref = refs[:8], refs[8], refs[9]
    for batch in range(2):
        blocks = [ref[...].astype(F32) for ref in block_refs[4 * batch : 4 * batch + 4]]
        total = sum(jnp.sum(block * block, axis=1, keepdims=True) for block in blocks)
        scale = lax.rsqrt(total * (1.0 / (blocks[0].shape[1] * len(blocks))) + norm_epsilon)
        for flip, block in enumerate(blocks):
            gain = gain_ref[flip : flip + 1].astype(F32)
            out_ref[flip, batch] = (block * scale * gain).astype(BF)


def normalize(blocks, gains, rows):
    width = gains.shape[1]
    step = 64
    split = [
        pl.BlockSpec((step, width), functools.partial(lambda skip, n: (skip + n, 0), part * (rows // step)))
        for _, part in blocks
    ]
    out = pl.pallas_call(
        normalize_kernel,
        grid=(rows // step,),
        in_specs=split + [pl.BlockSpec(gains.shape, lambda n: (0, 0))],
        out_specs=pl.BlockSpec((4, 2, step, width), lambda n: (0, 0, n, 0)),
        out_shape=jax.ShapeDtypeStruct((4, 2, rows, width), BF),
        compiler_params=pltpu.CompilerParams(vmem_limit_bytes=24 << 20),
        cost_estimate=pl.CostEstimate(flops=1024, transcendentals=0, bytes_accessed=1024),
        name="normalize",
    )(*[array for array, _ in blocks], gains)
    return out.reshape(4, 2 * rows, width)


def project_kernel(index_ref, normed_ref, own_ref, ahead_ref, across_ref, behind_ref, cosine_ref, sine_ref, out_ref, *, turned):
    shards = (own_ref, ahead_ref, across_ref, behind_ref)
    total = sum(
        jnp.dot(normed_ref[index_ref[step]], shard[...], preferred_element_type=F32)
        for step, shard in enumerate(shards)
    )
    for head in range(total.shape[1] // HEAD):
        raw = total[:, head * HEAD : (head + 1) * HEAD]
        if head < turned:
            raw = raw * cosine_ref[...] + pltpu.roll(raw, HEAD // 2, 1) * sine_ref[...]
        out_ref[:, head * HEAD : (head + 1) * HEAD] = raw.astype(BF)


def project(order, normed, shards, cosine, sine, turned, name):
    blocks, tokens, depth = normed.shape
    columns = shards[0].shape[1]
    wide = 2 * HEAD
    whole = lambda n, order: (0, 0)
    strip = lambda n, order: (0, n)
    return pl.pallas_call(
        functools.partial(project_kernel, turned=turned),
        grid_spec=pltpu.PrefetchScalarGridSpec(
            num_scalar_prefetch=1,
            grid=(columns // wide,),
            in_specs=[pl.BlockSpec((blocks, tokens, depth), lambda n, order: (0, 0, 0))]
            + [pl.BlockSpec((depth, wide), strip)] * 4
            + [pl.BlockSpec((tokens, HEAD), whole)] * 2,
            out_specs=pl.BlockSpec((tokens, wide), strip),
        ),
        out_shape=jax.ShapeDtypeStruct((tokens, columns), BF),
        compiler_params=pltpu.CompilerParams(vmem_limit_bytes=32 << 20),
        cost_estimate=pl.CostEstimate(flops=1024, transcendentals=0, bytes_accessed=1024),
        name=name,
    )(order, normed, *shards, cosine, sine)


def attend_kernel(query_ref, key_ref, value_ref, query_doc_ref, key_doc_ref, out_ref, bias_ref):
    rows, span = bias_ref.shape
    back = span - rows

    @pl.when(pl.program_id(1) == 0)
    def _():
        at_query = lax.broadcasted_iota(jnp.int32, (rows, span), 0)
        at_key = lax.broadcasted_iota(jnp.int32, (rows, span), 1) - back
        allowed = (at_key <= at_query) & (query_doc_ref[0] == key_doc_ref[0])
        bias_ref[...] = jnp.where(allowed, 0.0, -jnp.inf)

    for head in range(query_ref.shape[1] // HEAD):
        part = slice(head * HEAD, (head + 1) * HEAD)
        scores = lax.dot_general(
            query_ref[:, part], key_ref[0], (((1,), (1,)), ((), ())), preferred_element_type=F32
        )
        masked = scores + bias_ref[...]
        peak = jnp.max(masked, axis=1, keepdims=True)
        weights = jnp.exp((masked - peak) * (1.0 / math.sqrt(HEAD)))
        totals = jnp.sum(weights, axis=1, keepdims=True)
        mixed = jnp.dot(weights.astype(BF), value_ref[0], preferred_element_type=F32)
        out_ref[:, part] = (mixed / totals).astype(BF)


def attend(queries, pairs, query_docs, key_docs):
    batches, span, _ = pairs.shape
    rows = queries.shape[0] // batches
    wide = 2 * HEAD
    return pl.pallas_call(
        attend_kernel,
        grid=(batches, queries.shape[1] // wide),
        in_specs=[
            pl.BlockSpec((rows, wide), lambda b, h: (b, h)),
            pl.BlockSpec((1, span, HEAD), lambda b, h: (b, 0, 0)),
            pl.BlockSpec((1, span, HEAD), lambda b, h: (b, 0, 1)),
            pl.BlockSpec((1, rows, 1), lambda b, h: (b, 0, 0)),
            pl.BlockSpec((1, 1, span), lambda b, h: (b, 0, 0)),
        ],
        out_specs=pl.BlockSpec((rows, wide), lambda b, h: (b, h)),
        out_shape=jax.ShapeDtypeStruct(queries.shape, BF),
        scratch_shapes=[pltpu.VMEM((rows, span), F32)],
        compiler_params=pltpu.CompilerParams(vmem_limit_bytes=24 << 20),
        cost_estimate=pl.CostEstimate(flops=1024, transcendentals=0, bytes_accessed=1024),
        name="attend",
    )(queries, pairs, pairs, query_docs, key_docs)


def spread_kernel(index_ref, mixed_ref, own_ref, ahead_ref, across_ref, behind_ref, sent_kept_ref, sent_passed_ref, kept_ref, passed_ref, terms_ref):
    for step, shard in enumerate((own_ref, ahead_ref, across_ref, behind_ref)):
        terms_ref[step] = jnp.dot(mixed_ref[...], shard[...], preferred_element_type=F32)
    sent_kept_ref[...] = terms_ref[index_ref[1]].astype(BF)
    sent_passed_ref[...] = terms_ref[index_ref[3]].astype(BF)
    kept_ref[...] = terms_ref[index_ref[0]]
    passed_ref[...] = terms_ref[index_ref[2]]


def spread(order, mixed, shards, name):
    tokens, _ = mixed.shape
    columns = shards[0].shape[1]
    return pl.pallas_call(
        spread_kernel,
        in_specs=[pl.BlockSpec(memory_space=pltpu.SMEM)] + [pl.BlockSpec(memory_space=pltpu.VMEM)] * 5,
        out_specs=[pl.BlockSpec(memory_space=pltpu.VMEM)] * 4,
        out_shape=[
            jax.ShapeDtypeStruct((tokens, columns), BF),
            jax.ShapeDtypeStruct((tokens, columns), BF),
            jax.ShapeDtypeStruct((tokens, columns), F32),
            jax.ShapeDtypeStruct((tokens, columns), F32),
        ],
        scratch_shapes=[pltpu.VMEM((4, tokens, columns), F32)],
        compiler_params=pltpu.CompilerParams(vmem_limit_bytes=24 << 20),
        cost_estimate=pl.CostEstimate(flops=1024, transcendentals=0, bytes_accessed=1024),
        name=name,
    )(order, mixed, *shards)


def body(
    arriving,
    stored,
    docs_forward,
    docs_backward,
    norm_gain,
    query_weight,
    key_weight,
    value_projection_weight,
    out_weight,
):
    mine = arriving[0]
    held = stored[0]
    rows, width = mine.shape
    ring = lax.axis_size("ctx")
    c = lax.axis_index("ctx")
    t = lax.axis_index("tensor")
    near_high = lax.axis_index("section") < lax.axis_size("section") // 2
    docs = jnp.stack((docs_forward[0], docs_backward[0]), axis=0)
    flips = jnp.arange(4, dtype=jnp.int32)
    half = rows // 2

    strips = []
    start = 0
    for share in STRIPS:
        strips.append((start, start + width * share // sum(STRIPS)))
        start = strips[-1][1]
    out_own = [out_weight[0][:, low:high] for low, high in strips]

    kv_weight = jnp.concatenate((key_weight[0], value_projection_weight[0]), axis=1)
    with jax.named_scope("kv_hop1"):
        kv_ahead, kv_behind = first_hop(kv_weight)
    both = jnp.concatenate((mine, held), axis=0)
    with jax.named_scope("z_in"):
        up, down = from_z(both, 2), from_z(both, -2)
    q_weight = query_weight[0]
    with jax.named_scope("q_hop1"):
        q_ahead, q_behind = first_hop(after(q_weight, kv_ahead, kv_behind))
    stashed = jnp.where(near_high, up[:rows], down[:rows])
    fetched = jnp.where(near_high, up[rows:], down[rows:])
    fetched_far = jnp.where(near_high, down[rows:], up[rows:])
    near_blocks = jnp.concatenate((mine, fetched, fetched_far), axis=0)
    with jax.named_scope("sib_near"):
        sib_near = from_tensor(near_blocks, 1)
    up, down, q_ahead, q_behind, kv_ahead, kv_behind, sib_near = lax.optimization_barrier(
        (up, down, q_ahead, q_behind, kv_ahead, kv_behind, sib_near)
    )

    with jax.named_scope("kv_hop2"):
        kv_across = jnp.concatenate(second_hop(kv_ahead, kv_behind), axis=0)
    with jax.named_scope("q_hop2"):
        q_across = jnp.concatenate(second_hop(q_ahead, q_behind), axis=0)
    with jax.named_scope("far"):
        mine_far = jnp.concatenate((from_z(up[:half], 2), from_z(down[half:rows], -2)), axis=0)
    with jax.named_scope("out_hop1_0"):
        out_hops = [first_hop(after(out_own[0], kv_across))]
    with jax.named_scope("sib_far"):
        sib_far = from_tensor(mine_far, 1)
    blocks = (
        ((mine, 0), (sib_near, 0), (mine_far, 0), (sib_far, 0))
        + ((fetched, 0), (sib_near, 1), (fetched_far, 0), (sib_near, 2))
    )
    gains = norm_gain[0].reshape(-1, width)
    normed = normalize(blocks, jnp.take(gains, t ^ flips, axis=0), rows)
    cosine, sine = rope_tables(rows)
    cosine, sine = jnp.concatenate((cosine, cosine), axis=0), jnp.concatenate((sine, sine), axis=0)
    feature_order = t ^ ((c + flips) % ring)

    own_kv = project(
        feature_order,
        after(normed, q_across),
        (kv_weight, kv_ahead, kv_across, kv_behind),
        cosine,
        sine,
        1,
        "project_kv",
    )
    id_rows = 16
    ids = jnp.broadcast_to(docs.astype(BF)[:, None, :], (2, id_rows, rows))
    own_pair = jnp.concatenate((ids, own_kv.reshape(2, rows, 2 * HEAD)), axis=1)
    with jax.named_scope("kv_rows"):
        kv_one, kv_two = from_before(own_pair, 1), from_before(own_pair, 2)
    all_kv = jnp.concatenate((kv_two[:, id_rows:], kv_one[:, id_rows:], own_pair[:, id_rows:]), axis=1)
    docs_one = jnp.where(c >= 1, kv_one[:, 0].astype(jnp.int32), -1)
    docs_two = jnp.where(c >= 2, kv_two[:, 0].astype(jnp.int32), -1)
    key_docs = jnp.concatenate((docs_two, docs_one, docs), axis=1)
    queries = project(
        feature_order,
        after(normed, own_kv),
        (q_weight, q_ahead, q_across, q_behind),
        cosine,
        sine,
        2,
        "project_q",
    )
    mixed = attend(queries, all_kv, docs[:, :, None], key_docs[:, None, :])

    residual = jnp.concatenate((mine, fetched), axis=0)
    term_order = ((t ^ flips) - c) % ring
    passed_before = []
    outputs = []
    for index, (low, high) in enumerate(strips):
        ahead, behind = out_hops[index]
        with jax.named_scope("out_hop2_%d" % index):
            across = jnp.concatenate(second_hop(ahead, behind), axis=0)
        if index + 1 < len(strips):
            with jax.named_scope("out_hop1_%d" % (index + 1)):
                out_hops.append(first_hop(after(out_own[index + 1], across)))
        sent_kept, sent_passed, kept, passed = spread(
            term_order, after(mixed, *passed_before), (out_own[index], ahead, across, behind), "spread_%d" % index
        )
        if index:
            sent_passed = after(sent_passed, outputs[-1])
        with jax.named_scope("core_passed_%d" % index):
            passed = (passed + from_tensor(sent_passed, 1).astype(F32)).astype(BF)
        with jax.named_scope("z_sum_%d" % index):
            arrived = from_tensor(passed, 2)
        with jax.named_scope("core_kept_%d" % index):
            kept = kept + from_tensor(sent_kept, 1).astype(F32)
        passed_before = [passed]
        base = residual[:, low:high].astype(F32)
        outputs.append((base + (kept + arrived.astype(F32))).astype(BF))
    result = jnp.concatenate(outputs, axis=1)
    return (result[:rows][None], stashed[None], result[rows:][None])


def solution(mesh):
    return jax.shard_map(
        body,
        mesh=mesh,
        in_specs=(
            P("section", "ctx", "tensor"),
            P("section", "ctx", "tensor"),
            P("section", "ctx"),
            P("section", "ctx"),
            P("section", None),
            P("section", "ctx", "tensor"),
            P("section", "ctx", "tensor"),
            P("section", "ctx", "tensor"),
            P("section", "tensor", "ctx"),
        ),
        out_specs=(
            P("section", "ctx", "tensor"),
            P("section", "ctx", "tensor"),
            P("section", "ctx", "tensor"),
        ),
        check_vma=False,
    )
```

profile of v0, /device:TPU:79, one launch (start us, length us, event | category | flops | bytes accessed | tf_op | source)
XLA Modules:
  0.0 247.2 jit_solution(13356854219823273275)
XLA Ops:
  0.7 2.3 pad_maximum_fusion.1
  3.0 4.2 %collective-permute-start.1 = (bf16[512,1024]{1,0:T(8,128)(2,1)}, bf16[512,1024]{1,0:T(8,128)(2,1)S(1)}, u32[]{:S(2)}, u32[]{:S(2)}) collective-permute-start(bf16[512,1024]{1,0:T(8,128)(2,1)} %pad_maximum_fusion.1), channel_id=1, source_target_pairs={{130,0},{131,1},{146,16},{147,17},{162,32},{163,33},{178,48},{179,... | collective-permute-start | bytes 3145736 | tf_op jit(solution)/shard_map/z_in/ppermute | solution.py:42
  10.8 10.3 %collective-permute-done.2.ahead_ref = bf16[1024,256]{1,0:T(8,128)(2,1)S(1)} collective-permute-done((bf16[1024,256]{1,0:T(8,128)(2,1)S(1)}, bf16[1024,256]{1,0:T(8,128)(2,1)S(1)}, u32[]{:S(2)}, u32[]{:S(2)}) %collective-permute-start.2) | collective-permute-done | bytes 524320 | tf_op jit(solution)/shard_map/kv_hop1/ppermute | solution.py:47
  22.7 2.7 %collective-permute-start.5 = (bf16[1024,1024]{1,0:T(8,128)(2,1)}, bf16[1024,1024]{1,0:T(8,128)(2,1)}, u32[]{:S(2)}, u32[]{:S(2)}) collective-permute-start(bf16[1024,1024]{1,0:T(8,128)(2,1)} %bitcast.2.own_ref), channel_id=1, source_target_pairs={{12,0},{0,4},{4,8},{8,12},{13,1},{1,5},{5,9},{9,13},{14,2},{2,6},{... | collective-permute-start | bytes 6291464 | tf_op jit(solution)/shard_map/q_hop1/ppermute | solution.py:47
  25.4 27.5 %collective-permute-done = bf16[512,1024]{1,0:T(8,128)(2,1)} collective-permute-done((bf16[512,1024]{1,0:T(8,128)(2,1)}, bf16[512,1024]{1,0:T(8,128)(2,1)}, u32[]{:S(2)}, u32[]{:S(2)}) %collective-permute-start) | collective-permute-done | bytes 1048608 | tf_op jit(solution)/shard_map/z_in/ppermute | solution.py:42
  52.9 2.5 %fusion.4 = (bf16[1,256,1024]{2,1,0:T(8,128)(2,1)}, bf16[256,1024]{1,0:T(8,128)(2,1)S(1)}, bf16[256,1024]{1,0:T(8,128)(2,1)S(1)}) fusion(bf16[512,1024]{1,0:T(8,128)(2,1)S(1)} %collective-permute-done.1, bf16[512,1024]{1,0:T(8,128)(2,1)} %collective-permute-done, pred[]{:T(512)S(6)} %lt.28), kind=kLoop, calls=%fused_computation.19 | loop fusion | flops 786432 | bytes 3670017 | tf_op jit(solution)/shard_map/broadcast_in_dim | solution.py:346
  59.2 10.4 %collective-permute-done.4.ahead_ref = bf16[1024,1024]{1,0:T(8,128)(2,1)} collective-permute-done((bf16[1024,1024]{1,0:T(8,128)(2,1)}, bf16[1024,1024]{1,0:T(8,128)(2,1)}, u32[]{:S(2)}, u32[]{:S(2)}) %collective-permute-start.4) | collective-permute-done | bytes 2097184 | tf_op jit(solution)/shard_map/q_hop1/ppermute | solution.py:47
  74.0 2.6 %collective-permute-start.8 = (bf16[128,1024]{1,0:T(8,128)(2,1)}, bf16[128,1024]{1,0:T(8,128)(2,1)}, u32[]{:S(2)}, u32[]{:S(2)}) collective-permute-start(bf16[128,1024]{1,0:T(8,128)(2,1)} %slice.78), channel_id=1, source_target_pairs={{130,0},{131,1},{146,16},{147,17},{162,32},{163,33},{178,48},{179,... | collective-permute-start | bytes 786440 | tf_op jit(solution)/shard_map/far/ppermute | solution.py:42
  80.9 2.5 %slice.108.own_ref = bf16[1024,640]{1,0:T(8,128)(2,1)} slice(bf16[1024,1024]{1,0:T(8,128)(2,1)} %bitcast.30), slice={[0:1024], [0:640]} | slice | bytes 2621440 | tf_op jit(solution)/shard_map/slice | solution.py:250
  91.3 4.2 %collective-permute-start.9 = (bf16[256,1024]{1,0:T(8,128)(2,1)S(1)}, bf16[256,1024]{1,0:T(8,128)(2,1)S(1)}, u32[]{:S(2)}, u32[]{:S(2)}) collective-permute-start(bf16[256,1024]{1,0:T(8,128)(2,1)S(1)} %constant_dynamic-update-slice_fusion.refs_2_), channel_id=1, source_target_pairs={{0,1},{1,0},{2,3},{3,2},{4,5},{5,4},{6,7},{7,6},{8,9},{9,8},{10,11... | collective-permute-start | bytes 1572872 | tf_op jit(solution)/shard_map/sib_far/ppermute | solution.py:57
  95.4 12.5 %collective-permute-done.12 = bf16[512,256]{1,0:T(8,128)(2,1)} collective-permute-done((bf16[512,256]{1,0:T(8,128)(2,1)}, bf16[512,256]{1,0:T(8,128)(2,1)}, u32[]{:S(2)}, u32[]{:S(2)}) %collective-permute-start.12) | collective-permute-done | bytes 262176 | tf_op jit(solution)/shard_map/kv_hop2/ppermute | solution.py:47
  108.9 4.1 %collective-permute-done.13 = bf16[512,256]{1,0:T(8,128)(2,1)S(1)} collective-permute-done((bf16[512,256]{1,0:T(8,128)(2,1)S(1)}, bf16[512,256]{1,0:T(8,128)(2,1)S(1)}, u32[]{:S(2)}, u32[]{:S(2)}) %collective-permute-start.13) | collective-permute-done | bytes 262176 | tf_op jit(solution)/shard_map/kv_hop2/ppermute | solution.py:47
  132.9 7.5 %project_q.1.query_ref = bf16[512,1024]{1,0:T(8,128)(2,1)S(1)} custom-call(s32[4]{0:T(128)S(1)} %fusion.8.index_ref, bf16[4,512,1024]{2,1,0:T(8,128)(2,1)S(1)} %bitcast.23, bf16[1024,1024]{1,0:T(8,128)(2,1)} %bitcast.2.own_ref, bf16[1024,1024]{1,0:T(8,128)(2,1)} %collective-permute-done.4.ahead_ref, bf16[1024,1024]{1,0:T(8,128)(2,1)S(1)} %copy-done.4, ...), custom_call_target="tpu_custom_call" | custom-call | flops 1024 | bytes 1024 | tf_op jit(solution)/shard_map/project_q/pallas_call | solution.py:130
  140.4 4.6 %collective-permute-done.15 = bf16[2,272,256]{2,0,1:T(2,128)(2,1)} collective-permute-done((bf16[2,272,256]{2,0,1:T(2,128)(2,1)}, bf16[2,272,256]{2,0,1:T(2,128)(2,1)}, u32[]{:S(2)}, u32[]{:S(2)}) %collective-permute-start.15) | collective-permute-done | bytes 278560 | tf_op jit(solution)/shard_map/kv_rows/ppermute | solution.py:52
  150.0 6.6 %collective-permute-start.17 = (bf16[512,640]{1,0:T(8,128)(2,1)S(1)}, bf16[512,640]{1,0:T(8,128)(2,1)S(1)}, u32[]{:S(2)}, u32[]{:S(2)}) collective-permute-start(bf16[512,640]{1,0:T(8,128)(2,1)S(1)} %slice.109), channel_id=1, source_target_pairs={{4,0},{8,4},{12,8},{0,12},{5,1},{9,5},{13,9},{1,13},{6,2},{10,6},{... | collective-permute-start | bytes 1966088 | tf_op jit(solution)/shard_map/out_hop2_0/ppermute | solution.py:47
  159.8 9.3 %attend.1.mixed_ref = bf16[512,1024]{1,0:T(8,128)(2,1)S(1)} custom-call(bf16[512,1024]{1,0:T(8,128)(2,1)S(1)} %project_q.1.query_ref, bf16[2,768,256]{2,1,0:T(8,128)(2,1)S(1)} %copy.17.key_ref.value_ref, bf16[2,768,256]{2,1,0:T(8,128)(2,1)S(1)} %copy.17.key_ref.value_ref, s32[2,256,1]{2,1,0:T(8,128)S(1)} %copy.19.query_doc_ref, ...), custom_call_target="tpu_custom_call" | custom-call | flops 1024 | bytes 1024 | tf_op jit(solution)/shard_map/attend/pallas_call | solution.py:175
  169.4 5.9 %spread_0.1 = (bf16[512,640]{1,0:T(8,128)(2,1)S(1)}, bf16[512,640]{1,0:T(8,128)(2,1)S(1)}, f32[512,640]{1,0:T(8,128)S(1)}, f32[512,640]{1,0:T(8,128)S(1)}) custom-call(s32[4]{0:T(128)S(1)} %and_select_fusion.1.index_ref, bf16[512,1024]{1,0:T(8,128)(2,1)S(1)} %attend.1.mixed_ref, bf16[1024,640]{1,0:T(8,128)(2,1)} %slice.108.own_ref, ...), custom_call_target="tpu_custom_call" | custom-call | flops 1024 | bytes 1024 | tf_op jit(solution)/shard_map/spread_0/pallas_call | solution.py:206
  175.2 6.6 %collective-permute-start.21 = (bf16[512,640]{1,0:T(8,128)(2,1)S(1)}, bf16[512,640]{1,0:T(8,128)(2,1)S(1)}, u32[]{:S(2)}, u32[]{:S(2)}) collective-permute-start(bf16[512,640]{1,0:T(8,128)(2,1)S(1)} %get-tuple-element.39), channel_id=1, source_target_pairs={{0,1},{1,0},{2,3},{3,2},{4,5},{5,4},{6,7},{7,6},{8,9},{9,8},{10,11... | collective-permute-start | bytes 1966088 | tf_op jit(solution)/shard_map/core_passed_0/ppermute | solution.py:57
  185.4 3.7 %collective-permute-start.22 = (bf16[512,640]{1,0:T(8,128)(2,1)S(1)}, bf16[512,640]{1,0:T(8,128)(2,1)S(1)}, u32[]{:S(2)}, u32[]{:S(2)}) collective-permute-start(bf16[512,640]{1,0:T(8,128)(2,1)S(1)} %add_convert_fusion.1), channel_id=1, source_target_pairs={{0,2},{1,3},{2,0},{3,1},{4,6},{5,7},{6,4},{7,5},{8,10},{9,11},{10,... | collective-permute-start | bytes 1966088 | tf_op jit(solution)/shard_map/z_sum_0/ppermute | solution.py:57
  189.0 13.7 %collective-permute-done.25.behind_ref = bf16[1024,384]{1,0:T(8,128)(2,1)S(1)} collective-permute-done((bf16[1024,384]{1,0:T(8,128)(2,1)S(1)}, bf16[1024,384]{1,0:T(8,128)(2,1)S(1)}, u32[]{:S(2)}, u32[]{:S(2)}) %collective-permute-start.25) | collective-permute-done | bytes 786464 | tf_op jit(solution)/shard_map/out_hop1_1/ppermute | solution.py:47
  204.4 8.4 %collective-permute-done.26 = bf16[512,384]{1,0:T(8,128)(2,1)S(1)} collective-permute-done((bf16[512,384]{1,0:T(8,128)(2,1)S(1)}, bf16[512,384]{1,0:T(8,128)(2,1)S(1)}, u32[]{:S(2)}, u32[]{:S(2)}) %collective-permute-start.26) | collective-permute-done | bytes 393248 | tf_op jit(solution)/shard_map/out_hop2_1/ppermute | solution.py:47
  215.2 3.1 %spread_1.1 = (bf16[512,384]{1,0:T(8,128)(2,1)S(1)}, bf16[512,384]{1,0:T(8,128)(2,1)S(1)}, f32[512,384]{1,0:T(8,128)S(1)}, f32[512,384]{1,0:T(8,128)S(1)}) custom-call(s32[4]{0:T(128)S(1)} %and_select_fusion.1.index_ref, bf16[512,1024]{1,0:T(8,128)(2,1)S(1)} %attend.1.mixed_ref, bf16[1024,384]{1,0:T(8,128)(2,1)S(1)} %slice.111.own_ref, ...), custom_call_target="tpu_custom_call" | custom-call | flops 1024 | bytes 1024 | tf_op jit(solution)/shard_map/spread_1/pallas_call | solution.py:206
  222.4 3.2 %collective-permute-start.29 = (bf16[512,384]{1,0:T(8,128)(2,1)S(1)}, bf16[512,384]{1,0:T(8,128)(2,1)S(1)}, u32[]{:S(2)}, u32[]{:S(2)}) collective-permute-start(bf16[512,384]{1,0:T(8,128)(2,1)S(1)} %add_convert_fusion.3), channel_id=1, source_target_pairs={{0,2},{1,3},{2,0},{3,1},{4,6},{5,7},{6,4},{7,5},{8,10},{9,11},{10,... | collective-permute-start | bytes 1179656 | tf_op jit(solution)/shard_map/z_sum_1/ppermute | solution.py:57
  225.6 20.2 %collective-permute-done.29 = bf16[512,384]{1,0:T(8,128)(2,1)S(1)} collective-permute-done((bf16[512,384]{1,0:T(8,128)(2,1)S(1)}, bf16[512,384]{1,0:T(8,128)(2,1)S(1)}, u32[]{:S(2)}, u32[]{:S(2)}) %collective-permute-start.29) | collective-permute-done | bytes 393248 | tf_op jit(solution)/shard_map/z_sum_1/ppermute | solution.py:57
  (148 shorter events, 67.5 us)
Async XLA Ops:
  3.0 49.9 %collective-permute-start = (bf16[512,1024]{1,0:T(8,128)(2,1)}, bf16[512,1024]{1,0:T(8,128)(2,1)}, u32[]{:S(2)}, u32[]{:S(2)}) collective-permute-start(bf16[512,1024]{1,0:T(8,128)(2,1)} %pad_maximum_fusion.1), channel_id=1, source_target_pairs={{128,0},{129,1},{144,16},{145,17},{160,32},{161,33},{176,48},{177,... | collective-permute-start | bytes 3145736 | tf_op jit(solution)/shard_map/z_in/ppermute | solution.py:42
  3.0 49.9 %collective-permute-start.1 = (bf16[512,1024]{1,0:T(8,128)(2,1)}, bf16[512,1024]{1,0:T(8,128)(2,1)S(1)}, u32[]{:S(2)}, u32[]{:S(2)}) collective-permute-start(bf16[512,1024]{1,0:T(8,128)(2,1)} %pad_maximum_fusion.1), channel_id=1, source_target_pairs={{130,0},{131,1},{146,16},{147,17},{162,32},{163,33},{178,48},{179,... | collective-permute-start | bytes 3145736 | tf_op jit(solution)/shard_map/z_in/ppermute | solution.py:42
  7.3 13.9 %collective-permute-start.2 = (bf16[1024,256]{1,0:T(8,128)(2,1)S(1)}, bf16[1024,256]{1,0:T(8,128)(2,1)S(1)}, u32[]{:S(2)}, u32[]{:S(2)}) collective-permute-start(bf16[1024,256]{1,0:T(8,128)(2,1)S(1)} %pad_maximum_fusion.5.own_ref), channel_id=1, source_target_pairs={{4,0},{8,4},{12,8},{0,12},{5,1},{9,5},{13,9},{1,13},{6,2},{10,6},{... | collective-permute-start | bytes 1572872 | tf_op jit(solution)/shard_map/kv_hop1/ppermute | solution.py:47
  7.9 13.2 %collective-permute-start.3 = (bf16[1024,256]{1,0:T(8,128)(2,1)S(1)}, bf16[1024,256]{1,0:T(8,128)(2,1)S(1)}, u32[]{:S(2)}, u32[]{:S(2)}) collective-permute-start(bf16[1024,256]{1,0:T(8,128)(2,1)S(1)} %pad_maximum_fusion.5.own_ref), channel_id=1, source_target_pairs={{12,0},{0,4},{4,8},{8,12},{13,1},{1,5},{5,9},{9,13},{14,2},{2,6},{... | collective-permute-start | bytes 1572872 | tf_op jit(solution)/shard_map/kv_hop1/ppermute | solution.py:47
  22.7 46.9 %collective-permute-start.4 = (bf16[1024,1024]{1,0:T(8,128)(2,1)}, bf16[1024,1024]{1,0:T(8,128)(2,1)}, u32[]{:S(2)}, u32[]{:S(2)}) collective-permute-start(bf16[1024,1024]{1,0:T(8,128)(2,1)} %bitcast.2.own_ref), channel_id=1, source_target_pairs={{4,0},{8,4},{12,8},{0,12},{5,1},{9,5},{13,9},{1,13},{6,2},{10,6},{... | collective-permute-start | bytes 6291464 | tf_op jit(solution)/shard_map/q_hop1/ppermute | solution.py:47
  22.7 46.9 %collective-permute-start.5 = (bf16[1024,1024]{1,0:T(8,128)(2,1)}, bf16[1024,1024]{1,0:T(8,128)(2,1)}, u32[]{:S(2)}, u32[]{:S(2)}) collective-permute-start(bf16[1024,1024]{1,0:T(8,128)(2,1)} %bitcast.2.own_ref), channel_id=1, source_target_pairs={{12,0},{0,4},{4,8},{8,12},{13,1},{1,5},{5,9},{9,13},{14,2},{2,6},{... | collective-permute-start | bytes 6291464 | tf_op jit(solution)/shard_map/q_hop1/ppermute | solution.py:47
  56.7 12.9 %collective-permute-start.6 = (bf16[768,1024]{1,0:T(8,128)(2,1)}, bf16[768,1024]{1,0:T(8,128)(2,1)S(1)}, u32[]{:S(2)}, u32[]{:S(2)}) collective-permute-start(bf16[768,1024]{1,0:T(8,128)(2,1)} %pad_maximum_fusion), channel_id=1, source_target_pairs={{0,1},{1,0},{2,3},{3,2},{4,5},{5,4},{6,7},{7,6},{8,9},{9,8},{10,11... | collective-permute-start | bytes 4718600 | tf_op jit(solution)/shard_map/sib_near/ppermute | solution.py:57
  71.3 16.2 %collective-permute-start.7 = (bf16[128,1024]{1,0:T(8,128)(2,1)}, bf16[128,1024]{1,0:T(8,128)(2,1)}, u32[]{:S(2)}, u32[]{:S(2)}) collective-permute-start(bf16[128,1024]{1,0:T(8,128)(2,1)} %slice.77), channel_id=1, source_target_pairs={{128,0},{129,1},{144,16},{145,17},{160,32},{161,33},{176,48},{177,... | collective-permute-start | bytes 786440 | tf_op jit(solution)/shard_map/far/ppermute | solution.py:42
  74.0 16.3 %collective-permute-start.8 = (bf16[128,1024]{1,0:T(8,128)(2,1)}, bf16[128,1024]{1,0:T(8,128)(2,1)}, u32[]{:S(2)}, u32[]{:S(2)}) collective-permute-start(bf16[128,1024]{1,0:T(8,128)(2,1)} %slice.78), channel_id=1, source_target_pairs={{130,0},{131,1},{146,16},{147,17},{162,32},{163,33},{178,48},{179,... | collective-permute-start | bytes 786440 | tf_op jit(solution)/shard_map/far/ppermute | solution.py:42
  79.4 39.0 %collective-permute-start.10 = (bf16[512,1024]{1,0:T(8,128)(2,1)}, bf16[512,1024]{1,0:T(8,128)(2,1)}, u32[]{:S(2)}, u32[]{:S(2)}) collective-permute-start(bf16[512,1024]{1,0:T(8,128)(2,1)} %slice.79), channel_id=1, source_target_pairs={{4,0},{8,4},{12,8},{0,12},{5,1},{9,5},{13,9},{1,13},{6,2},{10,6},{... | collective-permute-start | bytes 3145736 | tf_op jit(solution)/shard_map/q_hop2/ppermute | solution.py:47
  80.1 27.8 %collective-permute-start.12 = (bf16[512,256]{1,0:T(8,128)(2,1)}, bf16[512,256]{1,0:T(8,128)(2,1)}, u32[]{:S(2)}, u32[]{:S(2)}) collective-permute-start(bf16[512,256]{1,0:T(8,128)(2,1)} %slice.81), channel_id=1, source_target_pairs={{4,0},{8,4},{12,8},{0,12},{5,1},{9,5},{13,9},{1,13},{6,2},{10,6},{... | collective-permute-start | bytes 786440 | tf_op jit(solution)/shard_map/kv_hop2/ppermute | solution.py:47
  85.3 35.2 %collective-permute-start.11 = (bf16[512,1024]{1,0:T(8,128)(2,1)S(1)}, bf16[512,1024]{1,0:T(8,128)(2,1)S(1)}, u32[]{:S(2)}, u32[]{:S(2)}) collective-permute-start(bf16[512,1024]{1,0:T(8,128)(2,1)S(1)} %slice.80), channel_id=1, source_target_pairs={{12,0},{0,4},{4,8},{8,12},{13,1},{1,5},{5,9},{9,13},{14,2},{2,6},{... | collective-permute-start | bytes 3145736 | tf_op jit(solution)/shard_map/q_hop2/ppermute | solution.py:47
  87.5 25.5 %collective-permute-start.13 = (bf16[512,256]{1,0:T(8,128)(2,1)S(1)}, bf16[512,256]{1,0:T(8,128)(2,1)S(1)}, u32[]{:S(2)}, u32[]{:S(2)}) collective-permute-start(bf16[512,256]{1,0:T(8,128)(2,1)S(1)} %slice.82), channel_id=1, source_target_pairs={{12,0},{0,4},{4,8},{8,12},{13,1},{1,5},{5,9},{9,13},{14,2},{2,6},{... | collective-permute-start | bytes 786440 | tf_op jit(solution)/shard_map/kv_hop2/ppermute | solution.py:47
  91.3 25.1 %collective-permute-start.9 = (bf16[256,1024]{1,0:T(8,128)(2,1)S(1)}, bf16[256,1024]{1,0:T(8,128)(2,1)S(1)}, u32[]{:S(2)}, u32[]{:S(2)}) collective-permute-start(bf16[256,1024]{1,0:T(8,128)(2,1)S(1)} %constant_dynamic-update-slice_fusion.refs_2_), channel_id=1, source_target_pairs={{0,1},{1,0},{2,3},{3,2},{4,5},{5,4},{6,7},{7,6},{8,9},{9,8},{10,11... | collective-permute-start | bytes 1572872 | tf_op jit(solution)/shard_map/sib_far/ppermute | solution.py:57
  113.0 35.8 %collective-permute-start.16 = (bf16[1024,640]{1,0:T(8,128)(2,1)}, bf16[1024,640]{1,0:T(8,128)(2,1)}, u32[]{:S(2)}, u32[]{:S(2)}) collective-permute-start(bf16[1024,640]{1,0:T(8,128)(2,1)} %slice.108.own_ref), channel_id=1, source_target_pairs={{4,0},{8,4},{12,8},{0,12},{5,1},{9,5},{13,9},{1,13},{6,2},{10,6},{... | collective-permute-start | bytes 3932168 | tf_op jit(solution)/shard_map/out_hop1_0/ppermute | solution.py:47
  114.5 42.1 %collective-permute-start.18 = (bf16[1024,640]{1,0:T(8,128)(2,1)}, bf16[1024,640]{1,0:T(8,128)(2,1)}, u32[]{:S(2)}, u32[]{:S(2)}) collective-permute-start(bf16[1024,640]{1,0:T(8,128)(2,1)} %slice.108.own_ref), channel_id=1, source_target_pairs={{12,0},{0,4},{4,8},{8,12},{13,1},{1,5},{5,9},{9,13},{14,2},{2,6},{... | collective-permute-start | bytes 3932168 | tf_op jit(solution)/shard_map/out_hop1_0/ppermute | solution.py:47
  125.4 19.6 %collective-permute-start.15 = (bf16[2,272,256]{2,0,1:T(2,128)(2,1)}, bf16[2,272,256]{2,0,1:T(2,128)(2,1)}, u32[]{:S(2)}, u32[]{:S(2)}) collective-permute-start(bf16[2,272,256]{2,0,1:T(2,128)(2,1)} %pad_maximum_fusion.7), channel_id=1, source_target_pairs={{0,4},{4,8},{8,12},{1,5},{5,9},{9,13},{2,6},{6,10},{10,14},{3,7},{... | collective-permute-start | bytes 835592 | tf_op jit(solution)/shard_map/kv_rows/ppermute | solution.py:52
  126.7 20.3 %collective-permute-start.14 = (bf16[2,272,256]{2,0,1:T(2,128)(2,1)}, bf16[2,272,256]{2,0,1:T(2,128)(2,1)}, u32[]{:S(2)}, u32[]{:S(2)}) collective-permute-start(bf16[2,272,256]{2,0,1:T(2,128)(2,1)} %pad_maximum_fusion.7), channel_id=1, source_target_pairs={{0,8},{4,12},{1,9},{5,13},{2,10},{6,14},{3,11},{7,15},{16,24},{20,... | collective-permute-start | bytes 835592 | tf_op jit(solution)/shard_map/kv_rows/ppermute | solution.py:52
  150.0 19.2 %collective-permute-start.17 = (bf16[512,640]{1,0:T(8,128)(2,1)S(1)}, bf16[512,640]{1,0:T(8,128)(2,1)S(1)}, u32[]{:S(2)}, u32[]{:S(2)}) collective-permute-start(bf16[512,640]{1,0:T(8,128)(2,1)S(1)} %slice.109), channel_id=1, source_target_pairs={{4,0},{8,4},{12,8},{0,12},{5,1},{9,5},{13,9},{1,13},{6,2},{10,6},{... | collective-permute-start | bytes 1966088 | tf_op jit(solution)/shard_map/out_hop2_0/ppermute | solution.py:47
  183.1 19.7 %collective-permute-start.25 = (bf16[1024,384]{1,0:T(8,128)(2,1)S(1)}, bf16[1024,384]{1,0:T(8,128)(2,1)S(1)}, u32[]{:S(2)}, u32[]{:S(2)}) collective-permute-start(bf16[1024,384]{1,0:T(8,128)(2,1)S(1)} %slice.111.own_ref), channel_id=1, source_target_pairs={{12,0},{0,4},{4,8},{8,12},{13,1},{1,5},{5,9},{9,13},{14,2},{2,6},{... | collective-permute-start | bytes 2359304 | tf_op jit(solution)/shard_map/out_hop1_1/ppermute | solution.py:47
  183.8 20.5 %collective-permute-start.23 = (bf16[1024,384]{1,0:T(8,128)(2,1)S(1)}, bf16[1024,384]{1,0:T(8,128)(2,1)S(1)}, u32[]{:S(2)}, u32[]{:S(2)}) collective-permute-start(bf16[1024,384]{1,0:T(8,128)(2,1)S(1)} %slice.111.own_ref), channel_id=1, source_target_pairs={{4,0},{8,4},{12,8},{0,12},{5,1},{9,5},{13,9},{1,13},{6,2},{10,6},{... | collective-permute-start | bytes 2359304 | tf_op jit(solution)/shard_map/out_hop1_1/ppermute | solution.py:47
  184.9 33.4 %collective-permute-start.20 = (bf16[512,640]{1,0:T(8,128)(2,1)S(1)}, bf16[512,640]{1,0:T(8,128)(2,1)S(1)}, u32[]{:S(2)}, u32[]{:S(2)}) collective-permute-start(bf16[512,640]{1,0:T(8,128)(2,1)S(1)} %get-tuple-element.37), channel_id=1, source_target_pairs={{0,1},{1,0},{2,3},{3,2},{4,5},{5,4},{6,7},{7,6},{8,9},{9,8},{10,11... | collective-permute-start | bytes 1966088 | tf_op jit(solution)/shard_map/core_kept_0/ppermute | solution.py:57
  185.4 34.5 %collective-permute-start.22 = (bf16[512,640]{1,0:T(8,128)(2,1)S(1)}, bf16[512,640]{1,0:T(8,128)(2,1)S(1)}, u32[]{:S(2)}, u32[]{:S(2)}) collective-permute-start(bf16[512,640]{1,0:T(8,128)(2,1)S(1)} %add_convert_fusion.1), channel_id=1, source_target_pairs={{0,2},{1,3},{2,0},{3,1},{4,6},{5,7},{6,4},{7,5},{8,10},{9,11},{10,... | collective-permute-start | bytes 1966088 | tf_op jit(solution)/shard_map/z_sum_0/ppermute | solution.py:57
  222.4 23.4 %collective-permute-start.29 = (bf16[512,384]{1,0:T(8,128)(2,1)S(1)}, bf16[512,384]{1,0:T(8,128)(2,1)S(1)}, u32[]{:S(2)}, u32[]{:S(2)}) collective-permute-start(bf16[512,384]{1,0:T(8,128)(2,1)S(1)} %add_convert_fusion.3), channel_id=1, source_target_pairs={{0,2},{1,3},{2,0},{3,1},{4,6},{5,7},{6,4},{7,5},{8,10},{9,11},{10,... | collective-permute-start | bytes 1179656 | tf_op jit(solution)/shard_map/z_sum_1/ppermute | solution.py:57
  (31 other events, 257.7 us)
where the time goes:
time: 248 us; the launch traced here: 247 us
  waiting for transfers between devices  118 us (48%)
  starting transfers between devices  53.6 us (22%)
  local copies, waits for them, and re-layouts  31.2 us (13%)
  Pallas kernels  29.7 us (12%)
  other arithmetic  13.9 us (6%)
    ppermute x16, waiting for transfers between devices, from_x(): lax.ppermute(block, 'ctx', [((c + step) % count, c) for c in range(count)])  61.8 us
    ppermute x4, waiting for transfers between devices, from_z(): return lax.ppermute(block, ('section', 'tensor'), route)  27.5 us
    ppermute x16, starting transfers between devices, from_x(): lax.ppermute(block, 'ctx', [((c + step) % count, c) for c in range(count)])  23.2 us
    ppermute x8, waiting for transfers between devices, from_tensor(): return lax.ppermute(block, 'tensor', [(t, t ^ flip) for t in range(count)])  23 us
    ppermute x8, starting transfers between devices, from_tensor(): return lax.ppermute(block, 'tensor', [(t, t ^ flip) for t in range(count)])  20 us
    unnamed x54, local copies, waits for them, and re-layouts  12.8 us
    pallas_call x2, Pallas kernels, project(): pl.pallas_call(functools.partial(project_kernel, turned=turned), grid_spe...  9.37 us
    pallas_call x1, Pallas kernels, attend(): pl.pallas_call(attend_kernel, grid=(batches, queries.shape[1] // wide), i...  9.32 us
  transfers between devices with their start and end apart: 30, of which 13 were waited for; matrix products, arithmetic and copies ran while one was open for 12% of the time, Pallas kernels for 10%

commit v1 on v0

--- a/solution.py
+++ b/solution.py
@@ -13,11 +13,29 @@
 rope_base = 500000.0
 BF = jnp.bfloat16
 F32 = jnp.float32
-STRIPS = (5, 3)
+STRIPS = (1, 1)
+HOLD_FLOPS = 10**10
 
 
 def after(value, *earlier):
     return lax.optimization_barrier((value,) + earlier)[0]
+
+
+def hold_kernel(*refs):
+    del refs
+
+
+def hold(value, *earlier):
+    anywhere = pl.BlockSpec(memory_space=pl.ANY)
+    return pl.pallas_call(
+        hold_kernel,
+        in_specs=[anywhere] * (1 + len(earlier)),
+        out_specs=anywhere,
+        out_shape=jax.ShapeDtypeStruct(value.shape, value.dtype),
+        input_output_aliases={0: 0},
+        cost_estimate=pl.CostEstimate(flops=HOLD_FLOPS, transcendentals=0, bytes_accessed=1024),
+        name="hold",
+    )(value, *earlier)
 
 
 def z_route(step, sections, tensors):
@@ -108,11 +126,13 @@
     return out.reshape(4, 2 * rows, width)
 
 
-def project_kernel(index_ref, normed_ref, own_ref, ahead_ref, across_ref, behind_ref, cosine_ref, sine_ref, out_ref, *, turned):
-    shards = (own_ref, ahead_ref, across_ref, behind_ref)
+def project_kernel(index_ref, normed_ref, *refs, pieces, turned):
+    piece_refs, (cosine_ref, sine_ref, out_ref) = refs[: len(pieces)], refs[len(pieces) :]
     total = sum(
-        jnp.dot(normed_ref[index_ref[step]], shard[...], preferred_element_type=F32)
-        for step, shard in enumerate(shards)
+        jnp.dot(
+            normed_ref[index_ref[step], :, low : low + ref.shape[0]], ref[...], preferred_element_type=F32
+        )
+        for (step, low), ref in zip(pieces, piece_refs)
     )
     for head in range(total.shape[1] // HEAD):
         raw = total[:, head * HEAD : (head + 1) * HEAD]
@@ -123,17 +143,18 @@
 
 def project(order, normed, shards, cosine, sine, turned, name):
     blocks, tokens, depth = normed.shape
-    columns = shards[0].shape[1]
+    arrays = [array for array, _, _ in shards]
+    columns = arrays[0].shape[1]
     wide = 2 * HEAD
     whole = lambda n, order: (0, 0)
     strip = lambda n, order: (0, n)
     return pl.pallas_call(
-        functools.partial(project_kernel, turned=turned),
+        functools.partial(project_kernel, pieces=[(step, low) for _, step, low in shards], turned=turned),
         grid_spec=pltpu.PrefetchScalarGridSpec(
             num_scalar_prefetch=1,
             grid=(columns // wide,),
             in_specs=[pl.BlockSpec((blocks, tokens, depth), lambda n, order: (0, 0, 0))]
-            + [pl.BlockSpec((depth, wide), strip)] * 4
+            + [pl.BlockSpec((array.shape[0], wide), strip) for array in arrays]
             + [pl.BlockSpec((tokens, HEAD), whole)] * 2,
             out_specs=pl.BlockSpec((tokens, wide), strip),
         ),
@@ -141,7 +162,7 @@
         compiler_params=pltpu.CompilerParams(vmem_limit_bytes=32 << 20),
         cost_estimate=pl.CostEstimate(flops=1024, transcendentals=0, bytes_accessed=1024),
         name=name,
-    )(order, normed, *shards, cosine, sine)
+    )(order, normed, *arrays, cosine, sine)
 
 
 def attend_kernel(query_ref, key_ref, value_ref, query_doc_ref, key_doc_ref, out_ref, bias_ref):
@@ -191,9 +212,16 @@
     )(queries, pairs, pairs, query_docs, key_docs)
 
 
-def spread_kernel(index_ref, mixed_ref, own_ref, ahead_ref, across_ref, behind_ref, sent_kept_ref, sent_passed_ref, kept_ref, passed_ref, terms_ref):
-    for step, shard in enumerate((own_ref, ahead_ref, across_ref, behind_ref)):
+def spread_kernel(
+    index_ref, mixed_ref, own_ref, ahead_ref, near_ref, back_ref, behind_ref,
+    sent_kept_ref, sent_passed_ref, kept_ref, passed_ref, terms_ref,
+):
+    half = near_ref.shape[0]
+    for step, shard in ((0, own_ref), (1, ahead_ref), (3, behind_ref)):
         terms_ref[step] = jnp.dot(mixed_ref[...], shard[...], preferred_element_type=F32)
+    terms_ref[2] = jnp.dot(mixed_ref[:, :half], near_ref[...], preferred_element_type=F32) + jnp.dot(
+        mixed_ref[:, half:], back_ref[...], preferred_element_type=F32
+    )
     sent_kept_ref[...] = terms_ref[index_ref[1]].astype(BF)
     sent_passed_ref[...] = terms_ref[index_ref[3]].astype(BF)
     kept_ref[...] = terms_ref[index_ref[0]]
@@ -205,7 +233,7 @@
     columns = shards[0].shape[1]
     return pl.pallas_call(
         spread_kernel,
-        in_specs=[pl.BlockSpec(memory_space=pltpu.SMEM)] + [pl.BlockSpec(memory_space=pltpu.VMEM)] * 5,
+        in_specs=[pl.BlockSpec(memory_space=pltpu.SMEM)] + [pl.BlockSpec(memory_space=pltpu.VMEM)] * 6,
         out_specs=[pl.BlockSpec(memory_space=pltpu.VMEM)] * 4,
         out_shape=[
             jax.ShapeDtypeStruct((tokens, columns), BF),
@@ -255,32 +283,28 @@
     both = jnp.concatenate((mine, held), axis=0)
     with jax.named_scope("z_in"):
         up, down = from_z(both, 2), from_z(both, -2)
+    with jax.named_scope("far"):
+        mine_far = from_tensor(mine, 2)
     q_weight = query_weight[0]
+    depth = q_weight.shape[0] // 2
     with jax.named_scope("q_hop1"):
         q_ahead, q_behind = first_hop(after(q_weight, kv_ahead, kv_behind))
+    q_ahead, q_behind, kv_ahead, up, down, mine_far = lax.optimization_barrier(
+        (q_ahead, q_behind, kv_ahead, up, down, mine_far)
+    )
+    with jax.named_scope("q_hop2"):
+        across_low, across_high = second_hop(q_ahead, q_behind)
+    with jax.named_scope("kv_hop2"):
+        kv_across = from_x(kv_ahead, 1)
+
     stashed = jnp.where(near_high, up[:rows], down[:rows])
     fetched = jnp.where(near_high, up[rows:], down[rows:])
     fetched_far = jnp.where(near_high, down[rows:], up[rows:])
-    near_blocks = jnp.concatenate((mine, fetched, fetched_far), axis=0)
-    with jax.named_scope("sib_near"):
-        sib_near = from_tensor(near_blocks, 1)
-    up, down, q_ahead, q_behind, kv_ahead, kv_behind, sib_near = lax.optimization_barrier(
-        (up, down, q_ahead, q_behind, kv_ahead, kv_behind, sib_near)
-    )
-
-    with jax.named_scope("kv_hop2"):
-        kv_across = jnp.concatenate(second_hop(kv_ahead, kv_behind), axis=0)
-    with jax.named_scope("q_hop2"):
-        q_across = jnp.concatenate(second_hop(q_ahead, q_behind), axis=0)
-    with jax.named_scope("far"):
-        mine_far = jnp.concatenate((from_z(up[:half], 2), from_z(down[half:rows], -2)), axis=0)
-    with jax.named_scope("out_hop1_0"):
-        out_hops = [first_hop(after(out_own[0], kv_across))]
-    with jax.named_scope("sib_far"):
-        sib_far = from_tensor(mine_far, 1)
+    with jax.named_scope("sib"):
+        sib = from_tensor(jnp.concatenate((mine, fetched, fetched_far, mine_far), axis=0), 1)
     blocks = (
-        ((mine, 0), (sib_near, 0), (mine_far, 0), (sib_far, 0))
-        + ((fetched, 0), (sib_near, 1), (fetched_far, 0), (sib_near, 2))
+        ((mine, 0), (sib, 0), (mine_far, 0), (sib, 3))
+        + ((fetched, 0), (sib, 1), (fetched_far, 0), (sib, 2))
     )
     gains = norm_gain[0].reshape(-1, width)
     normed = normalize(blocks, jnp.take(gains, t ^ flips, axis=0), rows)
@@ -290,8 +314,8 @@
 
     own_kv = project(
         feature_order,
-        after(normed, q_across),
-        (kv_weight, kv_ahead, kv_across, kv_behind),
+        normed,
+        ((kv_weight, 0, 0), (kv_ahead, 1, 0), (kv_across, 2, 0), (kv_behind, 3, 0)),
         cosine,
         sine,
         1,
@@ -302,6 +326,8 @@
     own_pair = jnp.concatenate((ids, own_kv.reshape(2, rows, 2 * HEAD)), axis=1)
     with jax.named_scope("kv_rows"):
         kv_one, kv_two = from_before(own_pair, 1), from_before(own_pair, 2)
+    with jax.named_scope("out_hop1_0"):
+        out_hops = [first_hop(hold(out_own[0], across_low, across_high, kv_across))]
     all_kv = jnp.concatenate((kv_two[:, id_rows:], kv_one[:, id_rows:], own_pair[:, id_rows:]), axis=1)
     docs_one = jnp.where(c >= 1, kv_one[:, 0].astype(jnp.int32), -1)
     docs_two = jnp.where(c >= 2, kv_two[:, 0].astype(jnp.int32), -1)
@@ -309,7 +335,13 @@
     queries = project(
         feature_order,
         after(normed, own_kv),
-        (q_weight, q_ahead, q_across, q_behind),
+        (
+            (q_weight, 0, 0),
+            (q_ahead, 1, 0),
+            (q_behind, 3, 0),
+            (across_low, 2, 0),
+            (across_high, 2, depth),
+        ),
         cosine,
         sine,
         2,
@@ -324,17 +356,20 @@
     for index, (low, high) in enumerate(strips):
         ahead, behind = out_hops[index]
         with jax.named_scope("out_hop2_%d" % index):
-            across = jnp.concatenate(second_hop(ahead, behind), axis=0)
+            near, back = second_hop(ahead, behind)
         if index + 1 < len(strips):
             with jax.named_scope("out_hop1_%d" % (index + 1)):
-                out_hops.append(first_hop(after(out_own[index + 1], across)))
+                out_hops.append(first_hop(after(out_own[index + 1], ahead, behind)))
         sent_kept, sent_passed, kept, passed = spread(
-            term_order, after(mixed, *passed_before), (out_own[index], ahead, across, behind), "spread_%d" % index
+            term_order,
+            after(mixed, *passed_before),
+            (out_own[index], ahead, near, back, behind),
+            "spread_%d" % index,
         )
-        if index:
-            sent_passed = after(sent_passed, outputs[-1])
         with jax.named_scope("core_passed_%d" % index):
             passed = (passed + from_tensor(sent_passed, 1).astype(F32)).astype(BF)
+        if index:
+            passed = after(passed, outputs[-1])
         with jax.named_scope("z_sum_%d" % index):
             arrived = from_tensor(passed, 2)
         with jax.named_scope("core_kept_%d" % index):

time: 248 us -> 263 us (1.060)
  the two profiles are of different devices: /device:TPU:79 before, /device:TPU:49 now
where the time goes in v1:
time: 263 us
  waiting for transfers between devices  134 us (51%)
  starting transfers between devices  58.5 us (22%)
  Pallas kernels  30.9 us (12%)
  local copies, waits for them, and re-layouts  24.2 us (9%)
  other arithmetic  14.1 us (5%)
    ppermute x8, waiting for transfers between devices, from_tensor(): return lax.ppermute(block, 'tensor', [(t, t ^ flip) for t in range(count)])  92.6 us
    ppermute x15, waiting for transfers between devices, from_x(): lax.ppermute(block, 'ctx', [((c + step) % count, c) for c in range(count)])  41.3 us
    ppermute x8, starting transfers between devices, from_tensor(): return lax.ppermute(block, 'tensor', [(t, t ^ flip) for t in range(count)])  27.9 us
    ppermute x15, starting transfers between devices, from_x(): lax.ppermute(block, 'ctx', [((c + step) % count, c) for c in range(count)])  17.1 us
    pallas_call x2, Pallas kernels, project(): pl.pallas_call(functools.partial(project_kernel, pieces=[(step, low) for...  12.3 us
    unnamed x49, local copies, waits for them, and re-layouts  11.5 us
    pallas_call x1, Pallas kernels, attend(): pl.pallas_call(attend_kernel, grid=(batches, queries.shape[1] // wide), i...  9.32 us
    ppermute x2, starting transfers between devices, from_before(): lax.ppermute(block, 'ctx', [(c - step, c) for c in range(step, count)])  8.39 us
  transfers between devices with their start and end apart: 27, of which 10 were waited for; matrix products, arithmetic and copies ran while one was open for 10% of the time, Pallas kernels for 12%

profile of v1, /device:TPU:49, one launch (start us, length us, event | category | flops | bytes accessed | tf_op | source)
XLA Modules:
  0.0 262.5 jit_solution(9567185432888651867)
XLA Ops:
  1.8 2.6 collective-permute-start
  5.2 9.8 %collective-permute-done.refs_1_ = bf16[1024,256]{1,0:T(8,128)(2,1)} collective-permute-done((bf16[1024,256]{1,0:T(8,128)(2,1)S(1)}, bf16[1024,256]{1,0:T(8,128)(2,1)}, u32[]{:S(2)}, u32[]{:S(2)}) %collective-permute-start) | collective-permute-done | bytes 524320 | tf_op jit(solution)/shard_map/kv_hop1/ppermute | solution.py:65
  14.9 3.1 %collective-permute-done.1.refs_3_ = bf16[1024,256]{1,0:T(8,128)(2,1)S(1)} collective-permute-done((bf16[1024,256]{1,0:T(8,128)(2,1)S(1)}, bf16[1024,256]{1,0:T(8,128)(2,1)S(1)}, u32[]{:S(2)}, u32[]{:S(2)}) %collective-permute-start.1) | collective-permute-done | bytes 524320 | tf_op jit(solution)/shard_map/kv_hop1/ppermute | solution.py:65
  22.6 5.1 %collective-permute-start.4 = (bf16[512,1024]{1,0:T(8,128)(2,1)}, bf16[512,1024]{1,0:T(8,128)(2,1)}, u32[]{:S(2)}, u32[]{:S(2)}) collective-permute-start(bf16[512,1024]{1,0:T(8,128)(2,1)} %pad_maximum_fusion.1), channel_id=1, source_target_pairs={{128,0},{129,1},{144,16},{145,17},{160,32},{161,33},{176,48},{177,... | collective-permute-start | bytes 3145736 | tf_op jit(solution)/shard_map/z_in/ppermute | solution.py:60
  27.7 3.3 %collective-permute-start.6 = (bf16[256,1024]{1,0:T(8,128)(2,1)S(1)}, bf16[256,1024]{1,0:T(8,128)(2,1)S(1)}, u32[]{:S(2)}, u32[]{:S(2)}) collective-permute-start(bf16[256,1024]{1,0:T(8,128)(2,1)S(1)} %bitcast.25), channel_id=1, source_target_pairs={{0,2},{1,3},{2,0},{3,1},{4,6},{5,7},{6,4},{7,5},{8,10},{9,11},{10,... | collective-permute-start | bytes 1572872 | tf_op jit(solution)/shard_map/far/ppermute | solution.py:75
  30.9 3.0 %fusion.11 = (bf16[1024,512]{1,0:T(8,128)(2,1)}, bf16[1024,512]{1,0:T(8,128)(2,1)}) fusion(bf16[1024,1024]{1,0:T(8,128)(2,1)} %bitcast.34), kind=kLoop, calls=%fused_computation.52 | loop fusion | bytes 4194304 | tf_op jit(solution)/shard_map/slice | solution.py:278
  33.9 61.5 %collective-permute-done.6.refs_2_ = bf16[256,1024]{1,0:T(8,128)(2,1)S(1)} collective-permute-done((bf16[256,1024]{1,0:T(8,128)(2,1)S(1)}, bf16[256,1024]{1,0:T(8,128)(2,1)S(1)}, u32[]{:S(2)}, u32[]{:S(2)}) %collective-permute-start.6) | collective-permute-done | bytes 524320 | tf_op jit(solution)/shard_map/far/ppermute | solution.py:75
  104.8 5.2 %collective-permute-start.7 = (bf16[1024,1024]{1,0:T(8,128)(2,1)}, bf16[1024,1024]{1,0:T(8,128)(2,1)S(1)}, u32[]{:S(2)}, u32[]{:S(2)}) collective-permute-start(bf16[1024,1024]{1,0:T(8,128)(2,1)} %pad_maximum_fusion), channel_id=1, source_target_pairs={{0,1},{1,0},{2,3},{3,2},{4,5},{5,4},{6,7},{7,6},{8,9},{9,8},{10,11... | collective-permute-start | bytes 6291464 | tf_op jit(solution)/shard_map/sib/ppermute | solution.py:75
  110.0 2.9 %collective-permute-start.8 = (bf16[1024,256]{1,0:T(8,128)(2,1)}, bf16[1024,256]{1,0:T(8,128)(2,1)}, u32[]{:S(2)}, u32[]{:S(2)}) collective-permute-start(bf16[1024,256]{1,0:T(8,128)(2,1)} %collective-permute-done.refs_1_), channel_id=1, source_target_pairs={{4,0},{8,4},{12,8},{0,12},{5,1},{9,5},{13,9},{1,13},{6,2},{10,6},{... | collective-permute-start | bytes 1572872 | tf_op jit(solution)/shard_map/kv_hop2/ppermute | solution.py:65
  115.9 11.8 %collective-permute-done.8.refs_2_.refs_3_ = bf16[1024,256]{1,0:T(8,128)(2,1)} collective-permute-done((bf16[1024,256]{1,0:T(8,128)(2,1)}, bf16[1024,256]{1,0:T(8,128)(2,1)}, u32[]{:S(2)}, u32[]{:S(2)}) %collective-permute-start.8) | collective-permute-done | bytes 524320 | tf_op jit(solution)/shard_map/kv_hop2/ppermute | solution.py:65
  127.7 3.5 %collective-permute-start.13 = (bf16[1024,512]{1,0:T(8,128)(2,1)}, bf16[1024,512]{1,0:T(8,128)(2,1)}, u32[]{:S(2)}, u32[]{:S(2)}) collective-permute-start(bf16[1024,512]{1,0:T(8,128)(2,1)} %hold.1), channel_id=1, source_target_pairs={{4,0},{8,4},{12,8},{0,12},{5,1},{9,5},{13,9},{1,13},{6,2},{10,6},{... | collective-permute-start | bytes 3145736 | tf_op jit(solution)/shard_map/out_hop1_0/ppermute | solution.py:65
  136.2 4.6 %project_kv.1 = bf16[512,256]{1,0:T(8,128)(2,1)S(1)} custom-call(s32[4]{0:T(128)S(1)} %fusion.7.index_ref, bf16[4,512,1024]{2,1,0:T(8,128)(2,1)S(1)} %bitcast.22, bf16[1024,256]{1,0:T(8,128)(2,1)S(1)} %copy-done.12, bf16[1024,256]{1,0:T(8,128)(2,1)} %collective-permute-done.refs_1_, bf16[1024,256]{1,0:T(8,128)(2,1)} %collective-permute-done.8.refs_2_.refs_3_, ...), custom_call_target="tpu_custom_call" | custom-call | flops 1024 | bytes 1024 | tf_op jit(solution)/shard_map/project_kv/pallas_call | solution.py:151
  144.9 6.4 %collective-permute-start.11 = (bf16[2,272,256]{2,0,1:T(2,128)(2,1)}, bf16[2,272,256]{2,0,1:T(2,128)(2,1)}, u32[]{:S(2)}, u32[]{:S(2)}) collective-permute-start(bf16[2,272,256]{2,0,1:T(2,128)(2,1)} %pad_maximum_fusion.6), channel_id=1, source_target_pairs={{0,8},{4,12},{1,9},{5,13},{2,10},{6,14},{3,11},{7,15},{16,24},{20,... | collective-permute-start | bytes 835592 | tf_op jit(solution)/shard_map/kv_rows/ppermute | solution.py:70
  156.9 7.6 %project_q.1.query_ref = bf16[512,1024]{1,0:T(8,128)(2,1)S(1)} custom-call(s32[4]{0:T(128)S(1)} %fusion.7.index_ref, bf16[4,512,1024]{2,1,0:T(8,128)(2,1)S(1)} %bitcast.23, bf16[1024,1024]{1,0:T(8,128)(2,1)S(1)} %bitcast.32, bf16[1024,1024]{1,0:T(8,128)(2,1)S(1)} %copy-done.5, bf16[1024,1024]{1,0:T(8,128)(2,1)} %collective-permute-done.3.refs_2_, ...), custom_call_target="tpu_custom_call" | custom-call | flops 1024 | bytes 1024 | tf_op jit(solution)/shard_map/project_q/pallas_call | solution.py:151
  175.0 9.3 %attend.1.mixed_ref = bf16[512,1024]{1,0:T(8,128)(2,1)S(1)} custom-call(bf16[512,1024]{1,0:T(8,128)(2,1)S(1)} %project_q.1.query_ref, bf16[2,768,256]{2,1,0:T(8,128)(2,1)S(1)} %copy.18.key_ref.value_ref, bf16[2,768,256]{2,1,0:T(8,128)(2,1)S(1)} %copy.18.key_ref.value_ref, s32[2,256,1]{2,1,0:T(8,128)S(1)} %copy-done.16, ...), custom_call_target="tpu_custom_call" | custom-call | flops 1024 | bytes 1024 | tf_op jit(solution)/shard_map/attend/pallas_call | solution.py:196
  184.3 8.4 %collective-permute-done.14.near_ref = bf16[512,512]{1,0:T(8,128)(2,1)S(1)} collective-permute-done((bf16[512,512]{1,0:T(8,128)(2,1)S(1)}, bf16[512,512]{1,0:T(8,128)(2,1)S(1)}, u32[]{:S(2)}, u32[]{:S(2)}) %collective-permute-start.14) | collective-permute-done | bytes 524320 | tf_op jit(solution)/shard_map/out_hop2_0/ppermute | solution.py:65
  194.0 4.1 %spread_0.1 = (bf16[512,512]{1,0:T(8,128)(2,1)S(1)}, bf16[512,512]{1,0:T(8,128)(2,1)S(1)}, f32[512,512]{1,0:T(8,128)S(1)}, f32[512,512]{1,0:T(8,128)S(1)}) custom-call(s32[4]{0:T(128)S(1)} %and_select_fusion.1.index_ref, bf16[512,1024]{1,0:T(8,128)(2,1)S(1)} %attend.1.mixed_ref, bf16[1024,512]{1,0:T(8,128)(2,1)S(1)} %copy-done.3, ...), custom_call_target="tpu_custom_call" | custom-call | flops 1024 | bytes 1024 | tf_op jit(solution)/shard_map/spread_0/pallas_call | solution.py:234
  198.1 8.9 %collective-permute-start.18 = (bf16[512,512]{1,0:T(8,128)(2,1)S(1)}, bf16[512,512]{1,0:T(8,128)(2,1)S(1)}, u32[]{:S(2)}, u32[]{:S(2)}) collective-permute-start(bf16[512,512]{1,0:T(8,128)(2,1)S(1)} %get-tuple-element.33), channel_id=1, source_target_pairs={{0,1},{1,0},{2,3},{3,2},{4,5},{5,4},{6,7},{7,6},{8,9},{9,8},{10,11... | collective-permute-start | bytes 1572872 | tf_op jit(solution)/shard_map/core_passed_0/ppermute | solution.py:75
  209.2 5.8 %collective-permute-start.19 = (bf16[512,512]{1,0:T(8,128)(2,1)S(1)}, bf16[512,512]{1,0:T(8,128)(2,1)S(1)}, u32[]{:S(2)}, u32[]{:S(2)}) collective-permute-start(bf16[512,512]{1,0:T(8,128)(2,1)S(1)} %add_convert_fusion.3), channel_id=1, source_target_pairs={{0,2},{1,3},{2,0},{3,1},{4,6},{5,7},{6,4},{7,5},{8,10},{9,11},{10,... | collective-permute-start | bytes 1572872 | tf_op jit(solution)/shard_map/z_sum_0/ppermute | solution.py:75
  215.0 5.8 %collective-permute-done.21.near_ref = bf16[512,512]{1,0:T(8,128)(2,1)S(1)} collective-permute-done((bf16[512,512]{1,0:T(8,128)(2,1)S(1)}, bf16[512,512]{1,0:T(8,128)(2,1)S(1)}, u32[]{:S(2)}, u32[]{:S(2)}) %collective-permute-start.21) | collective-permute-done | bytes 524320 | tf_op jit(solution)/shard_map/out_hop2_1/ppermute | solution.py:65
  222.0 3.1 %spread_1.1 = (bf16[512,512]{1,0:T(8,128)(2,1)S(1)}, bf16[512,512]{1,0:T(8,128)(2,1)S(1)}, f32[512,512]{1,0:T(8,128)S(1)}, f32[512,512]{1,0:T(8,128)S(1)}) custom-call(s32[4]{0:T(128)S(1)} %and_select_fusion.1.index_ref, bf16[512,1024]{1,0:T(8,128)(2,1)S(1)} %attend.1.mixed_ref, bf16[1024,512]{1,0:T(8,128)(2,1)S(1)} %copy-done.8, ...), custom_call_target="tpu_custom_call" | custom-call | flops 1024 | bytes 1024 | tf_op jit(solution)/shard_map/spread_1/pallas_call | solution.py:234
  226.4 10.1 %collective-permute-done.19 = bf16[512,512]{1,0:T(8,128)(2,1)S(1)} collective-permute-done((bf16[512,512]{1,0:T(8,128)(2,1)S(1)}, bf16[512,512]{1,0:T(8,128)(2,1)S(1)}, u32[]{:S(2)}, u32[]{:S(2)}) %collective-permute-start.19) | collective-permute-done | bytes 524320 | tf_op jit(solution)/shard_map/z_sum_0/ppermute | solution.py:75
  237.6 2.5 collective-permute-start.26
  240.1 21.0 %collective-permute-done.26 = bf16[512,512]{1,0:T(8,128)(2,1)S(1)} collective-permute-done((bf16[512,512]{1,0:T(8,128)(2,1)S(1)}, bf16[512,512]{1,0:T(8,128)(2,1)S(1)}, u32[]{:S(2)}, u32[]{:S(2)}) %collective-permute-start.26) | collective-permute-done | bytes 524320 | tf_op jit(solution)/shard_map/z_sum_1/ppermute | solution.py:75
  (128 shorter events, 52.2 us)
Async XLA Ops:
  1.8 13.1 %collective-permute-start = (bf16[1024,256]{1,0:T(8,128)(2,1)S(1)}, bf16[1024,256]{1,0:T(8,128)(2,1)}, u32[]{:S(2)}, u32[]{:S(2)}) collective-permute-start(bf16[1024,256]{1,0:T(8,128)(2,1)S(1)} %pad_maximum_fusion.5.refs_0_), channel_id=1, source_target_pairs={{4,0},{8,4},{12,8},{0,12},{5,1},{9,5},{13,9},{1,13},{6,2},{10,6},{... | collective-permute-start | bytes 1572872 | tf_op jit(solution)/shard_map/kv_hop1/ppermute | solution.py:65
  4.3 13.7 %collective-permute-start.1 = (bf16[1024,256]{1,0:T(8,128)(2,1)S(1)}, bf16[1024,256]{1,0:T(8,128)(2,1)S(1)}, u32[]{:S(2)}, u32[]{:S(2)}) collective-permute-start(bf16[1024,256]{1,0:T(8,128)(2,1)S(1)} %pad_maximum_fusion.5.refs_0_), channel_id=1, source_target_pairs={{12,0},{0,4},{4,8},{8,12},{13,1},{1,5},{5,9},{9,13},{14,2},{2,6},{... | collective-permute-start | bytes 1572872 | tf_op jit(solution)/shard_map/kv_hop1/ppermute | solution.py:65
  18.8 76.6 %collective-permute-start.2 = (bf16[1024,1024]{1,0:T(8,128)(2,1)}, bf16[1024,1024]{1,0:T(8,128)(2,1)S(1)}, u32[]{:S(2)}, u32[]{:S(2)}) collective-permute-start(bf16[1024,1024]{1,0:T(8,128)(2,1)} %bitcast.30), channel_id=1, source_target_pairs={{4,0},{8,4},{12,8},{0,12},{5,1},{9,5},{13,9},{1,13},{6,2},{10,6},{... | collective-permute-start | bytes 6291464 | tf_op jit(solution)/shard_map/q_hop1/ppermute | solution.py:65
  19.3 76.2 %collective-permute-start.3 = (bf16[1024,1024]{1,0:T(8,128)(2,1)}, bf16[1024,1024]{1,0:T(8,128)(2,1)}, u32[]{:S(2)}, u32[]{:S(2)}) collective-permute-start(bf16[1024,1024]{1,0:T(8,128)(2,1)} %bitcast.31), channel_id=1, source_target_pairs={{12,0},{0,4},{4,8},{8,12},{13,1},{1,5},{5,9},{9,13},{14,2},{2,6},{... | collective-permute-start | bytes 6291464 | tf_op jit(solution)/shard_map/q_hop1/ppermute | solution.py:65
  22.6 72.8 %collective-permute-start.4 = (bf16[512,1024]{1,0:T(8,128)(2,1)}, bf16[512,1024]{1,0:T(8,128)(2,1)}, u32[]{:S(2)}, u32[]{:S(2)}) collective-permute-start(bf16[512,1024]{1,0:T(8,128)(2,1)} %pad_maximum_fusion.1), channel_id=1, source_target_pairs={{128,0},{129,1},{144,16},{145,17},{160,32},{161,33},{176,48},{177,... | collective-permute-start | bytes 3145736 | tf_op jit(solution)/shard_map/z_in/ppermute | solution.py:60
  27.7 67.7 %collective-permute-start.5 = (bf16[512,1024]{1,0:T(8,128)(2,1)}, bf16[512,1024]{1,0:T(8,128)(2,1)}, u32[]{:S(2)}, u32[]{:S(2)}) collective-permute-start(bf16[512,1024]{1,0:T(8,128)(2,1)} %pad_maximum_fusion.1), channel_id=1, source_target_pairs={{130,0},{131,1},{146,16},{147,17},{162,32},{163,33},{178,48},{179,... | collective-permute-start | bytes 3145736 | tf_op jit(solution)/shard_map/z_in/ppermute | solution.py:60
  27.7 67.7 %collective-permute-start.6 = (bf16[256,1024]{1,0:T(8,128)(2,1)S(1)}, bf16[256,1024]{1,0:T(8,128)(2,1)S(1)}, u32[]{:S(2)}, u32[]{:S(2)}) collective-permute-start(bf16[256,1024]{1,0:T(8,128)(2,1)S(1)} %bitcast.25), channel_id=1, source_target_pairs={{0,2},{1,3},{2,0},{3,1},{4,6},{5,7},{6,4},{7,5},{8,10},{9,11},{10,... | collective-permute-start | bytes 1572872 | tf_op jit(solution)/shard_map/far/ppermute | solution.py:75
  96.6 31.1 %collective-permute-start.9 = (bf16[512,1024]{1,0:T(8,128)(2,1)}, bf16[512,1024]{1,0:T(8,128)(2,1)}, u32[]{:S(2)}, u32[]{:S(2)}) collective-permute-start(bf16[512,1024]{1,0:T(8,128)(2,1)} %slice.65), channel_id=1, source_target_pairs={{4,0},{8,4},{12,8},{0,12},{5,1},{9,5},{13,9},{1,13},{6,2},{10,6},{... | collective-permute-start | bytes 3145736 | tf_op jit(solution)/shard_map/q_hop2/ppermute | solution.py:65
  100.8 26.9 %collective-permute-start.10 = (bf16[512,1024]{1,0:T(8,128)(2,1)}, bf16[512,1024]{1,0:T(8,128)(2,1)}, u32[]{:S(2)}, u32[]{:S(2)}) collective-permute-start(bf16[512,1024]{1,0:T(8,128)(2,1)} %slice.66), channel_id=1, source_target_pairs={{12,0},{0,4},{4,8},{8,12},{13,1},{1,5},{5,9},{9,13},{14,2},{2,6},{... | collective-permute-start | bytes 3145736 | tf_op jit(solution)/shard_map/q_hop2/ppermute | solution.py:65
  104.8 27.2 %collective-permute-start.7 = (bf16[1024,1024]{1,0:T(8,128)(2,1)}, bf16[1024,1024]{1,0:T(8,128)(2,1)S(1)}, u32[]{:S(2)}, u32[]{:S(2)}) collective-permute-start(bf16[1024,1024]{1,0:T(8,128)(2,1)} %pad_maximum_fusion), channel_id=1, source_target_pairs={{0,1},{1,0},{2,3},{3,2},{4,5},{5,4},{6,7},{7,6},{8,9},{9,8},{10,11... | collective-permute-start | bytes 6291464 | tf_op jit(solution)/shard_map/sib/ppermute | solution.py:75
  110.0 17.6 %collective-permute-start.8 = (bf16[1024,256]{1,0:T(8,128)(2,1)}, bf16[1024,256]{1,0:T(8,128)(2,1)}, u32[]{:S(2)}, u32[]{:S(2)}) collective-permute-start(bf16[1024,256]{1,0:T(8,128)(2,1)} %collective-permute-done.refs_1_), channel_id=1, source_target_pairs={{4,0},{8,4},{12,8},{0,12},{5,1},{9,5},{13,9},{1,13},{6,2},{10,6},{... | collective-permute-start | bytes 1572872 | tf_op jit(solution)/shard_map/kv_hop2/ppermute | solution.py:65
  127.7 36.9 %collective-permute-start.13 = (bf16[1024,512]{1,0:T(8,128)(2,1)}, bf16[1024,512]{1,0:T(8,128)(2,1)}, u32[]{:S(2)}, u32[]{:S(2)}) collective-permute-start(bf16[1024,512]{1,0:T(8,128)(2,1)} %hold.1), channel_id=1, source_target_pairs={{4,0},{8,4},{12,8},{0,12},{5,1},{9,5},{13,9},{1,13},{6,2},{10,6},{... | collective-permute-start | bytes 3145736 | tf_op jit(solution)/shard_map/out_hop1_0/ppermute | solution.py:65
  131.2 33.4 %collective-permute-start.15 = (bf16[1024,512]{1,0:T(8,128)(2,1)}, bf16[1024,512]{1,0:T(8,128)(2,1)}, u32[]{:S(2)}, u32[]{:S(2)}) collective-permute-start(bf16[1024,512]{1,0:T(8,128)(2,1)} %hold.1), channel_id=1, source_target_pairs={{12,0},{0,4},{4,8},{8,12},{13,1},{1,5},{5,9},{9,13},{14,2},{2,6},{... | collective-permute-start | bytes 3145736 | tf_op jit(solution)/shard_map/out_hop1_0/ppermute | solution.py:65
  142.9 26.8 %collective-permute-start.12 = (bf16[2,272,256]{2,0,1:T(2,128)(2,1)}, bf16[2,272,256]{2,0,1:T(2,128)(2,1)}, u32[]{:S(2)}, u32[]{:S(2)}) collective-permute-start(bf16[2,272,256]{2,0,1:T(2,128)(2,1)} %pad_maximum_fusion.6), channel_id=1, source_target_pairs={{0,4},{4,8},{8,12},{1,5},{5,9},{9,13},{2,6},{6,10},{10,14},{3,7},{... | collective-permute-start | bytes 835592 | tf_op jit(solution)/shard_map/kv_rows/ppermute | solution.py:70
  144.9 26.1 %collective-permute-start.11 = (bf16[2,272,256]{2,0,1:T(2,128)(2,1)}, bf16[2,272,256]{2,0,1:T(2,128)(2,1)}, u32[]{:S(2)}, u32[]{:S(2)}) collective-permute-start(bf16[2,272,256]{2,0,1:T(2,128)(2,1)} %pad_maximum_fusion.6), channel_id=1, source_target_pairs={{0,8},{4,12},{1,9},{5,13},{2,10},{6,14},{3,11},{7,15},{16,24},{20,... | collective-permute-start | bytes 835592 | tf_op jit(solution)/shard_map/kv_rows/ppermute | solution.py:70
  164.6 42.7 %collective-permute-start.20 = (bf16[1024,512]{1,0:T(8,128)(2,1)S(1)}, bf16[1024,512]{1,0:T(8,128)(2,1)S(1)}, u32[]{:S(2)}, u32[]{:S(2)}) collective-permute-start(bf16[1024,512]{1,0:T(8,128)(2,1)S(1)} %copy-done.8), channel_id=1, source_target_pairs={{4,0},{8,4},{12,8},{0,12},{5,1},{9,5},{13,9},{1,13},{6,2},{10,6},{... | collective-permute-start | bytes 3145736 | tf_op jit(solution)/shard_map/out_hop1_1/ppermute | solution.py:65
  164.7 42.8 %collective-permute-start.22 = (bf16[1024,512]{1,0:T(8,128)(2,1)S(1)}, bf16[1024,512]{1,0:T(8,128)(2,1)S(1)}, u32[]{:S(2)}, u32[]{:S(2)}) collective-permute-start(bf16[1024,512]{1,0:T(8,128)(2,1)S(1)} %copy-done.8), channel_id=1, source_target_pairs={{12,0},{0,4},{4,8},{8,12},{13,1},{1,5},{5,9},{9,13},{14,2},{2,6},{... | collective-permute-start | bytes 3145736 | tf_op jit(solution)/shard_map/out_hop1_1/ppermute | solution.py:65
  167.2 25.4 %collective-permute-start.14 = (bf16[512,512]{1,0:T(8,128)(2,1)S(1)}, bf16[512,512]{1,0:T(8,128)(2,1)S(1)}, u32[]{:S(2)}, u32[]{:S(2)}) collective-permute-start(bf16[512,512]{1,0:T(8,128)(2,1)S(1)} %slice.91), channel_id=1, source_target_pairs={{4,0},{8,4},{12,8},{0,12},{5,1},{9,5},{13,9},{1,13},{6,2},{10,6},{... | collective-permute-start | bytes 1572872 | tf_op jit(solution)/shard_map/out_hop2_0/ppermute | solution.py:65
  169.7 24.3 %collective-permute-start.16 = (bf16[512,512]{1,0:T(8,128)(2,1)S(1)}, bf16[512,512]{1,0:T(8,128)(2,1)S(1)}, u32[]{:S(2)}, u32[]{:S(2)}) collective-permute-start(bf16[512,512]{1,0:T(8,128)(2,1)S(1)} %slice.92), channel_id=1, source_target_pairs={{12,0},{0,4},{4,8},{8,12},{13,1},{1,5},{5,9},{9,13},{14,2},{2,6},{... | collective-permute-start | bytes 1572872 | tf_op jit(solution)/shard_map/out_hop2_0/ppermute | solution.py:65
  207.0 19.4 %collective-permute-start.17 = (bf16[512,512]{1,0:T(8,128)(2,1)S(1)}, bf16[512,512]{1,0:T(8,128)(2,1)S(1)}, u32[]{:S(2)}, u32[]{:S(2)}) collective-permute-start(bf16[512,512]{1,0:T(8,128)(2,1)S(1)} %get-tuple-element.31), channel_id=1, source_target_pairs={{0,1},{1,0},{2,3},{3,2},{4,5},{5,4},{6,7},{7,6},{8,9},{9,8},{10,11... | collective-permute-start | bytes 1572872 | tf_op jit(solution)/shard_map/core_kept_0/ppermute | solution.py:75
  207.4 13.4 %collective-permute-start.21 = (bf16[512,512]{1,0:T(8,128)(2,1)S(1)}, bf16[512,512]{1,0:T(8,128)(2,1)S(1)}, u32[]{:S(2)}, u32[]{:S(2)}) collective-permute-start(bf16[512,512]{1,0:T(8,128)(2,1)S(1)} %slice.94), channel_id=1, source_target_pairs={{4,0},{8,4},{12,8},{0,12},{5,1},{9,5},{13,9},{1,13},{6,2},{10,6},{... | collective-permute-start | bytes 1572872 | tf_op jit(solution)/shard_map/out_hop2_1/ppermute | solution.py:65
  207.5 14.4 %collective-permute-start.23 = (bf16[512,512]{1,0:T(8,128)(2,1)S(1)}, bf16[512,512]{1,0:T(8,128)(2,1)S(1)}, u32[]{:S(2)}, u32[]{:S(2)}) collective-permute-start(bf16[512,512]{1,0:T(8,128)(2,1)S(1)} %slice.95), channel_id=1, source_target_pairs={{12,0},{0,4},{4,8},{8,12},{13,1},{1,5},{5,9},{9,13},{14,2},{2,6},{... | collective-permute-start | bytes 1572872 | tf_op jit(solution)/shard_map/out_hop2_1/ppermute | solution.py:65
  209.2 27.3 %collective-permute-start.19 = (bf16[512,512]{1,0:T(8,128)(2,1)S(1)}, bf16[512,512]{1,0:T(8,128)(2,1)S(1)}, u32[]{:S(2)}, u32[]{:S(2)}) collective-permute-start(bf16[512,512]{1,0:T(8,128)(2,1)S(1)} %add_convert_fusion.3), channel_id=1, source_target_pairs={{0,2},{1,3},{2,0},{3,1},{4,6},{5,7},{6,4},{7,5},{8,10},{9,11},{10,... | collective-permute-start | bytes 1572872 | tf_op jit(solution)/shard_map/z_sum_0/ppermute | solution.py:75
  237.6 23.5 %collective-permute-start.26 = (bf16[512,512]{1,0:T(8,128)(2,1)S(1)}, bf16[512,512]{1,0:T(8,128)(2,1)S(1)}, u32[]{:S(2)}, u32[]{:S(2)}) collective-permute-start(bf16[512,512]{1,0:T(8,128)(2,1)S(1)} %add_convert_fusion.1), channel_id=1, source_target_pairs={{0,2},{1,3},{2,0},{3,1},{4,6},{5,7},{6,4},{7,5},{8,10},{9,11},{10,... | collective-permute-start | bytes 1572872 | tf_op jit(solution)/shard_map/z_sum_1/ppermute | solution.py:75
  (27 other events, 179.6 us)

commit v2 on v1

--- a/solution.py
+++ b/solution.py
@@ -13,8 +13,8 @@
 rope_base = 500000.0
 BF = jnp.bfloat16
 F32 = jnp.float32
-STRIPS = (1, 1)
-HOLD_FLOPS = 10**10
+STRIPS = (5, 3)
+HOLD_FLOPS = 4 * 10**10
 
 
 def after(value, *earlier):
@@ -277,26 +277,26 @@
         start = strips[-1][1]
     out_own = [out_weight[0][:, low:high] for low, high in strips]
 
+    q_weight = query_weight[0]
+    depth = q_weight.shape[0] // 2
+    with jax.named_scope("q_hop1"):
+        q_ahead, q_behind = first_hop(q_weight)
     kv_weight = jnp.concatenate((key_weight[0], value_projection_weight[0]), axis=1)
     with jax.named_scope("kv_hop1"):
         kv_ahead, kv_behind = first_hop(kv_weight)
     both = jnp.concatenate((mine, held), axis=0)
     with jax.named_scope("z_in"):
         up, down = from_z(both, 2), from_z(both, -2)
-    with jax.named_scope("far"):
-        mine_far = from_tensor(mine, 2)
-    q_weight = query_weight[0]
-    depth = q_weight.shape[0] // 2
-    with jax.named_scope("q_hop1"):
-        q_ahead, q_behind = first_hop(after(q_weight, kv_ahead, kv_behind))
-    q_ahead, q_behind, kv_ahead, up, down, mine_far = lax.optimization_barrier(
-        (q_ahead, q_behind, kv_ahead, up, down, mine_far)
-    )
+    q_ahead, q_behind, kv_ahead, kv_behind, up, down, out_own[0] = lax.optimization_barrier(
+        (q_ahead, q_behind, kv_ahead, kv_behind, up, down, out_own[0])
+    )
+
     with jax.named_scope("q_hop2"):
         across_low, across_high = second_hop(q_ahead, q_behind)
     with jax.named_scope("kv_hop2"):
         kv_across = from_x(kv_ahead, 1)
-
+    with jax.named_scope("far"):
+        mine_far = jnp.concatenate((from_z(up[:half], 2), from_z(down[half:rows], -2)), axis=0)
     stashed = jnp.where(near_high, up[:rows], down[:rows])
     fetched = jnp.where(near_high, up[rows:], down[rows:])
     fetched_far = jnp.where(near_high, down[rows:], up[rows:])
@@ -327,7 +327,8 @@
     with jax.named_scope("kv_rows"):
         kv_one, kv_two = from_before(own_pair, 1), from_before(own_pair, 2)
     with jax.named_scope("out_hop1_0"):
-        out_hops = [first_hop(hold(out_own[0], across_low, across_high, kv_across))]
+        out_own[0] = hold(out_own[0], across_low, across_high, kv_across)
+        out_hops = [first_hop(out_own[0])]
     all_kv = jnp.concatenate((kv_two[:, id_rows:], kv_one[:, id_rows:], own_pair[:, id_rows:]), axis=1)
     docs_one = jnp.where(c >= 1, kv_one[:, 0].astype(jnp.int32), -1)
     docs_two = jnp.where(c >= 2, kv_two[:, 0].astype(jnp.int32), -1)
@@ -347,6 +348,7 @@
         2,
         "project_q",
     )
+    queries, out_own[1] = lax.optimization_barrier((queries, out_own[1]))
     mixed = attend(queries, all_kv, docs[:, :, None], key_docs[:, None, :])
 
     residual = jnp.concatenate((mine, fetched), axis=0)
@@ -359,17 +361,17 @@
             near, back = second_hop(ahead, behind)
         if index + 1 < len(strips):
             with jax.named_scope("out_hop1_%d" % (index + 1)):
-                out_hops.append(first_hop(after(out_own[index + 1], ahead, behind)))
+                out_hops.append(first_hop(after(out_own[index + 1], near, back)))
         sent_kept, sent_passed, kept, passed = spread(
             term_order,
             after(mixed, *passed_before),
             (out_own[index], ahead, near, back, behind),
             "spread_%d" % index,
         )
+        if index:
+            sent_passed = after(sent_passed, outputs[-1])
         with jax.named_scope("core_passed_%d" % index):
             passed = (passed + from_tensor(sent_passed, 1).astype(F32)).astype(BF)
-        if index:
-            passed = after(passed, outputs[-1])
         with jax.named_scope("z_sum_%d" % index):
             arrived = from_tensor(passed, 2)
         with jax.named_scope("core_kept_%d" % index):

time: 263 us -> 240 us (0.913)
  waiting for transfers between devices: 134 us -> 108 us
    ppermute x8 -> x7, waiting for transfers between devices: 92.6 us -> 21.5 us  [from_tensor(): return lax.ppermute(block, 'tensor', [(t, t ^ flip) for t in range(count)])]
    ppermute x15, waiting for transfers between devices: 41.3 us -> 80.4 us  [from_x(): lax.ppermute(block, 'ctx', [((c + step) % count, c) for c in range(count)])]
    ppermute x8 -> x7, starting transfers between devices: 27.9 us -> 19.9 us  [from_tensor(): return lax.ppermute(block, 'tensor', [(t, t ^ flip) for t in range(count)])]
    ppermute x2 -> x4, waiting for transfers between devices: 0.01 us -> 6.27 us  [from_z(): return lax.ppermute(block, ('section', 'tensor'), route)]
    ppermute x2 -> x4, starting transfers between devices: 5.12 us -> 10.4 us  [from_z(): return lax.ppermute(block, ('section', 'tensor'), route)]
    unnamed x1 -> x3, other arithmetic: 0.05 us -> 5.19 us
    unnamed x49 -> x44, local copies, waits for them, and re-layouts: 11.5 us -> 7.12 us
  transfers between devices with their start and end apart: 27 -> 28, of which waited for: 10 -> 10; matrix products, arithmetic and copies ran while one was open for 10% -> 13% of each run, Pallas kernels for 12% -> 11%
where the time goes in v2:
time: 240 us; the launch traced here: 238 us
  waiting for transfers between devices  108 us (45%)
  starting transfers between devices  56.8 us (24%)
  Pallas kernels  31.8 us (13%)
  local copies, waits for them, and re-layouts  24.3 us (10%)
  other arithmetic  16 us (7%)
    ppermute x15, waiting for transfers between devices, from_x(): lax.ppermute(block, 'ctx', [((c + step) % count, c) for c in range(count)])  80.4 us
    ppermute x7, waiting for transfers between devices, from_tensor(): return lax.ppermute(block, 'tensor', [(t, t ^ flip) for t in range(count)])  21.5 us
    ppermute x7, starting transfers between devices, from_tensor(): return lax.ppermute(block, 'tensor', [(t, t ^ flip) for t in range(count)])  19.9 us
    ppermute x15, starting transfers between devices, from_x(): lax.ppermute(block, 'ctx', [((c + step) % count, c) for c in range(count)])  18.1 us
    pallas_call x2, Pallas kernels, project(): pl.pallas_call(functools.partial(project_kernel, pieces=[(step, low) for...  11.8 us
    ppermute x4, starting transfers between devices, from_z(): return lax.ppermute(block, ('section', 'tensor'), route)  10.4 us
    pallas_call x1, Pallas kernels, attend(): pl.pallas_call(attend_kernel, grid=(batches, queries.shape[1] // wide), i...  9.32 us
    pallas_call x2, Pallas kernels, spread(): pl.pallas_call(spread_kernel, in_specs=[pl.BlockSpec(memory_space=pltpu.S...  8.58 us
  transfers between devices with their start and end apart: 28, of which 10 were waited for; matrix products, arithmetic and copies ran while one was open for 13% of the time, Pallas kernels for 11%

profile of v2, /device:TPU:49, one launch (start us, length us, event | category | flops | bytes accessed | tf_op | source)
XLA Modules:
  0.0 238.2 jit_solution(6580232305880026552)
XLA Ops:
  0.6 2.6 %collective-permute-start = (bf16[1024,1024]{1,0:T(8,128)(2,1)}, bf16[1024,1024]{1,0:T(8,128)(2,1)S(1)}, u32[]{:S(2)}, u32[]{:S(2)}) collective-permute-start(bf16[1024,1024]{1,0:T(8,128)(2,1)} %bitcast.29), channel_id=1, source_target_pairs={{4,0},{8,4},{12,8},{0,12},{5,1},{9,5},{13,9},{1,13},{6,2},{10,6},{... | collective-permute-start | bytes 6291464 | tf_op jit(solution)/shard_map/q_hop1/ppermute | solution.py:65
  4.3 2.8 %collective-permute-start.2 = (bf16[1024,256]{1,0:T(8,128)(2,1)S(1)}, bf16[1024,256]{1,0:T(8,128)(2,1)}, u32[]{:S(2)}, u32[]{:S(2)}) collective-permute-start(bf16[1024,256]{1,0:T(8,128)(2,1)S(1)} %pad_maximum_fusion.3.refs_0_), channel_id=1, source_target_pairs={{4,0},{8,4},{12,8},{0,12},{5,1},{9,5},{13,9},{1,13},{6,2},{10,6},{... | collective-permute-start | bytes 1572872 | tf_op jit(solution)/shard_map/kv_hop1/ppermute | solution.py:65
  9.3 5.1 %collective-permute-start.4 = (bf16[512,1024]{1,0:T(8,128)(2,1)}, bf16[512,1024]{1,0:T(8,128)(2,1)}, u32[]{:S(2)}, u32[]{:S(2)}) collective-permute-start(bf16[512,1024]{1,0:T(8,128)(2,1)} %pad_maximum_fusion), channel_id=1, source_target_pairs={{128,0},{129,1},{144,16},{145,17},{160,32},{161,33},{176,48},{177,... | collective-permute-start | bytes 3145736 | tf_op jit(solution)/shard_map/z_in/ppermute | solution.py:60
  14.4 44.5 %collective-permute-done.2.refs_1_ = bf16[1024,256]{1,0:T(8,128)(2,1)} collective-permute-done((bf16[1024,256]{1,0:T(8,128)(2,1)S(1)}, bf16[1024,256]{1,0:T(8,128)(2,1)}, u32[]{:S(2)}, u32[]{:S(2)}) %collective-permute-start.2) | collective-permute-done | bytes 524320 | tf_op jit(solution)/shard_map/kv_hop1/ppermute | solution.py:65
  62.5 10.7 %collective-permute-done.3.refs_3_ = bf16[1024,256]{1,0:T(8,128)(2,1)} collective-permute-done((bf16[1024,256]{1,0:T(8,128)(2,1)S(1)}, bf16[1024,256]{1,0:T(8,128)(2,1)}, u32[]{:S(2)}, u32[]{:S(2)}) %collective-permute-start.3) | collective-permute-done | bytes 524320 | tf_op jit(solution)/shard_map/kv_hop1/ppermute | solution.py:65
  80.6 5.2 %collective-permute-start.6 = (bf16[128,1024]{1,0:T(8,128)(2,1)S(1)}, bf16[128,1024]{1,0:T(8,128)(2,1)S(1)}, u32[]{:S(2)}, u32[]{:S(2)}) collective-permute-start(bf16[128,1024]{1,0:T(8,128)(2,1)S(1)} %slice.72), channel_id=1, source_target_pairs={{128,0},{129,1},{144,16},{145,17},{160,32},{161,33},{176,48},{177,... | collective-permute-start | bytes 786440 | tf_op jit(solution)/shard_map/far/ppermute | solution.py:60
  91.6 2.9 %constant_dynamic-update-slice_fusion.2 = (bf16[1024,1024]{1,0:T(8,128)(2,1)}, bf16[256,1024]{1,0:T(8,128)(2,1)}, bf16[1,256,1024]{2,1,0:T(8,128)(2,1)}) fusion(bf16[1024,1024]{1,0:T(8,128)(2,1)} %get-tuple-element.47, bf16[512,1024]{1,0:T(8,128)(2,1)} %collective-permute-done.4, bf16[512,1024]{1,0:T(8,128)(2,1)} %collective-permute-done.5, pred[]{:T(512)S(6)} %lt.28), kind=kLoop, calls=%fused_computation.30 | loop fusion | flops 524288 | bytes 3670017
  95.2 6.3 %collective-permute-done.7 = bf16[128,1024]{1,0:T(8,128)(2,1)S(1)} collective-permute-done((bf16[128,1024]{1,0:T(8,128)(2,1)S(1)}, bf16[128,1024]{1,0:T(8,128)(2,1)S(1)}, u32[]{:S(2)}, u32[]{:S(2)}) %collective-permute-start.7) | collective-permute-done | bytes 262176 | tf_op jit(solution)/shard_map/far/ppermute | solution.py:60
  103.9 4.5 %collective-permute-done.9.refs_2_.refs_3_ = bf16[1024,256]{1,0:T(8,128)(2,1)} collective-permute-done((bf16[1024,256]{1,0:T(8,128)(2,1)}, bf16[1024,256]{1,0:T(8,128)(2,1)}, u32[]{:S(2)}, u32[]{:S(2)}) %collective-permute-start.9) | collective-permute-done | bytes 524320 | tf_op jit(solution)/shard_map/kv_hop2/ppermute | solution.py:65
  114.7 4.1 %project_kv.1 = bf16[512,256]{1,0:T(8,128)(2,1)S(1)} custom-call(s32[4]{0:T(128)S(1)} %fusion.7.index_ref, bf16[4,512,1024]{2,1,0:T(8,128)(2,1)S(1)} %bitcast.23, bf16[1024,256]{1,0:T(8,128)(2,1)S(1)} %copy-done.10, bf16[1024,256]{1,0:T(8,128)(2,1)} %collective-permute-done.2.refs_1_, bf16[1024,256]{1,0:T(8,128)(2,1)} %collective-permute-done.9.refs_2_.refs_3_, ...), custom_call_target="tpu_custom_call" | custom-call | flops 1024 | bytes 1024 | tf_op jit(solution)/shard_map/project_kv/pallas_call | solution.py:151
  122.9 6.4 %collective-permute-start.12 = (bf16[2,272,256]{2,0,1:T(2,128)(2,1)}, bf16[2,272,256]{2,0,1:T(2,128)(2,1)}, u32[]{:S(2)}, u32[]{:S(2)}) collective-permute-start(bf16[2,272,256]{2,0,1:T(2,128)(2,1)} %pad_maximum_fusion.6), channel_id=1, source_target_pairs={{0,8},{4,12},{1,9},{5,13},{2,10},{6,14},{3,11},{7,15},{16,24},{20,... | collective-permute-start | bytes 835592 | tf_op jit(solution)/shard_map/kv_rows/ppermute | solution.py:70
  137.0 7.7 %project_q.1.query_ref = bf16[512,1024]{1,0:T(8,128)(2,1)S(1)} custom-call(s32[4]{0:T(128)S(1)} %fusion.7.index_ref, bf16[4,512,1024]{2,1,0:T(8,128)(2,1)S(1)} %bitcast.24, bf16[1024,1024]{1,0:T(8,128)(2,1)S(1)} %bitcast.31, bf16[1024,1024]{1,0:T(8,128)(2,1)S(1)} %copy-done.5, bf16[1024,1024]{1,0:T(8,128)(2,1)} %collective-permute-done.1.refs_2_, ...), custom_call_target="tpu_custom_call" | custom-call | flops 1024 | bytes 1024 | tf_op jit(solution)/shard_map/project_q/pallas_call | solution.py:151
  153.8 9.3 %attend.1.mixed_ref = bf16[512,1024]{1,0:T(8,128)(2,1)S(1)} custom-call(bf16[512,1024]{1,0:T(8,128)(2,1)S(1)} %project_q.1.query_ref, bf16[2,768,256]{2,1,0:T(8,128)(2,1)S(1)} %copy.18.key_ref.value_ref, bf16[2,768,256]{2,1,0:T(8,128)(2,1)S(1)} %copy.18.key_ref.value_ref, s32[2,256,1]{2,1,0:T(8,128)S(1)} %copy-done.13, ...), custom_call_target="tpu_custom_call" | custom-call | flops 1024 | bytes 1024 | tf_op jit(solution)/shard_map/attend/pallas_call | solution.py:196
  163.1 5.5 %spread_0.1 = (bf16[512,640]{1,0:T(8,128)(2,1)S(1)}, bf16[512,640]{1,0:T(8,128)(2,1)S(1)}, f32[512,640]{1,0:T(8,128)S(1)}, f32[512,640]{1,0:T(8,128)S(1)}) custom-call(s32[4]{0:T(128)S(1)} %and_select_fusion.1.index_ref, bf16[512,1024]{1,0:T(8,128)(2,1)S(1)} %attend.1.mixed_ref, bf16[1024,640]{1,0:T(8,128)(2,1)S(1)} %copy-done.3, ...), custom_call_target="tpu_custom_call" | custom-call | flops 1024 | bytes 1024 | tf_op jit(solution)/shard_map/spread_0/pallas_call | solution.py:234
  168.7 5.2 %collective-permute-start.19 = (bf16[512,640]{1,0:T(8,128)(2,1)S(1)}, bf16[512,640]{1,0:T(8,128)(2,1)S(1)}, u32[]{:S(2)}, u32[]{:S(2)}) collective-permute-start(bf16[512,640]{1,0:T(8,128)(2,1)S(1)} %get-tuple-element.36), channel_id=1, source_target_pairs={{0,1},{1,0},{2,3},{3,2},{4,5},{5,4},{6,7},{7,6},{8,9},{9,8},{10,11... | collective-permute-start | bytes 1966088 | tf_op jit(solution)/shard_map/core_passed_0/ppermute | solution.py:75
  176.3 6.1 %collective-permute-start.20 = (bf16[512,640]{1,0:T(8,128)(2,1)S(1)}, bf16[512,640]{1,0:T(8,128)(2,1)S(1)}, u32[]{:S(2)}, u32[]{:S(2)}) collective-permute-start(bf16[512,640]{1,0:T(8,128)(2,1)S(1)} %add_convert_fusion.1), channel_id=1, source_target_pairs={{0,2},{1,3},{2,0},{3,1},{4,6},{5,7},{6,4},{7,5},{8,10},{9,11},{10,... | collective-permute-start | bytes 1966088 | tf_op jit(solution)/shard_map/z_sum_0/ppermute | solution.py:75
  182.4 10.2 %collective-permute-done.21.ahead_ref = bf16[1024,384]{1,0:T(8,128)(2,1)S(1)} collective-permute-done((bf16[1024,384]{1,0:T(8,128)(2,1)S(1)}, bf16[1024,384]{1,0:T(8,128)(2,1)S(1)}, u32[]{:S(2)}, u32[]{:S(2)}) %collective-permute-start.21) | collective-permute-done | bytes 786464 | tf_op jit(solution)/shard_map/out_hop1_1/ppermute | solution.py:65
  192.7 2.5 %collective-permute-start.22 = (bf16[512,384]{1,0:T(8,128)(2,1)S(1)}, bf16[512,384]{1,0:T(8,128)(2,1)S(1)}, u32[]{:S(2)}, u32[]{:S(2)}) collective-permute-start(bf16[512,384]{1,0:T(8,128)(2,1)S(1)} %slice.102), channel_id=1, source_target_pairs={{4,0},{8,4},{12,8},{0,12},{5,1},{9,5},{13,9},{1,13},{6,2},{10,6},{... | collective-permute-start | bytes 1179656 | tf_op jit(solution)/shard_map/out_hop2_1/ppermute | solution.py:65
  195.3 7.1 %collective-permute-done.22.near_ref = bf16[512,384]{1,0:T(8,128)(2,1)S(1)} collective-permute-done((bf16[512,384]{1,0:T(8,128)(2,1)S(1)}, bf16[512,384]{1,0:T(8,128)(2,1)S(1)}, u32[]{:S(2)}, u32[]{:S(2)}) %collective-permute-start.22) | collective-permute-done | bytes 393248 | tf_op jit(solution)/shard_map/out_hop2_1/ppermute | solution.py:65
  202.5 3.3 %collective-permute-done.24.back_ref = bf16[512,384]{1,0:T(8,128)(2,1)S(1)} collective-permute-done((bf16[512,384]{1,0:T(8,128)(2,1)S(1)}, bf16[512,384]{1,0:T(8,128)(2,1)S(1)}, u32[]{:S(2)}, u32[]{:S(2)}) %collective-permute-start.24) | collective-permute-done | bytes 393248 | tf_op jit(solution)/shard_map/out_hop2_1/ppermute | solution.py:65
  205.7 3.1 %spread_1.1 = (bf16[512,384]{1,0:T(8,128)(2,1)S(1)}, bf16[512,384]{1,0:T(8,128)(2,1)S(1)}, f32[512,384]{1,0:T(8,128)S(1)}, f32[512,384]{1,0:T(8,128)S(1)}) custom-call(s32[4]{0:T(128)S(1)} %and_select_fusion.1.index_ref, bf16[512,1024]{1,0:T(8,128)(2,1)S(1)} %attend.1.mixed_ref, bf16[1024,384]{1,0:T(8,128)(2,1)S(1)} %copy-done.6, ...), custom_call_target="tpu_custom_call" | custom-call | flops 1024 | bytes 1024 | tf_op jit(solution)/shard_map/spread_1/pallas_call | solution.py:234
  208.8 2.7 %collective-permute-done.20 = bf16[512,640]{1,0:T(8,128)(2,1)S(1)} collective-permute-done((bf16[512,640]{1,0:T(8,128)(2,1)S(1)}, bf16[512,640]{1,0:T(8,128)(2,1)S(1)}, u32[]{:S(2)}, u32[]{:S(2)}) %collective-permute-start.20) | collective-permute-done | bytes 655392 | tf_op jit(solution)/shard_map/z_sum_0/ppermute | solution.py:75
  214.2 5.3 %collective-permute-start.27 = (bf16[512,384]{1,0:T(8,128)(2,1)S(1)}, bf16[512,384]{1,0:T(8,128)(2,1)S(1)}, u32[]{:S(2)}, u32[]{:S(2)}) collective-permute-start(bf16[512,384]{1,0:T(8,128)(2,1)S(1)} %add_convert_fusion.3), channel_id=1, source_target_pairs={{0,2},{1,3},{2,0},{3,1},{4,6},{5,7},{6,4},{7,5},{8,10},{9,11},{10,... | collective-permute-start | bytes 1179656 | tf_op jit(solution)/shard_map/z_sum_1/ppermute | solution.py:75
  219.4 17.5 %collective-permute-done.27 = bf16[512,384]{1,0:T(8,128)(2,1)S(1)} collective-permute-done((bf16[512,384]{1,0:T(8,128)(2,1)S(1)}, bf16[512,384]{1,0:T(8,128)(2,1)S(1)}, u32[]{:S(2)}, u32[]{:S(2)}) %collective-permute-start.27) | collective-permute-done | bytes 393248 | tf_op jit(solution)/shard_map/z_sum_1/ppermute | solution.py:75
  (130 shorter events, 56.5 us)
Async XLA Ops:
  0.6 72.6 %collective-permute-start = (bf16[1024,1024]{1,0:T(8,128)(2,1)}, bf16[1024,1024]{1,0:T(8,128)(2,1)S(1)}, u32[]{:S(2)}, u32[]{:S(2)}) collective-permute-start(bf16[1024,1024]{1,0:T(8,128)(2,1)} %bitcast.29), channel_id=1, source_target_pairs={{4,0},{8,4},{12,8},{0,12},{5,1},{9,5},{13,9},{1,13},{6,2},{10,6},{... | collective-permute-start | bytes 6291464 | tf_op jit(solution)/shard_map/q_hop1/ppermute | solution.py:65
  3.2 70.1 %collective-permute-start.1 = (bf16[1024,1024]{1,0:T(8,128)(2,1)}, bf16[1024,1024]{1,0:T(8,128)(2,1)}, u32[]{:S(2)}, u32[]{:S(2)}) collective-permute-start(bf16[1024,1024]{1,0:T(8,128)(2,1)} %bitcast.30), channel_id=1, source_target_pairs={{12,0},{0,4},{4,8},{8,12},{13,1},{1,5},{5,9},{9,13},{14,2},{2,6},{... | collective-permute-start | bytes 6291464 | tf_op jit(solution)/shard_map/q_hop1/ppermute | solution.py:65
  4.3 54.6 %collective-permute-start.2 = (bf16[1024,256]{1,0:T(8,128)(2,1)S(1)}, bf16[1024,256]{1,0:T(8,128)(2,1)}, u32[]{:S(2)}, u32[]{:S(2)}) collective-permute-start(bf16[1024,256]{1,0:T(8,128)(2,1)S(1)} %pad_maximum_fusion.3.refs_0_), channel_id=1, source_target_pairs={{4,0},{8,4},{12,8},{0,12},{5,1},{9,5},{13,9},{1,13},{6,2},{10,6},{... | collective-permute-start | bytes 1572872 | tf_op jit(solution)/shard_map/kv_hop1/ppermute | solution.py:65
  9.3 64.0 %collective-permute-start.4 = (bf16[512,1024]{1,0:T(8,128)(2,1)}, bf16[512,1024]{1,0:T(8,128)(2,1)}, u32[]{:S(2)}, u32[]{:S(2)}) collective-permute-start(bf16[512,1024]{1,0:T(8,128)(2,1)} %pad_maximum_fusion), channel_id=1, source_target_pairs={{128,0},{129,1},{144,16},{145,17},{160,32},{161,33},{176,48},{177,... | collective-permute-start | bytes 3145736 | tf_op jit(solution)/shard_map/z_in/ppermute | solution.py:60
  14.4 58.8 %collective-permute-start.5 = (bf16[512,1024]{1,0:T(8,128)(2,1)}, bf16[512,1024]{1,0:T(8,128)(2,1)}, u32[]{:S(2)}, u32[]{:S(2)}) collective-permute-start(bf16[512,1024]{1,0:T(8,128)(2,1)} %pad_maximum_fusion), channel_id=1, source_target_pairs={{130,0},{131,1},{146,16},{147,17},{162,32},{163,33},{178,48},{179,... | collective-permute-start | bytes 3145736 | tf_op jit(solution)/shard_map/z_in/ppermute | solution.py:60
  58.9 14.3 %collective-permute-start.3 = (bf16[1024,256]{1,0:T(8,128)(2,1)S(1)}, bf16[1024,256]{1,0:T(8,128)(2,1)}, u32[]{:S(2)}, u32[]{:S(2)}) collective-permute-start(bf16[1024,256]{1,0:T(8,128)(2,1)S(1)} %pad_maximum_fusion.3.refs_0_), channel_id=1, source_target_pairs={{12,0},{0,4},{4,8},{8,12},{13,1},{1,5},{5,9},{9,13},{14,2},{2,6},{... | collective-permute-start | bytes 1572872 | tf_op jit(solution)/shard_map/kv_hop1/ppermute | solution.py:65
  74.4 34.0 %collective-permute-start.10 = (bf16[512,1024]{1,0:T(8,128)(2,1)}, bf16[512,1024]{1,0:T(8,128)(2,1)}, u32[]{:S(2)}, u32[]{:S(2)}) collective-permute-start(bf16[512,1024]{1,0:T(8,128)(2,1)} %slice.74), channel_id=1, source_target_pairs={{4,0},{8,4},{12,8},{0,12},{5,1},{9,5},{13,9},{1,13},{6,2},{10,6},{... | collective-permute-start | bytes 3145736 | tf_op jit(solution)/shard_map/q_hop2/ppermute | solution.py:65
  77.9 30.6 %collective-permute-start.11 = (bf16[512,1024]{1,0:T(8,128)(2,1)}, bf16[512,1024]{1,0:T(8,128)(2,1)}, u32[]{:S(2)}, u32[]{:S(2)}) collective-permute-start(bf16[512,1024]{1,0:T(8,128)(2,1)} %slice.75), channel_id=1, source_target_pairs={{12,0},{0,4},{4,8},{8,12},{13,1},{1,5},{5,9},{9,13},{14,2},{2,6},{... | collective-permute-start | bytes 3145736 | tf_op jit(solution)/shard_map/q_hop2/ppermute | solution.py:65
  80.6 13.9 %collective-permute-start.6 = (bf16[128,1024]{1,0:T(8,128)(2,1)S(1)}, bf16[128,1024]{1,0:T(8,128)(2,1)S(1)}, u32[]{:S(2)}, u32[]{:S(2)}) collective-permute-start(bf16[128,1024]{1,0:T(8,128)(2,1)S(1)} %slice.72), channel_id=1, source_target_pairs={{128,0},{129,1},{144,16},{145,17},{160,32},{161,33},{176,48},{177,... | collective-permute-start | bytes 786440 | tf_op jit(solution)/shard_map/far/ppermute | solution.py:60
  86.8 14.7 %collective-permute-start.7 = (bf16[128,1024]{1,0:T(8,128)(2,1)S(1)}, bf16[128,1024]{1,0:T(8,128)(2,1)S(1)}, u32[]{:S(2)}, u32[]{:S(2)}) collective-permute-start(bf16[128,1024]{1,0:T(8,128)(2,1)S(1)} %slice.73), channel_id=1, source_target_pairs={{130,0},{131,1},{146,16},{147,17},{162,32},{163,33},{178,48},{179,... | collective-permute-start | bytes 786440 | tf_op jit(solution)/shard_map/far/ppermute | solution.py:60
  86.9 21.5 %collective-permute-start.9 = (bf16[1024,256]{1,0:T(8,128)(2,1)}, bf16[1024,256]{1,0:T(8,128)(2,1)}, u32[]{:S(2)}, u32[]{:S(2)}) collective-permute-start(bf16[1024,256]{1,0:T(8,128)(2,1)} %collective-permute-done.2.refs_1_), channel_id=1, source_target_pairs={{4,0},{8,4},{12,8},{0,12},{5,1},{9,5},{13,9},{1,13},{6,2},{10,6},{... | collective-permute-start | bytes 1572872 | tf_op jit(solution)/shard_map/kv_hop2/ppermute | solution.py:65
  102.3 10.3 %collective-permute-start.8 = (bf16[1024,1024]{1,0:T(8,128)(2,1)}, bf16[1024,1024]{1,0:T(8,128)(2,1)S(1)}, u32[]{:S(2)}, u32[]{:S(2)}) collective-permute-start(bf16[1024,1024]{1,0:T(8,128)(2,1)} %constant_dynamic-update-slice_fusion), channel_id=1, source_target_pairs={{0,1},{1,0},{2,3},{3,2},{4,5},{5,4},{6,7},{7,6},{8,9},{9,8},{10,11... | collective-permute-start | bytes 6291464 | tf_op jit(solution)/shard_map/sib/ppermute | solution.py:75
  108.4 36.3 %collective-permute-start.14 = (bf16[1024,640]{1,0:T(8,128)(2,1)}, bf16[1024,640]{1,0:T(8,128)(2,1)}, u32[]{:S(2)}, u32[]{:S(2)}) collective-permute-start(bf16[1024,640]{1,0:T(8,128)(2,1)} %hold.1.own_ref), channel_id=1, source_target_pairs={{4,0},{8,4},{12,8},{0,12},{5,1},{9,5},{13,9},{1,13},{6,2},{10,6},{... | collective-permute-start | bytes 3932168 | tf_op jit(solution)/shard_map/out_hop1_0/ppermute | solution.py:65
  110.6 35.4 %collective-permute-start.16 = (bf16[1024,640]{1,0:T(8,128)(2,1)}, bf16[1024,640]{1,0:T(8,128)(2,1)}, u32[]{:S(2)}, u32[]{:S(2)}) collective-permute-start(bf16[1024,640]{1,0:T(8,128)(2,1)} %hold.1.own_ref), channel_id=1, source_target_pairs={{12,0},{0,4},{4,8},{8,12},{13,1},{1,5},{5,9},{9,13},{14,2},{2,6},{... | collective-permute-start | bytes 3932168 | tf_op jit(solution)/shard_map/out_hop1_0/ppermute | solution.py:65
  121.0 27.8 %collective-permute-start.13 = (bf16[2,272,256]{2,0,1:T(2,128)(2,1)}, bf16[2,272,256]{2,0,1:T(2,128)(2,1)}, u32[]{:S(2)}, u32[]{:S(2)}) collective-permute-start(bf16[2,272,256]{2,0,1:T(2,128)(2,1)} %pad_maximum_fusion.6), channel_id=1, source_target_pairs={{0,4},{4,8},{8,12},{1,5},{5,9},{9,13},{2,6},{6,10},{10,14},{3,7},{... | collective-permute-start | bytes 835592 | tf_op jit(solution)/shard_map/kv_rows/ppermute | solution.py:70
  122.9 26.9 %collective-permute-start.12 = (bf16[2,272,256]{2,0,1:T(2,128)(2,1)}, bf16[2,272,256]{2,0,1:T(2,128)(2,1)}, u32[]{:S(2)}, u32[]{:S(2)}) collective-permute-start(bf16[2,272,256]{2,0,1:T(2,128)(2,1)} %pad_maximum_fusion.6), channel_id=1, source_target_pairs={{0,8},{4,12},{1,9},{5,13},{2,10},{6,14},{3,11},{7,15},{16,24},{20,... | collective-permute-start | bytes 835592 | tf_op jit(solution)/shard_map/kv_rows/ppermute | solution.py:70
  145.9 17.2 %collective-permute-start.15 = (bf16[512,640]{1,0:T(8,128)(2,1)S(1)}, bf16[512,640]{1,0:T(8,128)(2,1)S(1)}, u32[]{:S(2)}, u32[]{:S(2)}) collective-permute-start(bf16[512,640]{1,0:T(8,128)(2,1)S(1)} %slice.100), channel_id=1, source_target_pairs={{4,0},{8,4},{12,8},{0,12},{5,1},{9,5},{13,9},{1,13},{6,2},{10,6},{... | collective-permute-start | bytes 1966088 | tf_op jit(solution)/shard_map/out_hop2_0/ppermute | solution.py:65
  147.2 15.9 %collective-permute-start.17 = (bf16[512,640]{1,0:T(8,128)(2,1)S(1)}, bf16[512,640]{1,0:T(8,128)(2,1)S(1)}, u32[]{:S(2)}, u32[]{:S(2)}) collective-permute-start(bf16[512,640]{1,0:T(8,128)(2,1)S(1)} %slice.101), channel_id=1, source_target_pairs={{12,0},{0,4},{4,8},{8,12},{13,1},{1,5},{5,9},{9,13},{14,2},{2,6},{... | collective-permute-start | bytes 1966088 | tf_op jit(solution)/shard_map/out_hop2_0/ppermute | solution.py:65
  173.8 18.8 %collective-permute-start.21 = (bf16[1024,384]{1,0:T(8,128)(2,1)S(1)}, bf16[1024,384]{1,0:T(8,128)(2,1)S(1)}, u32[]{:S(2)}, u32[]{:S(2)}) collective-permute-start(bf16[1024,384]{1,0:T(8,128)(2,1)S(1)} %copy-done.6), channel_id=1, source_target_pairs={{4,0},{8,4},{12,8},{0,12},{5,1},{9,5},{13,9},{1,13},{6,2},{10,6},{... | collective-permute-start | bytes 2359304 | tf_op jit(solution)/shard_map/out_hop1_1/ppermute | solution.py:65
  175.1 20.1 %collective-permute-start.23 = (bf16[1024,384]{1,0:T(8,128)(2,1)S(1)}, bf16[1024,384]{1,0:T(8,128)(2,1)S(1)}, u32[]{:S(2)}, u32[]{:S(2)}) collective-permute-start(bf16[1024,384]{1,0:T(8,128)(2,1)S(1)} %copy-done.6), channel_id=1, source_target_pairs={{12,0},{0,4},{4,8},{8,12},{13,1},{1,5},{5,9},{9,13},{14,2},{2,6},{... | collective-permute-start | bytes 2359304 | tf_op jit(solution)/shard_map/out_hop1_1/ppermute | solution.py:65
  175.3 33.5 %collective-permute-start.18 = (bf16[512,640]{1,0:T(8,128)(2,1)S(1)}, bf16[512,640]{1,0:T(8,128)(2,1)S(1)}, u32[]{:S(2)}, u32[]{:S(2)}) collective-permute-start(bf16[512,640]{1,0:T(8,128)(2,1)S(1)} %get-tuple-element.34), channel_id=1, source_target_pairs={{0,1},{1,0},{2,3},{3,2},{4,5},{5,4},{6,7},{7,6},{8,9},{9,8},{10,11... | collective-permute-start | bytes 1966088 | tf_op jit(solution)/shard_map/core_kept_0/ppermute | solution.py:75
  176.3 35.3 %collective-permute-start.20 = (bf16[512,640]{1,0:T(8,128)(2,1)S(1)}, bf16[512,640]{1,0:T(8,128)(2,1)S(1)}, u32[]{:S(2)}, u32[]{:S(2)}) collective-permute-start(bf16[512,640]{1,0:T(8,128)(2,1)S(1)} %add_convert_fusion.1), channel_id=1, source_target_pairs={{0,2},{1,3},{2,0},{3,1},{4,6},{5,7},{6,4},{7,5},{8,10},{9,11},{10,... | collective-permute-start | bytes 1966088 | tf_op jit(solution)/shard_map/z_sum_0/ppermute | solution.py:75
  195.3 10.5 %collective-permute-start.24 = (bf16[512,384]{1,0:T(8,128)(2,1)S(1)}, bf16[512,384]{1,0:T(8,128)(2,1)S(1)}, u32[]{:S(2)}, u32[]{:S(2)}) collective-permute-start(bf16[512,384]{1,0:T(8,128)(2,1)S(1)} %slice.103), channel_id=1, source_target_pairs={{12,0},{0,4},{4,8},{8,12},{13,1},{1,5},{5,9},{9,13},{14,2},{2,6},{... | collective-permute-start | bytes 1179656 | tf_op jit(solution)/shard_map/out_hop2_1/ppermute | solution.py:65
  214.2 22.7 %collective-permute-start.27 = (bf16[512,384]{1,0:T(8,128)(2,1)S(1)}, bf16[512,384]{1,0:T(8,128)(2,1)S(1)}, u32[]{:S(2)}, u32[]{:S(2)}) collective-permute-start(bf16[512,384]{1,0:T(8,128)(2,1)S(1)} %add_convert_fusion.3), channel_id=1, source_target_pairs={{0,2},{1,3},{2,0},{3,1},{4,6},{5,7},{6,4},{7,5},{8,10},{9,11},{10,... | collective-permute-start | bytes 1179656 | tf_op jit(solution)/shard_map/z_sum_1/ppermute | solution.py:75
  (25 other events, 212.8 us)

commit v3 on v2

--- a/solution.py
+++ b/solution.py
@@ -14,7 +14,8 @@
 BF = jnp.bfloat16
 F32 = jnp.float32
 STRIPS = (5, 3)
-HOLD_FLOPS = 4 * 10**10
+SHORT = 10**10
+LONG = 4 * 10**10
 
 
 def after(value, *earlier):
@@ -25,7 +26,7 @@
     del refs
 
 
-def hold(value, *earlier):
+def hold(value, *earlier, flops):
     anywhere = pl.BlockSpec(memory_space=pl.ANY)
     return pl.pallas_call(
         hold_kernel,
@@ -33,7 +34,7 @@
         out_specs=anywhere,
         out_shape=jax.ShapeDtypeStruct(value.shape, value.dtype),
         input_output_aliases={0: 0},
-        cost_estimate=pl.CostEstimate(flops=HOLD_FLOPS, transcendentals=0, bytes_accessed=1024),
+        cost_estimate=pl.CostEstimate(flops=flops, transcendentals=0, bytes_accessed=1024),
         name="hold",
     )(value, *earlier)
 
@@ -283,10 +284,11 @@
         q_ahead, q_behind = first_hop(q_weight)
     kv_weight = jnp.concatenate((key_weight[0], value_projection_weight[0]), axis=1)
     with jax.named_scope("kv_hop1"):
-        kv_ahead, kv_behind = first_hop(kv_weight)
+        kv_ahead, kv_behind = first_hop(after(kv_weight, q_ahead, q_behind))
     both = jnp.concatenate((mine, held), axis=0)
     with jax.named_scope("z_in"):
         up, down = from_z(both, 2), from_z(both, -2)
+        up = hold(up, down, flops=SHORT)
     q_ahead, q_behind, kv_ahead, kv_behind, up, down, out_own[0] = lax.optimization_barrier(
         (q_ahead, q_behind, kv_ahead, kv_behind, up, down, out_own[0])
     )
@@ -294,7 +296,7 @@
     with jax.named_scope("q_hop2"):
         across_low, across_high = second_hop(q_ahead, q_behind)
     with jax.named_scope("kv_hop2"):
-        kv_across = from_x(kv_ahead, 1)
+        kv_near, kv_back = second_hop(kv_ahead, kv_behind)
     with jax.named_scope("far"):
         mine_far = jnp.concatenate((from_z(up[:half], 2), from_z(down[half:rows], -2)), axis=0)
     stashed = jnp.where(near_high, up[:rows], down[:rows])
@@ -315,7 +317,7 @@
     own_kv = project(
         feature_order,
         normed,
-        ((kv_weight, 0, 0), (kv_ahead, 1, 0), (kv_across, 2, 0), (kv_behind, 3, 0)),
+        ((kv_weight, 0, 0), (kv_ahead, 1, 0), (kv_near, 2, 0), (kv_back, 2, depth), (kv_behind, 3, 0)),
         cosine,
         sine,
         1,
@@ -327,7 +329,7 @@
     with jax.named_scope("kv_rows"):
         kv_one, kv_two = from_before(own_pair, 1), from_before(own_pair, 2)
     with jax.named_scope("out_hop1_0"):
-        out_own[0] = hold(out_own[0], across_low, across_high, kv_across)
+        out_own[0] = hold(out_own[0], across_low, across_high, kv_near, kv_back, flops=LONG)
         out_hops = [first_hop(out_own[0])]
     all_kv = jnp.concatenate((kv_two[:, id_rows:], kv_one[:, id_rows:], own_pair[:, id_rows:]), axis=1)
     docs_one = jnp.where(c >= 1, kv_one[:, 0].astype(jnp.int32), -1)

time: 240 us -> 229 us (0.954)
  waiting for transfers between devices: 108 us -> 99.5 us
  starting transfers between devices: 56.8 us -> 53.1 us
    ppermute x15 -> x16, waiting for transfers between devices: 80.4 us -> 67 us  [from_x(): lax.ppermute(block, 'ctx', [((c + step) % count, c) for c in range(count)])]
    ppermute x4, waiting for transfers between devices: 6.27 us -> 12.1 us  [from_z(): return lax.ppermute(block, ('section', 'tensor'), route)]
    ppermute x15 -> x16, starting transfers between devices: 18.1 us -> 13.7 us  [from_x(): lax.ppermute(block, 'ctx', [((c + step) % count, c) for c in range(count)])]
    slice x6 -> x8, local copies, waits for them, and re-layouts: 5.81 us -> 7.66 us  [second_hop(): return (from_x(ahead[:half], 1), from_x(behind[half:], -1))]
    unnamed x44 -> x52, local copies, waits for them, and re-layouts: 7.12 us -> 7.04 us
  transfers between devices with their start and end apart: 28 -> 29, of which waited for: 10 -> 17; matrix products, arithmetic and copies ran while one was open for 13% -> 15% of each run, Pallas kernels for 11% -> 12%
where the time goes in v3:
time: 229 us; the launch traced here: 226 us
  waiting for transfers between devices  99.5 us (43%)
  starting transfers between devices  53.1 us (23%)
  Pallas kernels  31.6 us (14%)
  local copies, waits for them, and re-layouts  26.1 us (11%)
  other arithmetic  15 us (7%)
    ppermute x16, waiting for transfers between devices, from_x(): lax.ppermute(block, 'ctx', [((c + step) % count, c) for c in range(count)])  67 us
    ppermute x7, starting transfers between devices, from_tensor(): return lax.ppermute(block, 'tensor', [(t, t ^ flip) for t in range(count)])  21.8 us
    ppermute x7, waiting for transfers between devices, from_tensor(): return lax.ppermute(block, 'tensor', [(t, t ^ flip) for t in range(count)])  20.3 us
    ppermute x16, starting transfers between devices, from_x(): lax.ppermute(block, 'ctx', [((c + step) % count, c) for c in range(count)])  13.7 us
    ppermute x4, waiting for transfers between devices, from_z(): return lax.ppermute(block, ('section', 'tensor'), route)  12.1 us
    pallas_call x2, Pallas kernels, project(): pl.pallas_call(functools.partial(project_kernel, pieces=[(step, low) for...  11.7 us
    ppermute x4, starting transfers between devices, from_z(): return lax.ppermute(block, ('section', 'tensor'), route)  10.4 us
    pallas_call x1, Pallas kernels, attend(): pl.pallas_call(attend_kernel, grid=(batches, queries.shape[1] // wide), i...  9.32 us
  transfers between devices with their start and end apart: 29, of which 17 were waited for; matrix products, arithmetic and copies ran while one was open for 15% of the time, Pallas kernels for 12%

profile of v3, /device:TPU:49, one launch (start us, length us, event | category | flops | bytes accessed | tf_op | source)
XLA Modules:
  0.0 226.4 jit_solution(1573433129371360283)
XLA Ops:
  0.6 2.6 %collective-permute-start = (bf16[1024,1024]{1,0:T(8,128)(2,1)}, bf16[1024,1024]{1,0:T(8,128)(2,1)S(1)}, u32[]{:S(2)}, u32[]{:S(2)}) collective-permute-start(bf16[1024,1024]{1,0:T(8,128)(2,1)} %bitcast.29), channel_id=1, source_target_pairs={{4,0},{8,4},{12,8},{0,12},{5,1},{9,5},{13,9},{1,13},{6,2},{10,6},{... | collective-permute-start | bytes 6291464 | tf_op jit(solution)/shard_map/q_hop1/ppermute | solution.py:66
  5.5 5.1 %collective-permute-start.4 = (bf16[512,1024]{1,0:T(8,128)(2,1)}, bf16[512,1024]{1,0:T(8,128)(2,1)}, u32[]{:S(2)}, u32[]{:S(2)}) collective-permute-start(bf16[512,1024]{1,0:T(8,128)(2,1)} %pad_maximum_fusion), channel_id=1, source_target_pairs={{128,0},{129,1},{144,16},{145,17},{160,32},{161,33},{176,48},{177,... | collective-permute-start | bytes 3145736 | tf_op jit(solution)/shard_map/z_in/ppermute | solution.py:61
  10.6 2.5 %slice.100.refs_0_ = bf16[1024,640]{1,0:T(8,128)(2,1)} slice(bf16[1024,1024]{1,0:T(8,128)(2,1)} %bitcast.33), slice={[0:1024], [0:640]} | slice | bytes 2621440 | tf_op jit(solution)/shard_map/slice | solution.py:279
  13.2 34.6 %collective-permute-done.refs_1_ = bf16[1024,1024]{1,0:T(8,128)(2,1)S(1)} collective-permute-done((bf16[1024,1024]{1,0:T(8,128)(2,1)}, bf16[1024,1024]{1,0:T(8,128)(2,1)S(1)}, u32[]{:S(2)}, u32[]{:S(2)}) %collective-permute-start) | collective-permute-done | bytes 2097184 | tf_op jit(solution)/shard_map/q_hop1/ppermute | solution.py:66
  47.8 3.1 %collective-permute-done.1.refs_2_ = bf16[1024,1024]{1,0:T(8,128)(2,1)} collective-permute-done((bf16[1024,1024]{1,0:T(8,128)(2,1)}, bf16[1024,1024]{1,0:T(8,128)(2,1)}, u32[]{:S(2)}, u32[]{:S(2)}) %collective-permute-start.1) | collective-permute-done | bytes 2097184 | tf_op jit(solution)/shard_map/q_hop1/ppermute | solution.py:66
  54.4 5.5 %collective-permute-done.5.refs_1_ = bf16[512,1024]{1,0:T(8,128)(2,1)} collective-permute-done((bf16[512,1024]{1,0:T(8,128)(2,1)}, bf16[512,1024]{1,0:T(8,128)(2,1)}, u32[]{:S(2)}, u32[]{:S(2)}) %collective-permute-start.5) | collective-permute-done | bytes 1048608 | tf_op jit(solution)/shard_map/z_in/ppermute | solution.py:61
  59.9 2.6 %collective-permute-done.2.refs_1_ = bf16[1024,256]{1,0:T(8,128)(2,1)} collective-permute-done((bf16[1024,256]{1,0:T(8,128)(2,1)S(1)}, bf16[1024,256]{1,0:T(8,128)(2,1)}, u32[]{:S(2)}, u32[]{:S(2)}) %collective-permute-start.2) | collective-permute-done | bytes 524320 | tf_op jit(solution)/shard_map/kv_hop1/ppermute | solution.py:66
  71.5 5.2 %collective-permute-start.6 = (bf16[128,1024]{1,0:T(8,128)(2,1)S(1)}, bf16[128,1024]{1,0:T(8,128)(2,1)S(1)}, u32[]{:S(2)}, u32[]{:S(2)}) collective-permute-start(bf16[128,1024]{1,0:T(8,128)(2,1)S(1)} %slice.78), channel_id=1, source_target_pairs={{128,0},{129,1},{144,16},{145,17},{160,32},{161,33},{176,48},{177,... | collective-permute-start | bytes 786440 | tf_op jit(solution)/shard_map/far/ppermute | solution.py:61
  85.0 2.9 %constant_dynamic-update-slice_fusion.2 = (bf16[1024,1024]{1,0:T(8,128)(2,1)}, bf16[256,1024]{1,0:T(8,128)(2,1)}, bf16[1,256,1024]{2,1,0:T(8,128)(2,1)}) fusion(bf16[1024,1024]{1,0:T(8,128)(2,1)} %get-tuple-element.49, bf16[512,1024]{1,0:T(8,128)(2,1)} %hold.2, bf16[512,1024]{1,0:T(8,128)(2,1)} %collective-permute-done.5.refs_1_, pred[]{:T(512)S(6)} %lt.28), kind=kLoop, calls=%fused_computation.30 | loop fusion | flops 524288 | bytes 3670017
  88.7 3.2 %collective-permute-done.7 = bf16[128,1024]{1,0:T(8,128)(2,1)S(1)} collective-permute-done((bf16[128,1024]{1,0:T(8,128)(2,1)S(1)}, bf16[128,1024]{1,0:T(8,128)(2,1)S(1)}, u32[]{:S(2)}, u32[]{:S(2)}) %collective-permute-start.7) | collective-permute-done | bytes 262176 | tf_op jit(solution)/shard_map/far/ppermute | solution.py:61
  102.7 4.0 %project_kv.1 = bf16[512,256]{1,0:T(8,128)(2,1)S(1)} custom-call(s32[4]{0:T(128)S(1)} %fusion.7.index_ref, bf16[4,512,1024]{2,1,0:T(8,128)(2,1)S(1)} %bitcast.23, bf16[1024,256]{1,0:T(8,128)(2,1)S(1)} %copy-done.10, bf16[1024,256]{1,0:T(8,128)(2,1)} %collective-permute-done.2.refs_1_, bf16[512,256]{1,0:T(8,128)(2,1)S(1)} %copy-done.15, ...), custom_call_target="tpu_custom_call" | custom-call | flops 1024 | bytes 1024 | tf_op jit(solution)/shard_map/project_kv/pallas_call | solution.py:152
  108.8 2.7 %collective-permute-start.14 = (bf16[2,272,256]{2,0,1:T(2,128)(2,1)}, bf16[2,272,256]{2,0,1:T(2,128)(2,1)}, u32[]{:S(2)}, u32[]{:S(2)}) collective-permute-start(bf16[2,272,256]{2,0,1:T(2,128)(2,1)} %pad_maximum_fusion.6), channel_id=1, source_target_pairs={{0,4},{4,8},{8,12},{1,5},{5,9},{9,13},{2,6},{6,10},{10,14},{3,7},{... | collective-permute-start | bytes 835592 | tf_op jit(solution)/shard_map/kv_rows/ppermute | solution.py:71
  111.5 4.5 %collective-permute-start.13 = (bf16[2,272,256]{2,0,1:T(2,128)(2,1)}, bf16[2,272,256]{2,0,1:T(2,128)(2,1)}, u32[]{:S(2)}, u32[]{:S(2)}) collective-permute-start(bf16[2,272,256]{2,0,1:T(2,128)(2,1)} %pad_maximum_fusion.6), channel_id=1, source_target_pairs={{0,8},{4,12},{1,9},{5,13},{2,10},{6,14},{3,11},{7,15},{16,24},{20,... | collective-permute-start | bytes 835592 | tf_op jit(solution)/shard_map/kv_rows/ppermute | solution.py:71
  123.7 7.7 %project_q.1.query_ref = bf16[512,1024]{1,0:T(8,128)(2,1)S(1)} custom-call(s32[4]{0:T(128)S(1)} %fusion.7.index_ref, bf16[4,512,1024]{2,1,0:T(8,128)(2,1)S(1)} %bitcast.24, bf16[1024,1024]{1,0:T(8,128)(2,1)S(1)} %bitcast.31, bf16[1024,1024]{1,0:T(8,128)(2,1)S(1)} %copy-done.5, bf16[1024,1024]{1,0:T(8,128)(2,1)} %collective-permute-done.1.refs_2_, ...), custom_call_target="tpu_custom_call" | custom-call | flops 1024 | bytes 1024 | tf_op jit(solution)/shard_map/project_q/pallas_call | solution.py:152
  140.4 9.3 %attend.1.mixed_ref = bf16[512,1024]{1,0:T(8,128)(2,1)S(1)} custom-call(bf16[512,1024]{1,0:T(8,128)(2,1)S(1)} %project_q.1.query_ref, bf16[2,768,256]{2,1,0:T(8,128)(2,1)S(1)} %copy.19.key_ref.value_ref, bf16[2,768,256]{2,1,0:T(8,128)(2,1)S(1)} %copy.19.key_ref.value_ref, s32[2,256,1]{2,1,0:T(8,128)S(1)} %copy-done.13, ...), custom_call_target="tpu_custom_call" | custom-call | flops 1024 | bytes 1024 | tf_op jit(solution)/shard_map/attend/pallas_call | solution.py:197
  150.0 5.5 %spread_0.1 = (bf16[512,640]{1,0:T(8,128)(2,1)S(1)}, bf16[512,640]{1,0:T(8,128)(2,1)S(1)}, f32[512,640]{1,0:T(8,128)S(1)}, f32[512,640]{1,0:T(8,128)S(1)}) custom-call(s32[4]{0:T(128)S(1)} %and_select_fusion.1.index_ref, bf16[512,1024]{1,0:T(8,128)(2,1)S(1)} %attend.1.mixed_ref, bf16[1024,640]{1,0:T(8,128)(2,1)S(1)} %copy-done.3, ...), custom_call_target="tpu_custom_call" | custom-call | flops 1024 | bytes 1024 | tf_op jit(solution)/shard_map/spread_0/pallas_call | solution.py:235
  155.5 6.7 %collective-permute-start.20 = (bf16[512,640]{1,0:T(8,128)(2,1)S(1)}, bf16[512,640]{1,0:T(8,128)(2,1)S(1)}, u32[]{:S(2)}, u32[]{:S(2)}) collective-permute-start(bf16[512,640]{1,0:T(8,128)(2,1)S(1)} %get-tuple-element.38), channel_id=1, source_target_pairs={{0,1},{1,0},{2,3},{3,2},{4,5},{5,4},{6,7},{7,6},{8,9},{9,8},{10,11... | collective-permute-start | bytes 1966088 | tf_op jit(solution)/shard_map/core_passed_0/ppermute | solution.py:76
  164.5 6.1 %collective-permute-start.21 = (bf16[512,640]{1,0:T(8,128)(2,1)S(1)}, bf16[512,640]{1,0:T(8,128)(2,1)S(1)}, u32[]{:S(2)}, u32[]{:S(2)}) collective-permute-start(bf16[512,640]{1,0:T(8,128)(2,1)S(1)} %add_convert_fusion.1), channel_id=1, source_target_pairs={{0,2},{1,3},{2,0},{3,1},{4,6},{5,7},{6,4},{7,5},{8,10},{9,11},{10,... | collective-permute-start | bytes 1966088 | tf_op jit(solution)/shard_map/z_sum_0/ppermute | solution.py:76
  170.6 10.8 %collective-permute-done.22.ahead_ref = bf16[1024,384]{1,0:T(8,128)(2,1)S(1)} collective-permute-done((bf16[1024,384]{1,0:T(8,128)(2,1)S(1)}, bf16[1024,384]{1,0:T(8,128)(2,1)S(1)}, u32[]{:S(2)}, u32[]{:S(2)}) %collective-permute-start.22) | collective-permute-done | bytes 786464 | tf_op jit(solution)/shard_map/out_hop1_1/ppermute | solution.py:66
  184.0 8.4 %collective-permute-done.23.near_ref = bf16[512,384]{1,0:T(8,128)(2,1)S(1)} collective-permute-done((bf16[512,384]{1,0:T(8,128)(2,1)S(1)}, bf16[512,384]{1,0:T(8,128)(2,1)S(1)}, u32[]{:S(2)}, u32[]{:S(2)}) %collective-permute-start.23) | collective-permute-done | bytes 393248 | tf_op jit(solution)/shard_map/out_hop2_1/ppermute | solution.py:66
  192.4 2.6 %collective-permute-done.25.back_ref = bf16[512,384]{1,0:T(8,128)(2,1)S(1)} collective-permute-done((bf16[512,384]{1,0:T(8,128)(2,1)S(1)}, bf16[512,384]{1,0:T(8,128)(2,1)S(1)}, u32[]{:S(2)}, u32[]{:S(2)}) %collective-permute-start.25) | collective-permute-done | bytes 393248 | tf_op jit(solution)/shard_map/out_hop2_1/ppermute | solution.py:66
  194.9 3.1 %spread_1.1 = (bf16[512,384]{1,0:T(8,128)(2,1)S(1)}, bf16[512,384]{1,0:T(8,128)(2,1)S(1)}, f32[512,384]{1,0:T(8,128)S(1)}, f32[512,384]{1,0:T(8,128)S(1)}) custom-call(s32[4]{0:T(128)S(1)} %and_select_fusion.1.index_ref, bf16[512,1024]{1,0:T(8,128)(2,1)S(1)} %attend.1.mixed_ref, bf16[1024,384]{1,0:T(8,128)(2,1)S(1)} %copy-done.6, ...), custom_call_target="tpu_custom_call" | custom-call | flops 1024 | bytes 1024 | tf_op jit(solution)/shard_map/spread_1/pallas_call | solution.py:235
  202.2 5.5 %collective-permute-start.28 = (bf16[512,384]{1,0:T(8,128)(2,1)S(1)}, bf16[512,384]{1,0:T(8,128)(2,1)S(1)}, u32[]{:S(2)}, u32[]{:S(2)}) collective-permute-start(bf16[512,384]{1,0:T(8,128)(2,1)S(1)} %add_convert_fusion.3), channel_id=1, source_target_pairs={{0,2},{1,3},{2,0},{3,1},{4,6},{5,7},{6,4},{7,5},{8,10},{9,11},{10,... | collective-permute-start | bytes 1179656 | tf_op jit(solution)/shard_map/z_sum_1/ppermute | solution.py:76
  207.8 17.4 %collective-permute-done.28 = bf16[512,384]{1,0:T(8,128)(2,1)S(1)} collective-permute-done((bf16[512,384]{1,0:T(8,128)(2,1)S(1)}, bf16[512,384]{1,0:T(8,128)(2,1)S(1)}, u32[]{:S(2)}, u32[]{:S(2)}) %collective-permute-start.28) | collective-permute-done | bytes 393248 | tf_op jit(solution)/shard_map/z_sum_1/ppermute | solution.py:76
  (143 shorter events, 63.8 us)
Async XLA Ops:
  0.6 47.2 %collective-permute-start = (bf16[1024,1024]{1,0:T(8,128)(2,1)}, bf16[1024,1024]{1,0:T(8,128)(2,1)S(1)}, u32[]{:S(2)}, u32[]{:S(2)}) collective-permute-start(bf16[1024,1024]{1,0:T(8,128)(2,1)} %bitcast.29), channel_id=1, source_target_pairs={{4,0},{8,4},{12,8},{0,12},{5,1},{9,5},{13,9},{1,13},{6,2},{10,6},{... | collective-permute-start | bytes 6291464 | tf_op jit(solution)/shard_map/q_hop1/ppermute | solution.py:66
  3.2 47.7 %collective-permute-start.1 = (bf16[1024,1024]{1,0:T(8,128)(2,1)}, bf16[1024,1024]{1,0:T(8,128)(2,1)}, u32[]{:S(2)}, u32[]{:S(2)}) collective-permute-start(bf16[1024,1024]{1,0:T(8,128)(2,1)} %bitcast.30), channel_id=1, source_target_pairs={{12,0},{0,4},{4,8},{8,12},{13,1},{1,5},{5,9},{9,13},{14,2},{2,6},{... | collective-permute-start | bytes 6291464 | tf_op jit(solution)/shard_map/q_hop1/ppermute | solution.py:66
  5.5 48.9 %collective-permute-start.4 = (bf16[512,1024]{1,0:T(8,128)(2,1)}, bf16[512,1024]{1,0:T(8,128)(2,1)}, u32[]{:S(2)}, u32[]{:S(2)}) collective-permute-start(bf16[512,1024]{1,0:T(8,128)(2,1)} %pad_maximum_fusion), channel_id=1, source_target_pairs={{128,0},{129,1},{144,16},{145,17},{160,32},{161,33},{176,48},{177,... | collective-permute-start | bytes 3145736 | tf_op jit(solution)/shard_map/z_in/ppermute | solution.py:61
  10.6 49.3 %collective-permute-start.5 = (bf16[512,1024]{1,0:T(8,128)(2,1)}, bf16[512,1024]{1,0:T(8,128)(2,1)}, u32[]{:S(2)}, u32[]{:S(2)}) collective-permute-start(bf16[512,1024]{1,0:T(8,128)(2,1)} %pad_maximum_fusion), channel_id=1, source_target_pairs={{130,0},{131,1},{146,16},{147,17},{162,32},{163,33},{178,48},{179,... | collective-permute-start | bytes 3145736 | tf_op jit(solution)/shard_map/z_in/ppermute | solution.py:61
  50.9 11.7 %collective-permute-start.2 = (bf16[1024,256]{1,0:T(8,128)(2,1)S(1)}, bf16[1024,256]{1,0:T(8,128)(2,1)}, u32[]{:S(2)}, u32[]{:S(2)}) collective-permute-start(bf16[1024,256]{1,0:T(8,128)(2,1)S(1)} %pad_maximum_fusion.3.refs_0_), channel_id=1, source_target_pairs={{4,0},{8,4},{12,8},{0,12},{5,1},{9,5},{13,9},{1,13},{6,2},{10,6},{... | collective-permute-start | bytes 1572872 | tf_op jit(solution)/shard_map/kv_hop1/ppermute | solution.py:66
  51.2 13.0 %collective-permute-start.3 = (bf16[1024,256]{1,0:T(8,128)(2,1)S(1)}, bf16[1024,256]{1,0:T(8,128)(2,1)}, u32[]{:S(2)}, u32[]{:S(2)}) collective-permute-start(bf16[1024,256]{1,0:T(8,128)(2,1)S(1)} %pad_maximum_fusion.3.refs_0_), channel_id=1, source_target_pairs={{12,0},{0,4},{4,8},{8,12},{13,1},{1,5},{5,9},{9,13},{14,2},{2,6},{... | collective-permute-start | bytes 1572872 | tf_op jit(solution)/shard_map/kv_hop1/ppermute | solution.py:66
  65.3 31.7 %collective-permute-start.11 = (bf16[512,1024]{1,0:T(8,128)(2,1)}, bf16[512,1024]{1,0:T(8,128)(2,1)}, u32[]{:S(2)}, u32[]{:S(2)}) collective-permute-start(bf16[512,1024]{1,0:T(8,128)(2,1)} %slice.82), channel_id=1, source_target_pairs={{4,0},{8,4},{12,8},{0,12},{5,1},{9,5},{13,9},{1,13},{6,2},{10,6},{... | collective-permute-start | bytes 3145736 | tf_op jit(solution)/shard_map/q_hop2/ppermute | solution.py:66
  67.8 29.2 %collective-permute-start.12 = (bf16[512,1024]{1,0:T(8,128)(2,1)}, bf16[512,1024]{1,0:T(8,128)(2,1)}, u32[]{:S(2)}, u32[]{:S(2)}) collective-permute-start(bf16[512,1024]{1,0:T(8,128)(2,1)} %slice.83), channel_id=1, source_target_pairs={{12,0},{0,4},{4,8},{8,12},{13,1},{1,5},{5,9},{9,13},{14,2},{2,6},{... | collective-permute-start | bytes 3145736 | tf_op jit(solution)/shard_map/q_hop2/ppermute | solution.py:66
  71.5 13.4 %collective-permute-start.6 = (bf16[128,1024]{1,0:T(8,128)(2,1)S(1)}, bf16[128,1024]{1,0:T(8,128)(2,1)S(1)}, u32[]{:S(2)}, u32[]{:S(2)}) collective-permute-start(bf16[128,1024]{1,0:T(8,128)(2,1)S(1)} %slice.78), channel_id=1, source_target_pairs={{128,0},{129,1},{144,16},{145,17},{160,32},{161,33},{176,48},{177,... | collective-permute-start | bytes 786440 | tf_op jit(solution)/shard_map/far/ppermute | solution.py:61
  77.7 14.2 %collective-permute-start.7 = (bf16[128,1024]{1,0:T(8,128)(2,1)S(1)}, bf16[128,1024]{1,0:T(8,128)(2,1)S(1)}, u32[]{:S(2)}, u32[]{:S(2)}) collective-permute-start(bf16[128,1024]{1,0:T(8,128)(2,1)S(1)} %slice.79), channel_id=1, source_target_pairs={{130,0},{131,1},{146,16},{147,17},{162,32},{163,33},{178,48},{179,... | collective-permute-start | bytes 786440 | tf_op jit(solution)/shard_map/far/ppermute | solution.py:61
  78.7 15.8 %collective-permute-start.9 = (bf16[512,256]{1,0:T(8,128)(2,1)S(1)}, bf16[512,256]{1,0:T(8,128)(2,1)S(1)}, u32[]{:S(2)}, u32[]{:S(2)}) collective-permute-start(bf16[512,256]{1,0:T(8,128)(2,1)S(1)} %slice.80), channel_id=1, source_target_pairs={{4,0},{8,4},{12,8},{0,12},{5,1},{9,5},{13,9},{1,13},{6,2},{10,6},{... | collective-permute-start | bytes 786440 | tf_op jit(solution)/shard_map/kv_hop2/ppermute | solution.py:66
  84.9 12.0 %collective-permute-start.10 = (bf16[512,256]{1,0:T(8,128)(2,1)S(1)}, bf16[512,256]{1,0:T(8,128)(2,1)}, u32[]{:S(2)}, u32[]{:S(2)}) collective-permute-start(bf16[512,256]{1,0:T(8,128)(2,1)S(1)} %slice.81), channel_id=1, source_target_pairs={{12,0},{0,4},{4,8},{8,12},{13,1},{1,5},{5,9},{9,13},{14,2},{2,6},{... | collective-permute-start | bytes 786440 | tf_op jit(solution)/shard_map/kv_hop2/ppermute | solution.py:66
  97.0 34.4 %collective-permute-start.15 = (bf16[1024,640]{1,0:T(8,128)(2,1)}, bf16[1024,640]{1,0:T(8,128)(2,1)}, u32[]{:S(2)}, u32[]{:S(2)}) collective-permute-start(bf16[1024,640]{1,0:T(8,128)(2,1)} %hold.3.own_ref), channel_id=1, source_target_pairs={{4,0},{8,4},{12,8},{0,12},{5,1},{9,5},{13,9},{1,13},{6,2},{10,6},{... | collective-permute-start | bytes 3932168 | tf_op jit(solution)/shard_map/out_hop1_0/ppermute | solution.py:66
  97.1 35.6 %collective-permute-start.17 = (bf16[1024,640]{1,0:T(8,128)(2,1)}, bf16[1024,640]{1,0:T(8,128)(2,1)}, u32[]{:S(2)}, u32[]{:S(2)}) collective-permute-start(bf16[1024,640]{1,0:T(8,128)(2,1)} %hold.3.own_ref), channel_id=1, source_target_pairs={{12,0},{0,4},{4,8},{8,12},{13,1},{1,5},{5,9},{9,13},{14,2},{2,6},{... | collective-permute-start | bytes 3932168 | tf_op jit(solution)/shard_map/out_hop1_0/ppermute | solution.py:66
  108.8 26.6 %collective-permute-start.14 = (bf16[2,272,256]{2,0,1:T(2,128)(2,1)}, bf16[2,272,256]{2,0,1:T(2,128)(2,1)}, u32[]{:S(2)}, u32[]{:S(2)}) collective-permute-start(bf16[2,272,256]{2,0,1:T(2,128)(2,1)} %pad_maximum_fusion.6), channel_id=1, source_target_pairs={{0,4},{4,8},{8,12},{1,5},{5,9},{9,13},{2,6},{6,10},{10,14},{3,7},{... | collective-permute-start | bytes 835592 | tf_op jit(solution)/shard_map/kv_rows/ppermute | solution.py:71
  111.5 25.1 %collective-permute-start.13 = (bf16[2,272,256]{2,0,1:T(2,128)(2,1)}, bf16[2,272,256]{2,0,1:T(2,128)(2,1)}, u32[]{:S(2)}, u32[]{:S(2)}) collective-permute-start(bf16[2,272,256]{2,0,1:T(2,128)(2,1)} %pad_maximum_fusion.6), channel_id=1, source_target_pairs={{0,8},{4,12},{1,9},{5,13},{2,10},{6,14},{3,11},{7,15},{16,24},{20,... | collective-permute-start | bytes 835592 | tf_op jit(solution)/shard_map/kv_rows/ppermute | solution.py:71
  132.6 17.1 %collective-permute-start.16 = (bf16[512,640]{1,0:T(8,128)(2,1)S(1)}, bf16[512,640]{1,0:T(8,128)(2,1)S(1)}, u32[]{:S(2)}, u32[]{:S(2)}) collective-permute-start(bf16[512,640]{1,0:T(8,128)(2,1)S(1)} %slice.108), channel_id=1, source_target_pairs={{4,0},{8,4},{12,8},{0,12},{5,1},{9,5},{13,9},{1,13},{6,2},{10,6},{... | collective-permute-start | bytes 1966088 | tf_op jit(solution)/shard_map/out_hop2_0/ppermute | solution.py:66
  133.9 16.1 %collective-permute-start.18 = (bf16[512,640]{1,0:T(8,128)(2,1)S(1)}, bf16[512,640]{1,0:T(8,128)(2,1)S(1)}, u32[]{:S(2)}, u32[]{:S(2)}) collective-permute-start(bf16[512,640]{1,0:T(8,128)(2,1)S(1)} %slice.109), channel_id=1, source_target_pairs={{12,0},{0,4},{4,8},{8,12},{13,1},{1,5},{5,9},{9,13},{14,2},{2,6},{... | collective-permute-start | bytes 1966088 | tf_op jit(solution)/shard_map/out_hop2_0/ppermute | solution.py:66
  162.2 19.1 %collective-permute-start.22 = (bf16[1024,384]{1,0:T(8,128)(2,1)S(1)}, bf16[1024,384]{1,0:T(8,128)(2,1)S(1)}, u32[]{:S(2)}, u32[]{:S(2)}) collective-permute-start(bf16[1024,384]{1,0:T(8,128)(2,1)S(1)} %copy-done.6), channel_id=1, source_target_pairs={{4,0},{8,4},{12,8},{0,12},{5,1},{9,5},{13,9},{1,13},{6,2},{10,6},{... | collective-permute-start | bytes 2359304 | tf_op jit(solution)/shard_map/out_hop1_1/ppermute | solution.py:66
  162.2 21.6 %collective-permute-start.24 = (bf16[1024,384]{1,0:T(8,128)(2,1)S(1)}, bf16[1024,384]{1,0:T(8,128)(2,1)S(1)}, u32[]{:S(2)}, u32[]{:S(2)}) collective-permute-start(bf16[1024,384]{1,0:T(8,128)(2,1)S(1)} %copy-done.6), channel_id=1, source_target_pairs={{12,0},{0,4},{4,8},{8,12},{13,1},{1,5},{5,9},{9,13},{14,2},{2,6},{... | collective-permute-start | bytes 2359304 | tf_op jit(solution)/shard_map/out_hop1_1/ppermute | solution.py:66
  163.7 34.3 %collective-permute-start.19 = (bf16[512,640]{1,0:T(8,128)(2,1)S(1)}, bf16[512,640]{1,0:T(8,128)(2,1)S(1)}, u32[]{:S(2)}, u32[]{:S(2)}) collective-permute-start(bf16[512,640]{1,0:T(8,128)(2,1)S(1)} %get-tuple-element.36), channel_id=1, source_target_pairs={{0,1},{1,0},{2,3},{3,2},{4,5},{5,4},{6,7},{7,6},{8,9},{9,8},{10,11... | collective-permute-start | bytes 1966088 | tf_op jit(solution)/shard_map/core_kept_0/ppermute | solution.py:76
  164.5 35.2 %collective-permute-start.21 = (bf16[512,640]{1,0:T(8,128)(2,1)S(1)}, bf16[512,640]{1,0:T(8,128)(2,1)S(1)}, u32[]{:S(2)}, u32[]{:S(2)}) collective-permute-start(bf16[512,640]{1,0:T(8,128)(2,1)S(1)} %add_convert_fusion.1), channel_id=1, source_target_pairs={{0,2},{1,3},{2,0},{3,1},{4,6},{5,7},{6,4},{7,5},{8,10},{9,11},{10,... | collective-permute-start | bytes 1966088 | tf_op jit(solution)/shard_map/z_sum_0/ppermute | solution.py:76
  183.9 11.0 %collective-permute-start.25 = (bf16[512,384]{1,0:T(8,128)(2,1)S(1)}, bf16[512,384]{1,0:T(8,128)(2,1)S(1)}, u32[]{:S(2)}, u32[]{:S(2)}) collective-permute-start(bf16[512,384]{1,0:T(8,128)(2,1)S(1)} %slice.111), channel_id=1, source_target_pairs={{12,0},{0,4},{4,8},{8,12},{13,1},{1,5},{5,9},{9,13},{14,2},{2,6},{... | collective-permute-start | bytes 1179656 | tf_op jit(solution)/shard_map/out_hop2_1/ppermute | solution.py:66
  202.2 22.9 %collective-permute-start.28 = (bf16[512,384]{1,0:T(8,128)(2,1)S(1)}, bf16[512,384]{1,0:T(8,128)(2,1)S(1)}, u32[]{:S(2)}, u32[]{:S(2)}) collective-permute-start(bf16[512,384]{1,0:T(8,128)(2,1)S(1)} %add_convert_fusion.3), channel_id=1, source_target_pairs={{0,2},{1,3},{2,0},{3,1},{4,6},{5,7},{6,4},{7,5},{8,10},{9,11},{10,... | collective-permute-start | bytes 1179656 | tf_op jit(solution)/shard_map/z_sum_1/ppermute | solution.py:76
  (30 other events, 228.8 us)

commit v4 on v3

--- a/solution.py
+++ b/solution.py
@@ -13,7 +13,7 @@
 rope_base = 500000.0
 BF = jnp.bfloat16
 F32 = jnp.float32
-STRIPS = (5, 3)
+STRIPS = (1, 1)
 SHORT = 10**10
 LONG = 4 * 10**10
 
@@ -166,51 +166,63 @@
     )(order, normed, *arrays, cosine, sine)
 
 
-def attend_kernel(query_ref, key_ref, value_ref, query_doc_ref, key_doc_ref, out_ref, bias_ref):
+def attend_kernel(
+    place_ref, query_ref, query_doc_ref, two_ref, one_ref, own_ref, out_ref, bias_ref, key_scratch, value_scratch
+):
     rows, span = bias_ref.shape
     back = span - rows
 
     @pl.when(pl.program_id(1) == 0)
     def _():
-        at_query = lax.broadcasted_iota(jnp.int32, (rows, span), 0)
-        at_key = lax.broadcasted_iota(jnp.int32, (rows, span), 1) - back
-        allowed = (at_key <= at_query) & (query_doc_ref[0] == key_doc_ref[0])
-        bias_ref[...] = jnp.where(allowed, 0.0, -jnp.inf)
+        at_query = lax.broadcasted_iota(jnp.int32, (rows, rows), 0)
+        at_key = lax.broadcasted_iota(jnp.int32, (rows, rows), 1)
+        query_docs = query_doc_ref[0]
+        for part, ref in enumerate((two_ref, one_ref, own_ref)):
+            place = slice(part * rows, (part + 1) * rows)
+            first = ref.shape[1] - rows
+            key_scratch[place] = ref[0, first:, :HEAD]
+            value_scratch[place] = ref[0, first:, HEAD:]
+            exists = place_ref[0] >= 2 - part
+            key_docs = jnp.where(exists, ref[0, 0:1, :].astype(F32), -1.0)
+            allowed = (at_key + (part * rows - back) <= at_query) & (query_docs == key_docs)
+            bias_ref[:, place] = jnp.where(allowed, 0.0, -jnp.inf)
 
     for head in range(query_ref.shape[1] // HEAD):
         part = slice(head * HEAD, (head + 1) * HEAD)
         scores = lax.dot_general(
-            query_ref[:, part], key_ref[0], (((1,), (1,)), ((), ())), preferred_element_type=F32
+            query_ref[:, part], key_scratch[...], (((1,), (1,)), ((), ())), preferred_element_type=F32
         )
         masked = scores + bias_ref[...]
         peak = jnp.max(masked, axis=1, keepdims=True)
         weights = jnp.exp((masked - peak) * (1.0 / math.sqrt(HEAD)))
         totals = jnp.sum(weights, axis=1, keepdims=True)
-        mixed = jnp.dot(weights.astype(BF), value_ref[0], preferred_element_type=F32)
+        mixed = jnp.dot(weights.astype(BF), value_scratch[...], preferred_element_type=F32)
         out_ref[:, part] = (mixed / totals).astype(BF)
 
 
-def attend(queries, pairs, query_docs, key_docs):
-    batches, span, _ = pairs.shape
-    rows = queries.shape[0] // batches
+def attend(place, queries, query_docs, two, one, own):
+    batches, rows, _ = query_docs.shape
+    span = 3 * rows
     wide = 2 * HEAD
+    pair = pl.BlockSpec((1,) + own.shape[1:], lambda b, h: (b, 0, 0))
     return pl.pallas_call(
         attend_kernel,
         grid=(batches, queries.shape[1] // wide),
         in_specs=[
+            pl.BlockSpec(memory_space=pltpu.SMEM),
             pl.BlockSpec((rows, wide), lambda b, h: (b, h)),
-            pl.BlockSpec((1, span, HEAD), lambda b, h: (b, 0, 0)),
-            pl.BlockSpec((1, span, HEAD), lambda b, h: (b, 0, 1)),
             pl.BlockSpec((1, rows, 1), lambda b, h: (b, 0, 0)),
-            pl.BlockSpec((1, 1, span), lambda b, h: (b, 0, 0)),
+            pair,
+            pair,
+            pair,
         ],
         out_specs=pl.BlockSpec((rows, wide), lambda b, h: (b, h)),
         out_shape=jax.ShapeDtypeStruct(queries.shape, BF),
-        scratch_shapes=[pltpu.VMEM((rows, span), F32)],
+        scratch_shapes=[pltpu.VMEM((rows, span), F32), pltpu.VMEM((span, HEAD), BF), pltpu.VMEM((span, HEAD), BF)],
         compiler_params=pltpu.CompilerParams(vmem_limit_bytes=24 << 20),
         cost_estimate=pl.CostEstimate(flops=1024, transcendentals=0, bytes_accessed=1024),
         name="attend",
-    )(queries, pairs, pairs, query_docs, key_docs)
+    )(place, queries, query_docs, two, one, own)
 
 
 def spread_kernel(
@@ -331,10 +343,6 @@
     with jax.named_scope("out_hop1_0"):
         out_own[0] = hold(out_own[0], across_low, across_high, kv_near, kv_back, flops=LONG)
         out_hops = [first_hop(out_own[0])]
-    all_kv = jnp.concatenate((kv_two[:, id_rows:], kv_one[:, id_rows:], own_pair[:, id_rows:]), axis=1)
-    docs_one = jnp.where(c >= 1, kv_one[:, 0].astype(jnp.int32), -1)
-    docs_two = jnp.where(c >= 2, kv_two[:, 0].astype(jnp.int32), -1)
-    key_docs = jnp.concatenate((docs_two, docs_one, docs), axis=1)
     queries = project(
         feature_order,
         after(normed, own_kv),
@@ -351,7 +359,8 @@
         "project_q",
     )
     queries, out_own[1] = lax.optimization_barrier((queries, out_own[1]))
-    mixed = attend(queries, all_kv, docs[:, :, None], key_docs[:, None, :])
+    kv_one = hold(kv_one, kv_two, queries, flops=SHORT)
+    mixed = attend(c.reshape(1), queries, docs.astype(F32)[:, :, None], kv_two, kv_one, own_pair)
 
     residual = jnp.concatenate((mine, fetched), axis=0)
     term_order = ((t ^ flips) - c) % ring
@@ -360,10 +369,13 @@
     for index, (low, high) in enumerate(strips):
         ahead, behind = out_hops[index]
         with jax.named_scope("out_hop2_%d" % index):
-            near, back = second_hop(ahead, behind)
+            ahead_part, behind_part = ahead[: width // 2], behind[width // 2 :]
+            near, back = from_x(ahead_part, 1), from_x(behind_part, -1)
+        if index:
+            near = hold(near, back, flops=10000000000)
         if index + 1 < len(strips):
             with jax.named_scope("out_hop1_%d" % (index + 1)):
-                out_hops.append(first_hop(after(out_own[index + 1], near, back)))
+                out_hops.append(first_hop(after(out_own[index + 1], ahead_part, behind_part)))
         sent_kept, sent_passed, kept, passed = spread(
             term_order,
             after(mixed, *passed_before),
@@ -371,7 +383,8 @@
             "spread_%d" % index,
         )
         if index:
-            sent_passed = after(sent_passed, outputs[-1])
+            outputs[-1] = hold(outputs[-1], flops=5000000000)
+            sent_kept = after(sent_kept, outputs[-1])
         with jax.named_scope("core_passed_%d" % index):
             passed = (passed + from_tensor(sent_passed, 1).astype(F32)).astype(BF)
         with jax.named_scope("z_sum_%d" % index):

time: 229 us -> 237 us (1.035)
  starting transfers between devices: 53.1 us -> 61.3 us
  waiting for transfers between devices: 99.5 us -> 91.8 us
  Pallas kernels: 31.6 us -> 34.5 us
    ppermute x16, waiting for transfers between devices: 67 us -> 48.7 us  [from_x(): lax.ppermute(block, 'ctx', [((c + step) % count, c) for c in range(count)])]
    ppermute x7, waiting for transfers between devices: 20.3 us -> 29.9 us  [from_tensor(): return lax.ppermute(block, 'tensor', [(t, t ^ flip) for t in range(count)])]
    ppermute x7, starting transfers between devices: 21.8 us -> 28.7 us  [from_tensor(): return lax.ppermute(block, 'tensor', [(t, t ^ flip) for t in range(count)])]
    slice x2 -> x4, local copies, waits for them, and re-layouts: 2.26 us -> 5.89 us  [body(): ahead_part, behind_part = (ahead[:width // 2], behind[width // 2:])]
    slice x8 -> x4, local copies, waits for them, and re-layouts: 7.66 us -> 4.35 us  [second_hop(): return (from_x(ahead[:half], 1), from_x(behind[half:], -1))]
    unnamed x52 -> x68, local copies, waits for them, and re-layouts: 7.04 us -> 10.3 us
  transfers between devices with their start and end apart: 29 -> 29, of which waited for: 17 -> 14; matrix products, arithmetic and copies ran while one was open for 15% -> 14% of each run, Pallas kernels for 12% -> 15%
where the time goes in v4:
time: 237 us; the launch traced here: 233 us
  waiting for transfers between devices  91.8 us (39%)
  starting transfers between devices  61.3 us (26%)
  Pallas kernels  34.5 us (15%)
  local copies, waits for them, and re-layouts  28 us (12%)
  other arithmetic  16.6 us (7%)
    ppermute x16, waiting for transfers between devices, from_x(): lax.ppermute(block, 'ctx', [((c + step) % count, c) for c in range(count)])  48.7 us
    ppermute x7, waiting for transfers between devices, from_tensor(): return lax.ppermute(block, 'tensor', [(t, t ^ flip) for t in range(count)])  29.9 us
    ppermute x7, starting transfers between devices, from_tensor(): return lax.ppermute(block, 'tensor', [(t, t ^ flip) for t in range(count)])  28.7 us
    ppermute x16, starting transfers between devices, from_x(): lax.ppermute(block, 'ctx', [((c + step) % count, c) for c in range(count)])  14.8 us
    ppermute x4, waiting for transfers between devices, from_z(): return lax.ppermute(block, ('section', 'tensor'), route)  13.2 us
    pallas_call x2, Pallas kernels, project(): pl.pallas_call(functools.partial(project_kernel, pieces=[(step, low) for...  11.3 us
    pallas_call x2, Pallas kernels, spread(): pl.pallas_call(spread_kernel, in_specs=[pl.BlockSpec(memory_space=pltpu.S...  10.8 us
    ppermute x4, starting transfers between devices, from_z(): return lax.ppermute(block, ('section', 'tensor'), route)  10.4 us
  transfers between devices with their start and end apart: 29, of which 14 were waited for; matrix products, arithmetic and copies ran while one was open for 14% of the time, Pallas kernels for 15%

profile of v4, /device:TPU:49, one launch (start us, length us, event | category | flops | bytes accessed | tf_op | source)
XLA Modules:
  0.0 233.2 jit_solution(11791815741226428848)
XLA Ops:
  5.5 5.1 %collective-permute-start.4 = (bf16[512,1024]{1,0:T(8,128)(2,1)}, bf16[512,1024]{1,0:T(8,128)(2,1)}, u32[]{:S(2)}, u32[]{:S(2)}) collective-permute-start(bf16[512,1024]{1,0:T(8,128)(2,1)} %pad_maximum_fusion), channel_id=1, source_target_pairs={{128,0},{129,1},{144,16},{145,17},{160,32},{161,33},{176,48},{177,... | collective-permute-start | bytes 3145736 | tf_op jit(solution)/shard_map/z_in/ppermute | solution.py:61
  10.8 3.2 %fusion.9 = (bf16[1024,512]{1,0:T(8,128)(2,1)}, bf16[1024,512]{1,0:T(8,128)(2,1)}) fusion(bf16[1024,1024]{1,0:T(8,128)(2,1)} %bitcast.30), kind=kLoop, calls=%fused_computation.52 | loop fusion | bytes 4194304 | tf_op jit(solution)/shard_map/slice | solution.py:291
  14.0 33.8 %collective-permute-done.refs_1_ = bf16[1024,1024]{1,0:T(8,128)(2,1)S(1)} collective-permute-done((bf16[1024,1024]{1,0:T(8,128)(2,1)}, bf16[1024,1024]{1,0:T(8,128)(2,1)S(1)}, u32[]{:S(2)}, u32[]{:S(2)}) %collective-permute-start) | collective-permute-done | bytes 2097184 | tf_op jit(solution)/shard_map/q_hop1/ppermute | solution.py:66
  47.8 3.1 %collective-permute-done.1.refs_2_ = bf16[1024,1024]{1,0:T(8,128)(2,1)} collective-permute-done((bf16[1024,1024]{1,0:T(8,128)(2,1)}, bf16[1024,1024]{1,0:T(8,128)(2,1)}, u32[]{:S(2)}, u32[]{:S(2)}) %collective-permute-start.1) | collective-permute-done | bytes 2097184 | tf_op jit(solution)/shard_map/q_hop1/ppermute | solution.py:66
  54.3 5.5 %collective-permute-done.5.refs_1_ = bf16[512,1024]{1,0:T(8,128)(2,1)} collective-permute-done((bf16[512,1024]{1,0:T(8,128)(2,1)}, bf16[512,1024]{1,0:T(8,128)(2,1)}, u32[]{:S(2)}, u32[]{:S(2)}) %collective-permute-start.5) | collective-permute-done | bytes 1048608 | tf_op jit(solution)/shard_map/z_in/ppermute | solution.py:61
  59.9 2.7 %collective-permute-done.2.refs_1_ = bf16[1024,256]{1,0:T(8,128)(2,1)S(1)} collective-permute-done((bf16[1024,256]{1,0:T(8,128)(2,1)S(1)}, bf16[1024,256]{1,0:T(8,128)(2,1)S(1)}, u32[]{:S(2)}, u32[]{:S(2)}) %collective-permute-start.2) | collective-permute-done | bytes 524320 | tf_op jit(solution)/shard_map/kv_hop1/ppermute | solution.py:66
  71.6 5.2 %collective-permute-start.6 = (bf16[128,1024]{1,0:T(8,128)(2,1)S(1)}, bf16[128,1024]{1,0:T(8,128)(2,1)S(1)}, u32[]{:S(2)}, u32[]{:S(2)}) collective-permute-start(bf16[128,1024]{1,0:T(8,128)(2,1)S(1)} %slice.66), channel_id=1, source_target_pairs={{128,0},{129,1},{144,16},{145,17},{160,32},{161,33},{176,48},{177,... | collective-permute-start | bytes 786440 | tf_op jit(solution)/shard_map/far/ppermute | solution.py:61
  85.1 2.9 %constant_dynamic-update-slice_fusion.2 = (bf16[1024,1024]{1,0:T(8,128)(2,1)}, bf16[256,1024]{1,0:T(8,128)(2,1)}, bf16[1,256,1024]{2,1,0:T(8,128)(2,1)}) fusion(bf16[1024,1024]{1,0:T(8,128)(2,1)} %get-tuple-element.49, bf16[512,1024]{1,0:T(8,128)(2,1)} %hold.5, bf16[512,1024]{1,0:T(8,128)(2,1)} %collective-permute-done.5.refs_1_, pred[]{:T(512)S(6)} %lt.28), kind=kLoop, calls=%fused_computation.30 | loop fusion | flops 524288 | bytes 3670017
  88.8 3.2 %collective-permute-done.7 = bf16[128,1024]{1,0:T(8,128)(2,1)S(1)} collective-permute-done((bf16[128,1024]{1,0:T(8,128)(2,1)S(1)}, bf16[128,1024]{1,0:T(8,128)(2,1)S(1)}, u32[]{:S(2)}, u32[]{:S(2)}) %collective-permute-start.7) | collective-permute-done | bytes 262176 | tf_op jit(solution)/shard_map/far/ppermute | solution.py:61
  102.7 3.6 %project_kv.1 = bf16[512,256]{1,0:T(8,128)(2,1)S(1)} custom-call(s32[4]{0:T(128)S(1)} %fusion.5.index_ref, bf16[4,512,1024]{2,1,0:T(8,128)(2,1)S(1)} %bitcast.20, bf16[1024,256]{1,0:T(8,128)(2,1)S(1)} %copy-done.11, bf16[1024,256]{1,0:T(8,128)(2,1)S(1)} %copy-done.15, bf16[512,256]{1,0:T(8,128)(2,1)S(1)} %copy-done.22, ...), custom_call_target="tpu_custom_call" | custom-call | flops 1024 | bytes 1024 | tf_op jit(solution)/shard_map/project_kv/pallas_call | solution.py:152
  107.0 2.8 %collective-permute-start.13 = (bf16[2,272,256]{2,1,0:T(8,128)(2,1)}, bf16[2,272,256]{2,1,0:T(8,128)(2,1)}, u32[]{:S(2)}, u32[]{:S(2)}) collective-permute-start(bf16[2,272,256]{2,1,0:T(8,128)(2,1)} %pad_maximum_fusion.5.own_ref), channel_id=1, source_target_pairs={{0,8},{4,12},{1,9},{5,13},{2,10},{6,14},{3,11},{7,15},{16,24},{20,... | collective-permute-start | bytes 835592 | tf_op jit(solution)/shard_map/kv_rows/ppermute | solution.py:71
  109.8 4.5 %collective-permute-start.14 = (bf16[2,272,256]{2,1,0:T(8,128)(2,1)}, bf16[2,272,256]{2,1,0:T(8,128)(2,1)}, u32[]{:S(2)}, u32[]{:S(2)}) collective-permute-start(bf16[2,272,256]{2,1,0:T(8,128)(2,1)} %pad_maximum_fusion.5.own_ref), channel_id=1, source_target_pairs={{0,4},{4,8},{8,12},{1,5},{5,9},{9,13},{2,6},{6,10},{10,14},{3,7},{... | collective-permute-start | bytes 835592 | tf_op jit(solution)/shard_map/kv_rows/ppermute | solution.py:71
  127.5 7.7 %project_q.1.refs_2_.query_ref = bf16[512,1024]{1,0:T(8,128)(2,1)S(1)} custom-call(s32[4]{0:T(128)S(1)} %fusion.5.index_ref, bf16[4,512,1024]{2,1,0:T(8,128)(2,1)S(1)} %bitcast.21, bf16[1024,1024]{1,0:T(8,128)(2,1)S(1)} %bitcast.28, bf16[1024,1024]{1,0:T(8,128)(2,1)S(1)} %copy-done.4, bf16[1024,1024]{1,0:T(8,128)(2,1)} %collective-permute-done.1.refs_2_, ...), custom_call_target="tpu_custom_call" | custom-call | flops 1024 | bytes 1024 | tf_op jit(solution)/shard_map/project_q/pallas_call | solution.py:152
  136.3 2.7 %collective-permute-start.22 = (bf16[1024,512]{1,0:T(8,128)(2,1)}, bf16[1024,512]{1,0:T(8,128)(2,1)}, u32[]{:S(2)}, u32[]{:S(2)}) collective-permute-start(bf16[1024,512]{1,0:T(8,128)(2,1)} %get-tuple-element.41.own_ref), channel_id=1, source_target_pairs={{4,0},{8,4},{12,8},{0,12},{5,1},{9,5},{13,9},{1,13},{6,2},{10,6},{... | collective-permute-start | bytes 3145736 | tf_op jit(solution)/shard_map/out_hop1_1/ppermute | solution.py:66
  139.0 10.3 %attend.1.mixed_ref = bf16[512,1024]{1,0:T(8,128)(2,1)S(1)} custom-call(s32[1]{0:T(128)} %bitcast.6.place_ref, bf16[512,1024]{1,0:T(8,128)(2,1)S(1)} %copy-done.7, f32[2,256,1]{2,1,0:T(8,128)S(1)} %copy-done.20, bf16[2,272,256]{2,1,0:T(8,128)(2,1)} %collective-permute-done.13.refs_1_.two_ref, bf16[2,272,256]{2,1,0:T(8,128)(2,1)} %hold.6.one_ref, ...), custom_call_target="tpu_custom_call" | custom-call | flops 1024 | bytes 1024 | tf_op jit(solution)/shard_map/attend/pallas_call | solution.py:208
  149.4 5.3 %spread_0.1 = (bf16[512,512]{1,0:T(8,128)(2,1)}, bf16[512,512]{1,0:T(8,128)(2,1)S(1)}, f32[512,512]{1,0:T(8,128)S(1)}, f32[512,512]{1,0:T(8,128)S(1)}) custom-call(s32[4]{0:T(128)S(1)} %and_select_fusion.1.index_ref, bf16[512,1024]{1,0:T(8,128)(2,1)S(1)} %attend.1.mixed_ref, bf16[1024,512]{1,0:T(8,128)(2,1)S(1)} %copy-done.5, ...), custom_call_target="tpu_custom_call" | custom-call | flops 1024 | bytes 1024 | tf_op jit(solution)/shard_map/spread_0/pallas_call | solution.py:247
  154.6 9.8 %collective-permute-start.20 = (bf16[512,512]{1,0:T(8,128)(2,1)S(1)}, bf16[512,512]{1,0:T(8,128)(2,1)S(1)}, u32[]{:S(2)}, u32[]{:S(2)}) collective-permute-start(bf16[512,512]{1,0:T(8,128)(2,1)S(1)} %get-tuple-element.38), channel_id=1, source_target_pairs={{0,1},{1,0},{2,3},{3,2},{4,5},{5,4},{6,7},{7,6},{8,9},{9,8},{10,11... | collective-permute-start | bytes 1572872 | tf_op jit(solution)/shard_map/core_passed_0/ppermute | solution.py:76
  168.6 3.1 %collective-permute-start.19 = (bf16[512,512]{1,0:T(8,128)(2,1)}, bf16[512,512]{1,0:T(8,128)(2,1)}, u32[]{:S(2)}, u32[]{:S(2)}) collective-permute-start(bf16[512,512]{1,0:T(8,128)(2,1)} %get-tuple-element.36), channel_id=1, source_target_pairs={{0,1},{1,0},{2,3},{3,2},{4,5},{5,4},{6,7},{7,6},{8,9},{9,8},{10,11... | collective-permute-start | bytes 1572872 | tf_op jit(solution)/shard_map/core_kept_0/ppermute | solution.py:76
  172.7 6.0 %collective-permute-start.21 = (bf16[512,512]{1,0:T(8,128)(2,1)}, bf16[512,512]{1,0:T(8,128)(2,1)}, u32[]{:S(2)}, u32[]{:S(2)}) collective-permute-start(bf16[512,512]{1,0:T(8,128)(2,1)} %add_convert_fusion.3), channel_id=1, source_target_pairs={{0,2},{1,3},{2,0},{3,1},{4,6},{5,7},{6,4},{7,5},{8,10},{9,11},{10,... | collective-permute-start | bytes 1572872 | tf_op jit(solution)/shard_map/z_sum_0/ppermute | solution.py:76
  179.6 2.6 %collective-permute-done.25.refs_1_.back_ref = bf16[512,512]{1,0:T(8,128)(2,1)} collective-permute-done((bf16[512,512]{1,0:T(8,128)(2,1)S(1)}, bf16[512,512]{1,0:T(8,128)(2,1)}, u32[]{:S(2)}, u32[]{:S(2)}) %collective-permute-start.25) | collective-permute-done | bytes 524320 | tf_op jit(solution)/shard_map/out_hop2_1/ppermute | solution.py:66
  182.2 5.5 %spread_1.1 = (bf16[512,512]{1,0:T(8,128)(2,1)S(1)}, bf16[512,512]{1,0:T(8,128)(2,1)}, f32[512,512]{1,0:T(8,128)S(1)}, f32[512,512]{1,0:T(8,128)S(1)}) custom-call(s32[4]{0:T(128)S(1)} %and_select_fusion.1.index_ref, bf16[512,1024]{1,0:T(8,128)(2,1)S(1)} %attend.1.mixed_ref, bf16[1024,512]{1,0:T(8,128)(2,1)} %get-tuple-element.41.own_ref, ...), custom_call_target="tpu_custom_call" | custom-call | flops 1024 | bytes 1024 | tf_op jit(solution)/shard_map/spread_1/pallas_call | solution.py:247
  192.4 10.2 %collective-permute-done.21 = bf16[512,512]{1,0:T(8,128)(2,1)} collective-permute-done((bf16[512,512]{1,0:T(8,128)(2,1)}, bf16[512,512]{1,0:T(8,128)(2,1)}, u32[]{:S(2)}, u32[]{:S(2)}) %collective-permute-start.21) | collective-permute-done | bytes 524320 | tf_op jit(solution)/shard_map/z_sum_0/ppermute | solution.py:76
  206.8 5.3 %collective-permute-start.28 = (bf16[512,512]{1,0:T(8,128)(2,1)S(1)}, bf16[512,512]{1,0:T(8,128)(2,1)S(1)}, u32[]{:S(2)}, u32[]{:S(2)}) collective-permute-start(bf16[512,512]{1,0:T(8,128)(2,1)S(1)} %add_convert_fusion.1), channel_id=1, source_target_pairs={{0,2},{1,3},{2,0},{3,1},{4,6},{5,7},{6,4},{7,5},{8,10},{9,11},{10,... | collective-permute-start | bytes 1572872 | tf_op jit(solution)/shard_map/z_sum_1/ppermute | solution.py:76
  212.1 19.7 %collective-permute-done.28 = bf16[512,512]{1,0:T(8,128)(2,1)S(1)} collective-permute-done((bf16[512,512]{1,0:T(8,128)(2,1)S(1)}, bf16[512,512]{1,0:T(8,128)(2,1)S(1)}, u32[]{:S(2)}, u32[]{:S(2)}) %collective-permute-start.28) | collective-permute-done | bytes 524320 | tf_op jit(solution)/shard_map/z_sum_1/ppermute | solution.py:76
  (156 shorter events, 68.2 us)
Async XLA Ops:
  0.7 47.2 %collective-permute-start = (bf16[1024,1024]{1,0:T(8,128)(2,1)}, bf16[1024,1024]{1,0:T(8,128)(2,1)S(1)}, u32[]{:S(2)}, u32[]{:S(2)}) collective-permute-start(bf16[1024,1024]{1,0:T(8,128)(2,1)} %bitcast.26), channel_id=1, source_target_pairs={{4,0},{8,4},{12,8},{0,12},{5,1},{9,5},{13,9},{1,13},{6,2},{10,6},{... | collective-permute-start | bytes 6291464 | tf_op jit(solution)/shard_map/q_hop1/ppermute | solution.py:66
  3.2 47.7 %collective-permute-start.1 = (bf16[1024,1024]{1,0:T(8,128)(2,1)}, bf16[1024,1024]{1,0:T(8,128)(2,1)}, u32[]{:S(2)}, u32[]{:S(2)}) collective-permute-start(bf16[1024,1024]{1,0:T(8,128)(2,1)} %bitcast.27), channel_id=1, source_target_pairs={{12,0},{0,4},{4,8},{8,12},{13,1},{1,5},{5,9},{9,13},{14,2},{2,6},{... | collective-permute-start | bytes 6291464 | tf_op jit(solution)/shard_map/q_hop1/ppermute | solution.py:66
  5.5 48.9 %collective-permute-start.4 = (bf16[512,1024]{1,0:T(8,128)(2,1)}, bf16[512,1024]{1,0:T(8,128)(2,1)}, u32[]{:S(2)}, u32[]{:S(2)}) collective-permute-start(bf16[512,1024]{1,0:T(8,128)(2,1)} %pad_maximum_fusion), channel_id=1, source_target_pairs={{128,0},{129,1},{144,16},{145,17},{160,32},{161,33},{176,48},{177,... | collective-permute-start | bytes 3145736 | tf_op jit(solution)/shard_map/z_in/ppermute | solution.py:61
  10.6 49.3 %collective-permute-start.5 = (bf16[512,1024]{1,0:T(8,128)(2,1)}, bf16[512,1024]{1,0:T(8,128)(2,1)}, u32[]{:S(2)}, u32[]{:S(2)}) collective-permute-start(bf16[512,1024]{1,0:T(8,128)(2,1)} %pad_maximum_fusion), channel_id=1, source_target_pairs={{130,0},{131,1},{146,16},{147,17},{162,32},{163,33},{178,48},{179,... | collective-permute-start | bytes 3145736 | tf_op jit(solution)/shard_map/z_in/ppermute | solution.py:61
  65.3 31.7 %collective-permute-start.11 = (bf16[512,1024]{1,0:T(8,128)(2,1)}, bf16[512,1024]{1,0:T(8,128)(2,1)}, u32[]{:S(2)}, u32[]{:S(2)}) collective-permute-start(bf16[512,1024]{1,0:T(8,128)(2,1)} %slice.70), channel_id=1, source_target_pairs={{4,0},{8,4},{12,8},{0,12},{5,1},{9,5},{13,9},{1,13},{6,2},{10,6},{... | collective-permute-start | bytes 3145736 | tf_op jit(solution)/shard_map/q_hop2/ppermute | solution.py:66
  67.8 29.2 %collective-permute-start.12 = (bf16[512,1024]{1,0:T(8,128)(2,1)}, bf16[512,1024]{1,0:T(8,128)(2,1)}, u32[]{:S(2)}, u32[]{:S(2)}) collective-permute-start(bf16[512,1024]{1,0:T(8,128)(2,1)} %slice.71), channel_id=1, source_target_pairs={{12,0},{0,4},{4,8},{8,12},{13,1},{1,5},{5,9},{9,13},{14,2},{2,6},{... | collective-permute-start | bytes 3145736 | tf_op jit(solution)/shard_map/q_hop2/ppermute | solution.py:66
  71.6 13.4 %collective-permute-start.6 = (bf16[128,1024]{1,0:T(8,128)(2,1)S(1)}, bf16[128,1024]{1,0:T(8,128)(2,1)S(1)}, u32[]{:S(2)}, u32[]{:S(2)}) collective-permute-start(bf16[128,1024]{1,0:T(8,128)(2,1)S(1)} %slice.66), channel_id=1, source_target_pairs={{128,0},{129,1},{144,16},{145,17},{160,32},{161,33},{176,48},{177,... | collective-permute-start | bytes 786440 | tf_op jit(solution)/shard_map/far/ppermute | solution.py:61
  77.8 14.2 %collective-permute-start.7 = (bf16[128,1024]{1,0:T(8,128)(2,1)S(1)}, bf16[128,1024]{1,0:T(8,128)(2,1)S(1)}, u32[]{:S(2)}, u32[]{:S(2)}) collective-permute-start(bf16[128,1024]{1,0:T(8,128)(2,1)S(1)} %slice.67), channel_id=1, source_target_pairs={{130,0},{131,1},{146,16},{147,17},{162,32},{163,33},{178,48},{179,... | collective-permute-start | bytes 786440 | tf_op jit(solution)/shard_map/far/ppermute | solution.py:61
  77.9 16.8 %collective-permute-start.9 = (bf16[512,256]{1,0:T(8,128)(2,1)S(1)}, bf16[512,256]{1,0:T(8,128)(2,1)S(1)}, u32[]{:S(2)}, u32[]{:S(2)}) collective-permute-start(bf16[512,256]{1,0:T(8,128)(2,1)S(1)} %slice.68), channel_id=1, source_target_pairs={{4,0},{8,4},{12,8},{0,12},{5,1},{9,5},{13,9},{1,13},{6,2},{10,6},{... | collective-permute-start | bytes 786440 | tf_op jit(solution)/shard_map/kv_hop2/ppermute | solution.py:66
  97.0 21.5 %collective-permute-start.15 = (bf16[1024,512]{1,0:T(8,128)(2,1)}, bf16[1024,512]{1,0:T(8,128)(2,1)}, u32[]{:S(2)}, u32[]{:S(2)}) collective-permute-start(bf16[1024,512]{1,0:T(8,128)(2,1)} %hold.7.own_ref), channel_id=1, source_target_pairs={{4,0},{8,4},{12,8},{0,12},{5,1},{9,5},{13,9},{1,13},{6,2},{10,6},{... | collective-permute-start | bytes 3145736 | tf_op jit(solution)/shard_map/out_hop1_0/ppermute | solution.py:66
  97.1 24.8 %collective-permute-start.17 = (bf16[1024,512]{1,0:T(8,128)(2,1)}, bf16[1024,512]{1,0:T(8,128)(2,1)}, u32[]{:S(2)}, u32[]{:S(2)}) collective-permute-start(bf16[1024,512]{1,0:T(8,128)(2,1)} %hold.7.own_ref), channel_id=1, source_target_pairs={{12,0},{0,4},{4,8},{8,12},{13,1},{1,5},{5,9},{9,13},{14,2},{2,6},{... | collective-permute-start | bytes 3145736 | tf_op jit(solution)/shard_map/out_hop1_0/ppermute | solution.py:66
  107.0 31.9 %collective-permute-start.13 = (bf16[2,272,256]{2,1,0:T(8,128)(2,1)}, bf16[2,272,256]{2,1,0:T(8,128)(2,1)}, u32[]{:S(2)}, u32[]{:S(2)}) collective-permute-start(bf16[2,272,256]{2,1,0:T(8,128)(2,1)} %pad_maximum_fusion.5.own_ref), channel_id=1, source_target_pairs={{0,8},{4,12},{1,9},{5,13},{2,10},{6,14},{3,11},{7,15},{16,24},{20,... | collective-permute-start | bytes 835592 | tf_op jit(solution)/shard_map/kv_rows/ppermute | solution.py:71
  109.8 29.2 %collective-permute-start.14 = (bf16[2,272,256]{2,1,0:T(8,128)(2,1)}, bf16[2,272,256]{2,1,0:T(8,128)(2,1)}, u32[]{:S(2)}, u32[]{:S(2)}) collective-permute-start(bf16[2,272,256]{2,1,0:T(8,128)(2,1)} %pad_maximum_fusion.5.own_ref), channel_id=1, source_target_pairs={{0,4},{4,8},{8,12},{1,5},{5,9},{9,13},{2,6},{6,10},{10,14},{3,7},{... | collective-permute-start | bytes 835592 | tf_op jit(solution)/shard_map/kv_rows/ppermute | solution.py:71
  120.4 28.9 %collective-permute-start.16 = (bf16[512,512]{1,0:T(8,128)(2,1)}, bf16[512,512]{1,0:T(8,128)(2,1)}, u32[]{:S(2)}, u32[]{:S(2)}) collective-permute-start(bf16[512,512]{1,0:T(8,128)(2,1)} %slice.88), channel_id=1, source_target_pairs={{4,0},{8,4},{12,8},{0,12},{5,1},{9,5},{13,9},{1,13},{6,2},{10,6},{... | collective-permute-start | bytes 1572872 | tf_op jit(solution)/shard_map/out_hop2_0/ppermute | solution.py:66
  123.8 25.6 %collective-permute-start.18 = (bf16[512,512]{1,0:T(8,128)(2,1)}, bf16[512,512]{1,0:T(8,128)(2,1)}, u32[]{:S(2)}, u32[]{:S(2)}) collective-permute-start(bf16[512,512]{1,0:T(8,128)(2,1)} %slice.89), channel_id=1, source_target_pairs={{12,0},{0,4},{4,8},{8,12},{13,1},{1,5},{5,9},{9,13},{14,2},{2,6},{... | collective-permute-start | bytes 1572872 | tf_op jit(solution)/shard_map/out_hop2_0/ppermute | solution.py:66
  136.3 28.1 %collective-permute-start.22 = (bf16[1024,512]{1,0:T(8,128)(2,1)}, bf16[1024,512]{1,0:T(8,128)(2,1)}, u32[]{:S(2)}, u32[]{:S(2)}) collective-permute-start(bf16[1024,512]{1,0:T(8,128)(2,1)} %get-tuple-element.41.own_ref), channel_id=1, source_target_pairs={{4,0},{8,4},{12,8},{0,12},{5,1},{9,5},{13,9},{1,13},{6,2},{10,6},{... | collective-permute-start | bytes 3145736 | tf_op jit(solution)/shard_map/out_hop1_1/ppermute | solution.py:66
  139.0 28.0 %collective-permute-start.24 = (bf16[1024,512]{1,0:T(8,128)(2,1)}, bf16[1024,512]{1,0:T(8,128)(2,1)}, u32[]{:S(2)}, u32[]{:S(2)}) collective-permute-start(bf16[1024,512]{1,0:T(8,128)(2,1)} %get-tuple-element.41.own_ref), channel_id=1, source_target_pairs={{12,0},{0,4},{4,8},{8,12},{13,1},{1,5},{5,9},{9,13},{14,2},{2,6},{... | collective-permute-start | bytes 3145736 | tf_op jit(solution)/shard_map/out_hop1_1/ppermute | solution.py:66
  154.6 17.2 %collective-permute-start.20 = (bf16[512,512]{1,0:T(8,128)(2,1)S(1)}, bf16[512,512]{1,0:T(8,128)(2,1)S(1)}, u32[]{:S(2)}, u32[]{:S(2)}) collective-permute-start(bf16[512,512]{1,0:T(8,128)(2,1)S(1)} %get-tuple-element.38), channel_id=1, source_target_pairs={{0,1},{1,0},{2,3},{3,2},{4,5},{5,4},{6,7},{7,6},{8,9},{9,8},{10,11... | collective-permute-start | bytes 1572872 | tf_op jit(solution)/shard_map/core_passed_0/ppermute | solution.py:76
  165.5 14.1 %collective-permute-start.23 = (bf16[512,512]{1,0:T(8,128)(2,1)S(1)}, bf16[512,512]{1,0:T(8,128)(2,1)}, u32[]{:S(2)}, u32[]{:S(2)}) collective-permute-start(bf16[512,512]{1,0:T(8,128)(2,1)S(1)} %slice.90), channel_id=1, source_target_pairs={{4,0},{8,4},{12,8},{0,12},{5,1},{9,5},{13,9},{1,13},{6,2},{10,6},{... | collective-permute-start | bytes 1572872 | tf_op jit(solution)/shard_map/out_hop2_1/ppermute | solution.py:66
  168.1 14.1 %collective-permute-start.25 = (bf16[512,512]{1,0:T(8,128)(2,1)S(1)}, bf16[512,512]{1,0:T(8,128)(2,1)}, u32[]{:S(2)}, u32[]{:S(2)}) collective-permute-start(bf16[512,512]{1,0:T(8,128)(2,1)S(1)} %slice.91), channel_id=1, source_target_pairs={{12,0},{0,4},{4,8},{8,12},{13,1},{1,5},{5,9},{9,13},{14,2},{2,6},{... | collective-permute-start | bytes 1572872 | tf_op jit(solution)/shard_map/out_hop2_1/ppermute | solution.py:66
  168.6 23.7 %collective-permute-start.19 = (bf16[512,512]{1,0:T(8,128)(2,1)}, bf16[512,512]{1,0:T(8,128)(2,1)}, u32[]{:S(2)}, u32[]{:S(2)}) collective-permute-start(bf16[512,512]{1,0:T(8,128)(2,1)} %get-tuple-element.36), channel_id=1, source_target_pairs={{0,1},{1,0},{2,3},{3,2},{4,5},{5,4},{6,7},{7,6},{8,9},{9,8},{10,11... | collective-permute-start | bytes 1572872 | tf_op jit(solution)/shard_map/core_kept_0/ppermute | solution.py:76
  172.7 29.9 %collective-permute-start.21 = (bf16[512,512]{1,0:T(8,128)(2,1)}, bf16[512,512]{1,0:T(8,128)(2,1)}, u32[]{:S(2)}, u32[]{:S(2)}) collective-permute-start(bf16[512,512]{1,0:T(8,128)(2,1)} %add_convert_fusion.3), channel_id=1, source_target_pairs={{0,2},{1,3},{2,0},{3,1},{4,6},{5,7},{6,4},{7,5},{8,10},{9,11},{10,... | collective-permute-start | bytes 1572872 | tf_op jit(solution)/shard_map/z_sum_0/ppermute | solution.py:76
  190.5 16.1 %collective-permute-start.27 = (bf16[512,512]{1,0:T(8,128)(2,1)}, bf16[512,512]{1,0:T(8,128)(2,1)S(1)}, u32[]{:S(2)}, u32[]{:S(2)}) collective-permute-start(bf16[512,512]{1,0:T(8,128)(2,1)} %get-tuple-element.46), channel_id=1, source_target_pairs={{0,1},{1,0},{2,3},{3,2},{4,5},{5,4},{6,7},{7,6},{8,9},{9,8},{10,11... | collective-permute-start | bytes 1572872 | tf_op jit(solution)/shard_map/core_passed_1/ppermute | solution.py:76
  206.8 25.0 %collective-permute-start.28 = (bf16[512,512]{1,0:T(8,128)(2,1)S(1)}, bf16[512,512]{1,0:T(8,128)(2,1)S(1)}, u32[]{:S(2)}, u32[]{:S(2)}) collective-permute-start(bf16[512,512]{1,0:T(8,128)(2,1)S(1)} %add_convert_fusion.1), channel_id=1, source_target_pairs={{0,2},{1,3},{2,0},{3,1},{4,6},{5,7},{6,4},{7,5},{8,10},{9,11},{10,... | collective-permute-start | bytes 1572872 | tf_op jit(solution)/shard_map/z_sum_1/ppermute | solution.py:76
  (38 other events, 303.3 us)

commit v5 on v4

--- a/solution.py
+++ b/solution.py
@@ -13,7 +13,7 @@
 rope_base = 500000.0
 BF = jnp.bfloat16
 F32 = jnp.float32
-STRIPS = (1, 1)
+STRIPS = (5, 3)
 SHORT = 10**10
 LONG = 4 * 10**10
 
@@ -301,19 +301,21 @@
     with jax.named_scope("z_in"):
         up, down = from_z(both, 2), from_z(both, -2)
         up = hold(up, down, flops=SHORT)
-    q_ahead, q_behind, kv_ahead, kv_behind, up, down, out_own[0] = lax.optimization_barrier(
-        (q_ahead, q_behind, kv_ahead, kv_behind, up, down, out_own[0])
+    stashed = jnp.where(near_high, up[:rows], down[:rows])
+    fetched = jnp.where(near_high, up[rows:], down[rows:])
+    fetched_far = jnp.where(near_high, down[rows:], up[rows:])
+    q_low, q_high = q_ahead[:depth], q_behind[depth:]
+    far_up, far_down = up[:half], down[half:rows]
+    q_low, q_high, far_up, far_down, kv_ahead, kv_behind, fetched, fetched_far, out_own[0] = lax.optimization_barrier(
+        (q_low, q_high, far_up, far_down, kv_ahead, kv_behind, fetched, fetched_far, out_own[0])
     )
 
     with jax.named_scope("q_hop2"):
-        across_low, across_high = second_hop(q_ahead, q_behind)
+        across_low, across_high = from_x(q_low, 1), from_x(q_high, -1)
     with jax.named_scope("kv_hop2"):
         kv_near, kv_back = second_hop(kv_ahead, kv_behind)
     with jax.named_scope("far"):
-        mine_far = jnp.concatenate((from_z(up[:half], 2), from_z(down[half:rows], -2)), axis=0)
-    stashed = jnp.where(near_high, up[:rows], down[:rows])
-    fetched = jnp.where(near_high, up[rows:], down[rows:])
-    fetched_far = jnp.where(near_high, down[rows:], up[rows:])
+        mine_far = jnp.concatenate((from_z(far_up, 2), from_z(far_down, -2)), axis=0)
     with jax.named_scope("sib"):
         sib = from_tensor(jnp.concatenate((mine, fetched, fetched_far, mine_far), axis=0), 1)
     blocks = (
@@ -369,13 +371,10 @@
     for index, (low, high) in enumerate(strips):
         ahead, behind = out_hops[index]
         with jax.named_scope("out_hop2_%d" % index):
-            ahead_part, behind_part = ahead[: width // 2], behind[width // 2 :]
-            near, back = from_x(ahead_part, 1), from_x(behind_part, -1)
-        if index:
-            near = hold(near, back, flops=10000000000)
+            near, back = second_hop(ahead, behind)
         if index + 1 < len(strips):
             with jax.named_scope("out_hop1_%d" % (index + 1)):
-                out_hops.append(first_hop(after(out_own[index + 1], ahead_part, behind_part)))
+                out_hops.append(first_hop(after(out_own[index + 1], near, back)))
         sent_kept, sent_passed, kept, passed = spread(
             term_order,
             after(mixed, *passed_before),
@@ -383,8 +382,7 @@
             "spread_%d" % index,
         )
         if index:
-            outputs[-1] = hold(outputs[-1], flops=5000000000)
-            sent_kept = after(sent_kept, outputs[-1])
+            sent_passed = after(sent_passed, outputs[-1])
         with jax.named_scope("core_passed_%d" % index):
             passed = (passed + from_tensor(sent_passed, 1).astype(F32)).astype(BF)
         with jax.named_scope("z_sum_%d" % index):

time: 237 us -> 228 us (0.962); the launches traced: 233 us -> 227 us
  waiting for transfers between devices: 91.8 us -> 112 us
  starting transfers between devices: 61.3 us -> 41.1 us
  other arithmetic: 16.6 us -> 11.8 us
    ppermute x16, waiting for transfers between devices: 48.7 us -> 75.6 us  [from_x(): lax.ppermute(block, 'ctx', [((c + step) % count, c) for c in range(count)])]
    ppermute x7, starting transfers between devices: 28.7 us -> 10.4 us  [from_tensor(): return lax.ppermute(block, 'tensor', [(t, t ^ flip) for t in range(count)])]
    ppermute x7, waiting for transfers between devices: 29.9 us -> 24.1 us  [from_tensor(): return lax.ppermute(block, 'tensor', [(t, t ^ flip) for t in range(count)])]
    unnamed x3 -> x1, other arithmetic: 5.13 us -> 0.05 us
    ppermute x4, starting transfers between devices: 10.4 us -> 7.64 us  [from_z(): return lax.ppermute(block, ('section', 'tensor'), route)]
    broadcast_in_dim x1 -> x2, other arithmetic: 1.09 us -> 3.55 us  [body(): return (result[:rows][None], stashed[None], result[rows:][None])]
    slice x4 -> x6, local copies, waits for them, and re-layouts: 4.35 us -> 6.03 us  [second_hop(): return (from_x(ahead[:half], 1), from_x(behind[half:], -1))]
    slice x6 -> x4, local copies, waits for them, and re-layouts: 7.82 us -> 6.16 us  [the longest x2 3.37 us: body(): q_low, q_high = (q_ahead[:depth], q_behind[depth:])]
  transfers between devices with their start and end apart: 29 -> 29, of which waited for: 14 -> 15; matrix products, arithmetic and copies ran while one was open for 14% -> 14% of each run, Pallas kernels for 15% -> 12%
where the time goes in v5:
time: 228 us; the launch traced here: 227 us
  waiting for transfers between devices  112 us (49%)
  starting transfers between devices  41.1 us (18%)
  Pallas kernels  32.9 us (14%)
  local copies, waits for them, and re-layouts  28.9 us (13%)
  other arithmetic  11.8 us (5%)
    ppermute x16, waiting for transfers between devices, from_x(): lax.ppermute(block, 'ctx', [((c + step) % count, c) for c in range(count)])  75.6 us
    ppermute x7, waiting for transfers between devices, from_tensor(): return lax.ppermute(block, 'tensor', [(t, t ^ flip) for t in range(count)])  24.1 us
    ppermute x16, starting transfers between devices, from_x(): lax.ppermute(block, 'ctx', [((c + step) % count, c) for c in range(count)])  15.3 us
    ppermute x4, waiting for transfers between devices, from_z(): return lax.ppermute(block, ('section', 'tensor'), route)  12 us
    pallas_call x2, Pallas kernels, project(): pl.pallas_call(functools.partial(project_kernel, pieces=[(step, low) for...  11.8 us
    ppermute x7, starting transfers between devices, from_tensor(): return lax.ppermute(block, 'tensor', [(t, t ^ flip) for t in range(count)])  10.4 us
    pallas_call x1, Pallas kernels, attend(): pl.pallas_call(attend_kernel, grid=(batches, queries.shape[1] // wide), i...  10.3 us
    unnamed x52, local copies, waits for them, and re-layouts  9.79 us
  transfers between devices with their start and end apart: 29, of which 15 were waited for; matrix products, arithmetic and copies ran while one was open for 14% of the time, Pallas kernels for 12%

profile of v5, /device:TPU:49, one launch (start us, length us, event | category | flops | bytes accessed | tf_op | source)
XLA Modules:
  0.0 227.5 jit_solution(16202565419314933739)
XLA Ops:
  0.6 2.6 %collective-permute-start = (bf16[1024,1024]{1,0:T(8,128)(2,1)}, bf16[1024,1024]{1,0:T(8,128)(2,1)S(1)}, u32[]{:S(2)}, u32[]{:S(2)}) collective-permute-start(bf16[1024,1024]{1,0:T(8,128)(2,1)} %bitcast.26), channel_id=1, source_target_pairs={{4,0},{8,4},{12,8},{0,12},{5,1},{9,5},{13,9},{1,13},{6,2},{10,6},{... | collective-permute-start | bytes 6291464 | tf_op jit(solution)/shard_map/q_hop1/ppermute | solution.py:66
  4.5 5.2 %collective-permute-start.2 = (bf16[512,1024]{1,0:T(8,128)(2,1)S(1)}, bf16[512,1024]{1,0:T(8,128)(2,1)}, u32[]{:S(2)}, u32[]{:S(2)}) collective-permute-start(bf16[512,1024]{1,0:T(8,128)(2,1)S(1)} %pad_maximum_fusion), channel_id=1, source_target_pairs={{128,0},{129,1},{144,16},{145,17},{160,32},{161,33},{176,48},{177,... | collective-permute-start | bytes 3145736 | tf_op jit(solution)/shard_map/z_in/ppermute | solution.py:61
  9.7 2.5 %slice.90.refs_0_ = bf16[1024,640]{1,0:T(8,128)(2,1)} slice(bf16[1024,1024]{1,0:T(8,128)(2,1)} %bitcast.30), slice={[0:1024], [0:640]} | slice | bytes 2621440 | tf_op jit(solution)/shard_map/slice | solution.py:291
  14.1 33.7 %collective-permute-done.refs_1_ = bf16[1024,1024]{1,0:T(8,128)(2,1)S(1)} collective-permute-done((bf16[1024,1024]{1,0:T(8,128)(2,1)}, bf16[1024,1024]{1,0:T(8,128)(2,1)S(1)}, u32[]{:S(2)}, u32[]{:S(2)}) %collective-permute-start) | collective-permute-done | bytes 2097184 | tf_op jit(solution)/shard_map/q_hop1/ppermute | solution.py:66
  47.8 3.1 %collective-permute-done.1.refs_2_ = bf16[1024,1024]{1,0:T(8,128)(2,1)} collective-permute-done((bf16[1024,1024]{1,0:T(8,128)(2,1)}, bf16[1024,1024]{1,0:T(8,128)(2,1)}, u32[]{:S(2)}, u32[]{:S(2)}) %collective-permute-start.1) | collective-permute-done | bytes 2097184 | tf_op jit(solution)/shard_map/q_hop1/ppermute | solution.py:66
  53.1 5.5 %collective-permute-done.3.refs_1_ = bf16[512,1024]{1,0:T(8,128)(2,1)} collective-permute-done((bf16[512,1024]{1,0:T(8,128)(2,1)S(1)}, bf16[512,1024]{1,0:T(8,128)(2,1)}, u32[]{:S(2)}, u32[]{:S(2)}) %collective-permute-start.3) | collective-permute-done | bytes 1048608 | tf_op jit(solution)/shard_map/z_in/ppermute | solution.py:61
  61.4 2.4 %fusion.4 = (bf16[1,256,1024]{2,1,0:T(8,128)(2,1)}, bf16[256,1024]{1,0:T(8,128)(2,1)S(1)}, bf16[256,1024]{1,0:T(8,128)(2,1)S(1)}) fusion(bf16[512,1024]{1,0:T(8,128)(2,1)} %collective-permute-done.3.refs_1_, bf16[512,1024]{1,0:T(8,128)(2,1)} %hold.3, pred[]{:T(512)S(6)} %lt.28), kind=kLoop, calls=%fused_computation.16 | loop fusion | flops 786432 | bytes 3670017 | tf_op jit(solution)/shard_map/broadcast_in_dim | solution.py:396
  67.3 2.4 %collective-permute-start.11 = (bf16[512,1024]{1,0:T(8,128)(2,1)}, bf16[512,1024]{1,0:T(8,128)(2,1)}, u32[]{:S(2)}, u32[]{:S(2)}) collective-permute-start(bf16[512,1024]{1,0:T(8,128)(2,1)} %slice.84), channel_id=1, source_target_pairs={{4,0},{8,4},{12,8},{0,12},{5,1},{9,5},{13,9},{1,13},{6,2},{10,6},{... | collective-permute-start | bytes 3145736 | tf_op jit(solution)/shard_map/q_hop2/ppermute | solution.py:66
  74.7 2.7 %collective-permute-start.9 = (bf16[512,256]{1,0:T(8,128)(2,1)S(1)}, bf16[512,256]{1,0:T(8,128)(2,1)S(1)}, u32[]{:S(2)}, u32[]{:S(2)}) collective-permute-start(bf16[512,256]{1,0:T(8,128)(2,1)S(1)} %slice.70), channel_id=1, source_target_pairs={{4,0},{8,4},{12,8},{0,12},{5,1},{9,5},{13,9},{1,13},{6,2},{10,6},{... | collective-permute-start | bytes 786440 | tf_op jit(solution)/shard_map/kv_hop2/ppermute | solution.py:66
  82.4 4.1 %collective-permute-done.7 = bf16[128,1024]{1,0:T(8,128)(2,1)S(1)} collective-permute-done((bf16[128,1024]{1,0:T(8,128)(2,1)S(1)}, bf16[128,1024]{1,0:T(8,128)(2,1)S(1)}, u32[]{:S(2)}, u32[]{:S(2)}) %collective-permute-start.7) | collective-permute-done | bytes 262176 | tf_op jit(solution)/shard_map/far/ppermute | solution.py:61
  90.1 6.6 %collective-permute-done.9.refs_2_.refs_3_ = bf16[512,256]{1,0:T(8,128)(2,1)S(1)} collective-permute-done((bf16[512,256]{1,0:T(8,128)(2,1)S(1)}, bf16[512,256]{1,0:T(8,128)(2,1)S(1)}, u32[]{:S(2)}, u32[]{:S(2)}) %collective-permute-start.9) | collective-permute-done | bytes 262176 | tf_op jit(solution)/shard_map/kv_hop2/ppermute | solution.py:66
  96.7 3.1 %collective-permute-done.10.refs_3_.refs_4_ = bf16[512,256]{1,0:T(8,128)(2,1)} collective-permute-done((bf16[512,256]{1,0:T(8,128)(2,1)S(1)}, bf16[512,256]{1,0:T(8,128)(2,1)}, u32[]{:S(2)}, u32[]{:S(2)}) %collective-permute-start.10) | collective-permute-done | bytes 262176 | tf_op jit(solution)/shard_map/kv_hop2/ppermute | solution.py:66
  105.5 4.2 %project_kv.1 = bf16[512,256]{1,0:T(8,128)(2,1)S(1)} custom-call(s32[4]{0:T(128)S(1)} %fusion.6.index_ref, bf16[4,512,1024]{2,1,0:T(8,128)(2,1)S(1)} %bitcast.20, bf16[1024,256]{1,0:T(8,128)(2,1)} %pad_maximum_fusion.2.refs_0_, bf16[1024,256]{1,0:T(8,128)(2,1)} %collective-permute-done.4.refs_1_, bf16[512,256]{1,0:T(8,128)(2,1)S(1)} %copy-done.17, ...), custom_call_target="tpu_custom_call" | custom-call | flops 1024 | bytes 1024 | tf_op jit(solution)/shard_map/project_kv/pallas_call | solution.py:152
  110.4 3.1 %collective-permute-start.13 = (bf16[2,272,256]{2,1,0:T(8,128)(2,1)}, bf16[2,272,256]{2,1,0:T(8,128)(2,1)}, u32[]{:S(2)}, u32[]{:S(2)}) collective-permute-start(bf16[2,272,256]{2,1,0:T(8,128)(2,1)} %pad_maximum_fusion.5.own_ref), channel_id=1, source_target_pairs={{0,8},{4,12},{1,9},{5,13},{2,10},{6,14},{3,11},{7,15},{16,24},{20,... | collective-permute-start | bytes 835592 | tf_op jit(solution)/shard_map/kv_rows/ppermute | solution.py:71
  113.5 4.7 %collective-permute-start.14 = (bf16[2,272,256]{2,1,0:T(8,128)(2,1)}, bf16[2,272,256]{2,1,0:T(8,128)(2,1)}, u32[]{:S(2)}, u32[]{:S(2)}) collective-permute-start(bf16[2,272,256]{2,1,0:T(8,128)(2,1)} %pad_maximum_fusion.5.own_ref), channel_id=1, source_target_pairs={{0,4},{4,8},{8,12},{1,5},{5,9},{9,13},{2,6},{6,10},{10,14},{3,7},{... | collective-permute-start | bytes 835592 | tf_op jit(solution)/shard_map/kv_rows/ppermute | solution.py:71
  127.7 7.6 %project_q.1.refs_2_.query_ref = bf16[512,1024]{1,0:T(8,128)(2,1)S(1)} custom-call(s32[4]{0:T(128)S(1)} %fusion.6.index_ref, bf16[4,512,1024]{2,1,0:T(8,128)(2,1)S(1)} %bitcast.21, bf16[1024,1024]{1,0:T(8,128)(2,1)S(1)} %bitcast.28, bf16[1024,1024]{1,0:T(8,128)(2,1)S(1)} %copy-done.8, bf16[1024,1024]{1,0:T(8,128)(2,1)} %collective-permute-done.1.refs_2_, ...), custom_call_target="tpu_custom_call" | custom-call | flops 1024 | bytes 1024 | tf_op jit(solution)/shard_map/project_q/pallas_call | solution.py:152
  141.8 10.3 %attend.1.mixed_ref = bf16[512,1024]{1,0:T(8,128)(2,1)S(1)} custom-call(s32[1]{0:T(128)} %bitcast.6.place_ref, bf16[512,1024]{1,0:T(8,128)(2,1)S(1)} %copy-done.10, f32[2,256,1]{2,1,0:T(8,128)S(1)} %copy-done.15, bf16[2,272,256]{2,1,0:T(8,128)(2,1)} %collective-permute-done.13.refs_1_.two_ref, bf16[2,272,256]{2,1,0:T(8,128)(2,1)} %hold.4.one_ref, ...), custom_call_target="tpu_custom_call" | custom-call | flops 1024 | bytes 1024 | tf_op jit(solution)/shard_map/attend/pallas_call | solution.py:208
  154.6 5.6 %spread_0.1 = (bf16[512,640]{1,0:T(8,128)(2,1)S(1)}, bf16[512,640]{1,0:T(8,128)(2,1)S(1)}, f32[512,640]{1,0:T(8,128)S(1)}, f32[512,640]{1,0:T(8,128)S(1)}) custom-call(s32[4]{0:T(128)S(1)} %and_select_fusion.1.index_ref, bf16[512,1024]{1,0:T(8,128)(2,1)S(1)} %attend.1.mixed_ref, bf16[1024,640]{1,0:T(8,128)(2,1)S(1)} %copy-done.3, ...), custom_call_target="tpu_custom_call" | custom-call | flops 1024 | bytes 1024 | tf_op jit(solution)/shard_map/spread_0/pallas_call | solution.py:247
  160.3 4.5 %collective-permute-start.20 = (bf16[512,640]{1,0:T(8,128)(2,1)S(1)}, bf16[512,640]{1,0:T(8,128)(2,1)S(1)}, u32[]{:S(2)}, u32[]{:S(2)}) collective-permute-start(bf16[512,640]{1,0:T(8,128)(2,1)S(1)} %get-tuple-element.42), channel_id=1, source_target_pairs={{0,1},{1,0},{2,3},{3,2},{4,5},{5,4},{6,7},{7,6},{8,9},{9,8},{10,11... | collective-permute-start | bytes 1966088 | tf_op jit(solution)/shard_map/core_passed_0/ppermute | solution.py:76
  168.0 15.8 %collective-permute-done.22.ahead_ref = bf16[1024,384]{1,0:T(8,128)(2,1)S(1)} collective-permute-done((bf16[1024,384]{1,0:T(8,128)(2,1)S(1)}, bf16[1024,384]{1,0:T(8,128)(2,1)S(1)}, u32[]{:S(2)}, u32[]{:S(2)}) %collective-permute-start.22) | collective-permute-done | bytes 786464 | tf_op jit(solution)/shard_map/out_hop1_1/ppermute | solution.py:66
  185.6 8.2 %collective-permute-done.23.near_ref = bf16[512,384]{1,0:T(8,128)(2,1)S(1)} collective-permute-done((bf16[512,384]{1,0:T(8,128)(2,1)S(1)}, bf16[512,384]{1,0:T(8,128)(2,1)S(1)}, u32[]{:S(2)}, u32[]{:S(2)}) %collective-permute-start.23) | collective-permute-done | bytes 393248 | tf_op jit(solution)/shard_map/out_hop2_1/ppermute | solution.py:66
  193.7 2.6 %collective-permute-done.25.back_ref = bf16[512,384]{1,0:T(8,128)(2,1)S(1)} collective-permute-done((bf16[512,384]{1,0:T(8,128)(2,1)S(1)}, bf16[512,384]{1,0:T(8,128)(2,1)S(1)}, u32[]{:S(2)}, u32[]{:S(2)}) %collective-permute-start.25) | collective-permute-done | bytes 393248 | tf_op jit(solution)/shard_map/out_hop2_1/ppermute | solution.py:66
  196.4 3.1 %spread_1.1 = (bf16[512,384]{1,0:T(8,128)(2,1)S(1)}, bf16[512,384]{1,0:T(8,128)(2,1)S(1)}, f32[512,384]{1,0:T(8,128)S(1)}, f32[512,384]{1,0:T(8,128)S(1)}) custom-call(s32[4]{0:T(128)S(1)} %and_select_fusion.1.index_ref, bf16[512,1024]{1,0:T(8,128)(2,1)S(1)} %attend.1.mixed_ref, bf16[1024,384]{1,0:T(8,128)(2,1)S(1)} %copy-done.11, ...), custom_call_target="tpu_custom_call" | custom-call | flops 1024 | bytes 1024 | tf_op jit(solution)/shard_map/spread_1/pallas_call | solution.py:247
  205.1 21.1 %collective-permute-done.28 = bf16[512,384]{1,0:T(8,128)(2,1)S(1)} collective-permute-done((bf16[512,384]{1,0:T(8,128)(2,1)S(1)}, bf16[512,384]{1,0:T(8,128)(2,1)S(1)}, u32[]{:S(2)}, u32[]{:S(2)}) %collective-permute-start.28) | collective-permute-done | bytes 393248 | tf_op jit(solution)/shard_map/z_sum_1/ppermute | solution.py:76
  (138 shorter events, 61.5 us)
Async XLA Ops:
  0.6 47.2 %collective-permute-start = (bf16[1024,1024]{1,0:T(8,128)(2,1)}, bf16[1024,1024]{1,0:T(8,128)(2,1)S(1)}, u32[]{:S(2)}, u32[]{:S(2)}) collective-permute-start(bf16[1024,1024]{1,0:T(8,128)(2,1)} %bitcast.26), channel_id=1, source_target_pairs={{4,0},{8,4},{12,8},{0,12},{5,1},{9,5},{13,9},{1,13},{6,2},{10,6},{... | collective-permute-start | bytes 6291464 | tf_op jit(solution)/shard_map/q_hop1/ppermute | solution.py:66
  3.2 47.7 %collective-permute-start.1 = (bf16[1024,1024]{1,0:T(8,128)(2,1)}, bf16[1024,1024]{1,0:T(8,128)(2,1)}, u32[]{:S(2)}, u32[]{:S(2)}) collective-permute-start(bf16[1024,1024]{1,0:T(8,128)(2,1)} %bitcast.27), channel_id=1, source_target_pairs={{12,0},{0,4},{4,8},{8,12},{13,1},{1,5},{5,9},{9,13},{14,2},{2,6},{... | collective-permute-start | bytes 6291464 | tf_op jit(solution)/shard_map/q_hop1/ppermute | solution.py:66
  4.5 48.6 %collective-permute-start.2 = (bf16[512,1024]{1,0:T(8,128)(2,1)S(1)}, bf16[512,1024]{1,0:T(8,128)(2,1)}, u32[]{:S(2)}, u32[]{:S(2)}) collective-permute-start(bf16[512,1024]{1,0:T(8,128)(2,1)S(1)} %pad_maximum_fusion), channel_id=1, source_target_pairs={{128,0},{129,1},{144,16},{145,17},{160,32},{161,33},{176,48},{177,... | collective-permute-start | bytes 3145736 | tf_op jit(solution)/shard_map/z_in/ppermute | solution.py:61
  9.7 48.9 %collective-permute-start.3 = (bf16[512,1024]{1,0:T(8,128)(2,1)S(1)}, bf16[512,1024]{1,0:T(8,128)(2,1)}, u32[]{:S(2)}, u32[]{:S(2)}) collective-permute-start(bf16[512,1024]{1,0:T(8,128)(2,1)S(1)} %pad_maximum_fusion), channel_id=1, source_target_pairs={{130,0},{131,1},{146,16},{147,17},{162,32},{163,33},{178,48},{179,... | collective-permute-start | bytes 3145736 | tf_op jit(solution)/shard_map/z_in/ppermute | solution.py:61
  50.9 16.4 %collective-permute-start.4 = (bf16[1024,256]{1,0:T(8,128)(2,1)}, bf16[1024,256]{1,0:T(8,128)(2,1)}, u32[]{:S(2)}, u32[]{:S(2)}) collective-permute-start(bf16[1024,256]{1,0:T(8,128)(2,1)} %pad_maximum_fusion.2.refs_0_), channel_id=1, source_target_pairs={{4,0},{8,4},{12,8},{0,12},{5,1},{9,5},{13,9},{1,13},{6,2},{10,6},{... | collective-permute-start | bytes 1572872 | tf_op jit(solution)/shard_map/kv_hop1/ppermute | solution.py:66
  51.2 16.0 %collective-permute-start.5 = (bf16[1024,256]{1,0:T(8,128)(2,1)}, bf16[1024,256]{1,0:T(8,128)(2,1)}, u32[]{:S(2)}, u32[]{:S(2)}) collective-permute-start(bf16[1024,256]{1,0:T(8,128)(2,1)} %pad_maximum_fusion.2.refs_0_), channel_id=1, source_target_pairs={{12,0},{0,4},{4,8},{8,12},{13,1},{1,5},{5,9},{9,13},{14,2},{2,6},{... | collective-permute-start | bytes 1572872 | tf_op jit(solution)/shard_map/kv_hop1/ppermute | solution.py:66
  67.3 32.5 %collective-permute-start.11 = (bf16[512,1024]{1,0:T(8,128)(2,1)}, bf16[512,1024]{1,0:T(8,128)(2,1)}, u32[]{:S(2)}, u32[]{:S(2)}) collective-permute-start(bf16[512,1024]{1,0:T(8,128)(2,1)} %slice.84), channel_id=1, source_target_pairs={{4,0},{8,4},{12,8},{0,12},{5,1},{9,5},{13,9},{1,13},{6,2},{10,6},{... | collective-permute-start | bytes 3145736 | tf_op jit(solution)/shard_map/q_hop2/ppermute | solution.py:66
  69.7 30.1 %collective-permute-start.12 = (bf16[512,1024]{1,0:T(8,128)(2,1)}, bf16[512,1024]{1,0:T(8,128)(2,1)}, u32[]{:S(2)}, u32[]{:S(2)}) collective-permute-start(bf16[512,1024]{1,0:T(8,128)(2,1)} %slice.85), channel_id=1, source_target_pairs={{12,0},{0,4},{4,8},{8,12},{13,1},{1,5},{5,9},{9,13},{14,2},{2,6},{... | collective-permute-start | bytes 3145736 | tf_op jit(solution)/shard_map/q_hop2/ppermute | solution.py:66
  72.6 13.9 %collective-permute-start.7 = (bf16[128,1024]{1,0:T(8,128)(2,1)S(1)}, bf16[128,1024]{1,0:T(8,128)(2,1)S(1)}, u32[]{:S(2)}, u32[]{:S(2)}) collective-permute-start(bf16[128,1024]{1,0:T(8,128)(2,1)S(1)} %slice.87), channel_id=1, source_target_pairs={{130,0},{131,1},{146,16},{147,17},{162,32},{163,33},{178,48},{179,... | collective-permute-start | bytes 786440 | tf_op jit(solution)/shard_map/far/ppermute | solution.py:61
  74.7 22.0 %collective-permute-start.9 = (bf16[512,256]{1,0:T(8,128)(2,1)S(1)}, bf16[512,256]{1,0:T(8,128)(2,1)S(1)}, u32[]{:S(2)}, u32[]{:S(2)}) collective-permute-start(bf16[512,256]{1,0:T(8,128)(2,1)S(1)} %slice.70), channel_id=1, source_target_pairs={{4,0},{8,4},{12,8},{0,12},{5,1},{9,5},{13,9},{1,13},{6,2},{10,6},{... | collective-permute-start | bytes 786440 | tf_op jit(solution)/shard_map/kv_hop2/ppermute | solution.py:66
  80.8 19.0 %collective-permute-start.10 = (bf16[512,256]{1,0:T(8,128)(2,1)S(1)}, bf16[512,256]{1,0:T(8,128)(2,1)}, u32[]{:S(2)}, u32[]{:S(2)}) collective-permute-start(bf16[512,256]{1,0:T(8,128)(2,1)S(1)} %slice.71), channel_id=1, source_target_pairs={{12,0},{0,4},{4,8},{8,12},{13,1},{1,5},{5,9},{9,13},{14,2},{2,6},{... | collective-permute-start | bytes 786440 | tf_op jit(solution)/shard_map/kv_hop2/ppermute | solution.py:66
  88.0 15.4 %collective-permute-start.8 = (bf16[1024,1024]{1,0:T(8,128)(2,1)}, bf16[1024,1024]{1,0:T(8,128)(2,1)S(1)}, u32[]{:S(2)}, u32[]{:S(2)}) collective-permute-start(bf16[1024,1024]{1,0:T(8,128)(2,1)} %constant_dynamic-update-slice_fusion), channel_id=1, source_target_pairs={{0,1},{1,0},{2,3},{3,2},{4,5},{5,4},{6,7},{7,6},{8,9},{9,8},{10,11... | collective-permute-start | bytes 6291464 | tf_op jit(solution)/shard_map/sib/ppermute | solution.py:76
  99.8 36.5 %collective-permute-start.15 = (bf16[1024,640]{1,0:T(8,128)(2,1)}, bf16[1024,640]{1,0:T(8,128)(2,1)}, u32[]{:S(2)}, u32[]{:S(2)}) collective-permute-start(bf16[1024,640]{1,0:T(8,128)(2,1)} %hold.5.own_ref), channel_id=1, source_target_pairs={{4,0},{8,4},{12,8},{0,12},{5,1},{9,5},{13,9},{1,13},{6,2},{10,6},{... | collective-permute-start | bytes 3932168 | tf_op jit(solution)/shard_map/out_hop1_0/ppermute | solution.py:66
  100.7 37.6 %collective-permute-start.17 = (bf16[1024,640]{1,0:T(8,128)(2,1)}, bf16[1024,640]{1,0:T(8,128)(2,1)}, u32[]{:S(2)}, u32[]{:S(2)}) collective-permute-start(bf16[1024,640]{1,0:T(8,128)(2,1)} %hold.5.own_ref), channel_id=1, source_target_pairs={{12,0},{0,4},{4,8},{8,12},{13,1},{1,5},{5,9},{9,13},{14,2},{2,6},{... | collective-permute-start | bytes 3932168 | tf_op jit(solution)/shard_map/out_hop1_0/ppermute | solution.py:66
  110.4 31.4 %collective-permute-start.13 = (bf16[2,272,256]{2,1,0:T(8,128)(2,1)}, bf16[2,272,256]{2,1,0:T(8,128)(2,1)}, u32[]{:S(2)}, u32[]{:S(2)}) collective-permute-start(bf16[2,272,256]{2,1,0:T(8,128)(2,1)} %pad_maximum_fusion.5.own_ref), channel_id=1, source_target_pairs={{0,8},{4,12},{1,9},{5,13},{2,10},{6,14},{3,11},{7,15},{16,24},{20,... | collective-permute-start | bytes 835592 | tf_op jit(solution)/shard_map/kv_rows/ppermute | solution.py:71
  113.5 28.3 %collective-permute-start.14 = (bf16[2,272,256]{2,1,0:T(8,128)(2,1)}, bf16[2,272,256]{2,1,0:T(8,128)(2,1)}, u32[]{:S(2)}, u32[]{:S(2)}) collective-permute-start(bf16[2,272,256]{2,1,0:T(8,128)(2,1)} %pad_maximum_fusion.5.own_ref), channel_id=1, source_target_pairs={{0,4},{4,8},{8,12},{1,5},{5,9},{9,13},{2,6},{6,10},{10,14},{3,7},{... | collective-permute-start | bytes 835592 | tf_op jit(solution)/shard_map/kv_rows/ppermute | solution.py:71
  138.3 13.9 %collective-permute-start.16 = (bf16[512,640]{1,0:T(8,128)(2,1)}, bf16[512,640]{1,0:T(8,128)(2,1)S(1)}, u32[]{:S(2)}, u32[]{:S(2)}) collective-permute-start(bf16[512,640]{1,0:T(8,128)(2,1)} %slice.94), channel_id=1, source_target_pairs={{4,0},{8,4},{12,8},{0,12},{5,1},{9,5},{13,9},{1,13},{6,2},{10,6},{... | collective-permute-start | bytes 1966088 | tf_op jit(solution)/shard_map/out_hop2_0/ppermute | solution.py:66
  140.3 14.3 %collective-permute-start.18 = (bf16[512,640]{1,0:T(8,128)(2,1)}, bf16[512,640]{1,0:T(8,128)(2,1)}, u32[]{:S(2)}, u32[]{:S(2)}) collective-permute-start(bf16[512,640]{1,0:T(8,128)(2,1)} %slice.95), channel_id=1, source_target_pairs={{12,0},{0,4},{4,8},{8,12},{13,1},{1,5},{5,9},{9,13},{14,2},{2,6},{... | collective-permute-start | bytes 1966088 | tf_op jit(solution)/shard_map/out_hop2_0/ppermute | solution.py:66
  164.7 19.1 %collective-permute-start.22 = (bf16[1024,384]{1,0:T(8,128)(2,1)S(1)}, bf16[1024,384]{1,0:T(8,128)(2,1)S(1)}, u32[]{:S(2)}, u32[]{:S(2)}) collective-permute-start(bf16[1024,384]{1,0:T(8,128)(2,1)S(1)} %copy-done.11), channel_id=1, source_target_pairs={{4,0},{8,4},{12,8},{0,12},{5,1},{9,5},{13,9},{1,13},{6,2},{10,6},{... | collective-permute-start | bytes 2359304 | tf_op jit(solution)/shard_map/out_hop1_1/ppermute | solution.py:66
  164.7 20.6 %collective-permute-start.24 = (bf16[1024,384]{1,0:T(8,128)(2,1)S(1)}, bf16[1024,384]{1,0:T(8,128)(2,1)S(1)}, u32[]{:S(2)}, u32[]{:S(2)}) collective-permute-start(bf16[1024,384]{1,0:T(8,128)(2,1)S(1)} %copy-done.11), channel_id=1, source_target_pairs={{12,0},{0,4},{4,8},{8,12},{13,1},{1,5},{5,9},{9,13},{14,2},{2,6},{... | collective-permute-start | bytes 2359304 | tf_op jit(solution)/shard_map/out_hop1_1/ppermute | solution.py:66
  166.2 33.2 %collective-permute-start.19 = (bf16[512,640]{1,0:T(8,128)(2,1)S(1)}, bf16[512,640]{1,0:T(8,128)(2,1)S(1)}, u32[]{:S(2)}, u32[]{:S(2)}) collective-permute-start(bf16[512,640]{1,0:T(8,128)(2,1)S(1)} %get-tuple-element.40), channel_id=1, source_target_pairs={{0,1},{1,0},{2,3},{3,2},{4,5},{5,4},{6,7},{7,6},{8,9},{9,8},{10,11... | collective-permute-start | bytes 1966088 | tf_op jit(solution)/shard_map/core_kept_0/ppermute | solution.py:76
  167.0 34.2 %collective-permute-start.21 = (bf16[512,640]{1,0:T(8,128)(2,1)S(1)}, bf16[512,640]{1,0:T(8,128)(2,1)S(1)}, u32[]{:S(2)}, u32[]{:S(2)}) collective-permute-start(bf16[512,640]{1,0:T(8,128)(2,1)S(1)} %add_convert_fusion.1), channel_id=1, source_target_pairs={{0,2},{1,3},{2,0},{3,1},{4,6},{5,7},{6,4},{7,5},{8,10},{9,11},{10,... | collective-permute-start | bytes 1966088 | tf_op jit(solution)/shard_map/z_sum_0/ppermute | solution.py:76
  185.4 10.9 %collective-permute-start.25 = (bf16[512,384]{1,0:T(8,128)(2,1)S(1)}, bf16[512,384]{1,0:T(8,128)(2,1)S(1)}, u32[]{:S(2)}, u32[]{:S(2)}) collective-permute-start(bf16[512,384]{1,0:T(8,128)(2,1)S(1)} %slice.97), channel_id=1, source_target_pairs={{12,0},{0,4},{4,8},{8,12},{13,1},{1,5},{5,9},{9,13},{14,2},{2,6},{... | collective-permute-start | bytes 1179656 | tf_op jit(solution)/shard_map/out_hop2_1/ppermute | solution.py:66
  203.5 22.6 %collective-permute-start.28 = (bf16[512,384]{1,0:T(8,128)(2,1)S(1)}, bf16[512,384]{1,0:T(8,128)(2,1)S(1)}, u32[]{:S(2)}, u32[]{:S(2)}) collective-permute-start(bf16[512,384]{1,0:T(8,128)(2,1)S(1)} %add_convert_fusion.3), channel_id=1, source_target_pairs={{0,2},{1,3},{2,0},{3,1},{4,6},{5,7},{6,4},{7,5},{8,10},{9,11},{10,... | collective-permute-start | bytes 1179656 | tf_op jit(solution)/shard_map/z_sum_1/ppermute | solution.py:76
  (29 other events, 168.9 us)

commit v6 on v5

--- a/solution.py
+++ b/solution.py
@@ -301,14 +301,14 @@
     with jax.named_scope("z_in"):
         up, down = from_z(both, 2), from_z(both, -2)
         up = hold(up, down, flops=SHORT)
+    q_low, q_high = q_ahead[:depth], q_behind[depth:]
+    far_up, far_down = up[:half], down[half:rows]
+    q_low, q_high, far_up, far_down, kv_ahead, kv_behind, up, down, out_own[0] = lax.optimization_barrier(
+        (q_low, q_high, far_up, far_down, kv_ahead, kv_behind, up, down, out_own[0])
+    )
     stashed = jnp.where(near_high, up[:rows], down[:rows])
     fetched = jnp.where(near_high, up[rows:], down[rows:])
     fetched_far = jnp.where(near_high, down[rows:], up[rows:])
-    q_low, q_high = q_ahead[:depth], q_behind[depth:]
-    far_up, far_down = up[:half], down[half:rows]
-    q_low, q_high, far_up, far_down, kv_ahead, kv_behind, fetched, fetched_far, out_own[0] = lax.optimization_barrier(
-        (q_low, q_high, far_up, far_down, kv_ahead, kv_behind, fetched, fetched_far, out_own[0])
-    )
 
     with jax.named_scope("q_hop2"):
         across_low, across_high = from_x(q_low, 1), from_x(q_high, -1)

time: 228 us -> 226 us (level)
  waiting for transfers between devices: 112 us -> 108 us
  local copies, waits for them, and re-layouts: 28.9 us -> 26.3 us
    unnamed x1 -> x3, other arithmetic: 0.05 us -> 5.23 us
    ppermute x7, waiting for transfers between devices: 24.1 us -> 20.9 us  [from_tensor(): return lax.ppermute(block, 'tensor', [(t, t ^ flip) for t in range(count)])]
    broadcast_in_dim x2 -> x1, other arithmetic: 3.55 us -> 1.11 us  [body(): return (result[:rows][None], stashed[None], result[rows:][None])]
    unnamed x52 -> x54, local copies, waits for them, and re-layouts: 9.79 us -> 7.4 us
where the time goes in v6:
time: 226 us; the launch traced here: 225 us
  waiting for transfers between devices  108 us (48%)
  starting transfers between devices  42.5 us (19%)
  Pallas kernels  32.9 us (15%)
  local copies, waits for them, and re-layouts  26.3 us (12%)
  other arithmetic  13.8 us (6%)
    ppermute x16, waiting for transfers between devices, from_x(): lax.ppermute(block, 'ctx', [((c + step) % count, c) for c in range(count)])  76.4 us
    ppermute x7, waiting for transfers between devices, from_tensor(): return lax.ppermute(block, 'tensor', [(t, t ^ flip) for t in range(count)])  20.9 us
    ppermute x16, starting transfers between devices, from_x(): lax.ppermute(block, 'ctx', [((c + step) % count, c) for c in range(count)])  15.4 us
    pallas_call x2, Pallas kernels, project(): pl.pallas_call(functools.partial(project_kernel, pieces=[(step, low) for...  11.8 us
    ppermute x7, starting transfers between devices, from_tensor(): return lax.ppermute(block, 'tensor', [(t, t ^ flip) for t in range(count)])  11.7 us
    ppermute x4, waiting for transfers between devices, from_z(): return lax.ppermute(block, ('section', 'tensor'), route)  11 us
    pallas_call x1, Pallas kernels, attend(): pl.pallas_call(attend_kernel, grid=(batches, queries.shape[1] // wide), i...  10.3 us
    pallas_call x2, Pallas kernels, spread(): pl.pallas_call(spread_kernel, in_specs=[pl.BlockSpec(memory_space=pltpu.S...  8.73 us
  transfers between devices with their start and end apart: 29, of which 15 were waited for; matrix products, arithmetic and copies ran while one was open for 14% of the time, Pallas kernels for 12%

profile of v6, /device:TPU:49, one launch (start us, length us, event | category | flops | bytes accessed | tf_op | source)
XLA Modules:
  0.0 224.9 jit_solution(3959943039343089315)
XLA Ops:
  0.6 2.6 %collective-permute-start = (bf16[1024,1024]{1,0:T(8,128)(2,1)}, bf16[1024,1024]{1,0:T(8,128)(2,1)S(1)}, u32[]{:S(2)}, u32[]{:S(2)}) collective-permute-start(bf16[1024,1024]{1,0:T(8,128)(2,1)} %bitcast.26), channel_id=1, source_target_pairs={{4,0},{8,4},{12,8},{0,12},{5,1},{9,5},{13,9},{1,13},{6,2},{10,6},{... | collective-permute-start | bytes 6291464 | tf_op jit(solution)/shard_map/q_hop1/ppermute | solution.py:66
  5.5 5.1 %collective-permute-start.2 = (bf16[512,1024]{1,0:T(8,128)(2,1)}, bf16[512,1024]{1,0:T(8,128)(2,1)}, u32[]{:S(2)}, u32[]{:S(2)}) collective-permute-start(bf16[512,1024]{1,0:T(8,128)(2,1)} %pad_maximum_fusion), channel_id=1, source_target_pairs={{128,0},{129,1},{144,16},{145,17},{160,32},{161,33},{176,48},{177,... | collective-permute-start | bytes 3145736 | tf_op jit(solution)/shard_map/z_in/ppermute | solution.py:61
  10.6 2.5 %slice.88.refs_0_ = bf16[1024,640]{1,0:T(8,128)(2,1)} slice(bf16[1024,1024]{1,0:T(8,128)(2,1)} %bitcast.30), slice={[0:1024], [0:640]} | slice | bytes 2621440 | tf_op jit(solution)/shard_map/slice | solution.py:291
  13.3 34.5 %collective-permute-done.refs_1_ = bf16[1024,1024]{1,0:T(8,128)(2,1)S(1)} collective-permute-done((bf16[1024,1024]{1,0:T(8,128)(2,1)}, bf16[1024,1024]{1,0:T(8,128)(2,1)S(1)}, u32[]{:S(2)}, u32[]{:S(2)}) %collective-permute-start) | collective-permute-done | bytes 2097184 | tf_op jit(solution)/shard_map/q_hop1/ppermute | solution.py:66
  47.8 3.1 %collective-permute-done.1.refs_2_ = bf16[1024,1024]{1,0:T(8,128)(2,1)} collective-permute-done((bf16[1024,1024]{1,0:T(8,128)(2,1)}, bf16[1024,1024]{1,0:T(8,128)(2,1)}, u32[]{:S(2)}, u32[]{:S(2)}) %collective-permute-start.1) | collective-permute-done | bytes 2097184 | tf_op jit(solution)/shard_map/q_hop1/ppermute | solution.py:66
  54.4 5.5 %collective-permute-done.3.refs_1_ = bf16[512,1024]{1,0:T(8,128)(2,1)} collective-permute-done((bf16[512,1024]{1,0:T(8,128)(2,1)}, bf16[512,1024]{1,0:T(8,128)(2,1)}, u32[]{:S(2)}, u32[]{:S(2)}) %collective-permute-start.3) | collective-permute-done | bytes 1048608 | tf_op jit(solution)/shard_map/z_in/ppermute | solution.py:61
  65.9 2.6 %collective-permute-start.11 = (bf16[512,1024]{1,0:T(8,128)(2,1)}, bf16[512,1024]{1,0:T(8,128)(2,1)}, u32[]{:S(2)}, u32[]{:S(2)}) collective-permute-start(bf16[512,1024]{1,0:T(8,128)(2,1)} %slice.84), channel_id=1, source_target_pairs={{4,0},{8,4},{12,8},{0,12},{5,1},{9,5},{13,9},{1,13},{6,2},{10,6},{... | collective-permute-start | bytes 3145736 | tf_op jit(solution)/shard_map/q_hop2/ppermute | solution.py:66
  73.4 2.7 %collective-permute-start.9 = (bf16[512,256]{1,0:T(8,128)(2,1)S(1)}, bf16[512,256]{1,0:T(8,128)(2,1)S(1)}, u32[]{:S(2)}, u32[]{:S(2)}) collective-permute-start(bf16[512,256]{1,0:T(8,128)(2,1)S(1)} %slice.70), channel_id=1, source_target_pairs={{4,0},{8,4},{12,8},{0,12},{5,1},{9,5},{13,9},{1,13},{6,2},{10,6},{... | collective-permute-start | bytes 786440 | tf_op jit(solution)/shard_map/kv_hop2/ppermute | solution.py:66
  80.7 3.0 %constant_dynamic-update-slice_fusion.2 = (bf16[1024,1024]{1,0:T(8,128)(2,1)}, bf16[256,1024]{1,0:T(8,128)(2,1)}, bf16[1,256,1024]{2,1,0:T(8,128)(2,1)}) fusion(bf16[1024,1024]{1,0:T(8,128)(2,1)} %get-tuple-element.53, bf16[512,1024]{1,0:T(8,128)(2,1)} %hold.3, bf16[512,1024]{1,0:T(8,128)(2,1)} %collective-permute-done.3.refs_1_, pred[]{:T(512)S(6)} %lt.28), kind=kLoop, calls=%fused_computation.30 | loop fusion | flops 524288 | bytes 3670017
  89.2 6.4 %collective-permute-done.9.refs_2_.refs_3_ = bf16[512,256]{1,0:T(8,128)(2,1)S(1)} collective-permute-done((bf16[512,256]{1,0:T(8,128)(2,1)S(1)}, bf16[512,256]{1,0:T(8,128)(2,1)S(1)}, u32[]{:S(2)}, u32[]{:S(2)}) %collective-permute-start.9) | collective-permute-done | bytes 262176 | tf_op jit(solution)/shard_map/kv_hop2/ppermute | solution.py:66
  95.5 3.2 %collective-permute-done.10.refs_3_.refs_4_ = bf16[512,256]{1,0:T(8,128)(2,1)} collective-permute-done((bf16[512,256]{1,0:T(8,128)(2,1)S(1)}, bf16[512,256]{1,0:T(8,128)(2,1)}, u32[]{:S(2)}, u32[]{:S(2)}) %collective-permute-start.10) | collective-permute-done | bytes 262176 | tf_op jit(solution)/shard_map/kv_hop2/ppermute | solution.py:66
  104.5 4.0 %project_kv.1 = bf16[512,256]{1,0:T(8,128)(2,1)S(1)} custom-call(s32[4]{0:T(128)S(1)} %fusion.5.index_ref, bf16[4,512,1024]{2,1,0:T(8,128)(2,1)S(1)} %bitcast.20, bf16[1024,256]{1,0:T(8,128)(2,1)S(1)} %copy-done.12, bf16[1024,256]{1,0:T(8,128)(2,1)} %collective-permute-done.4.refs_1_, bf16[512,256]{1,0:T(8,128)(2,1)S(1)} %copy-done.17, ...), custom_call_target="tpu_custom_call" | custom-call | flops 1024 | bytes 1024 | tf_op jit(solution)/shard_map/project_kv/pallas_call | solution.py:152
  109.3 3.1 %collective-permute-start.13 = (bf16[2,272,256]{2,1,0:T(8,128)(2,1)}, bf16[2,272,256]{2,1,0:T(8,128)(2,1)}, u32[]{:S(2)}, u32[]{:S(2)}) collective-permute-start(bf16[2,272,256]{2,1,0:T(8,128)(2,1)} %pad_maximum_fusion.5.own_ref), channel_id=1, source_target_pairs={{0,8},{4,12},{1,9},{5,13},{2,10},{6,14},{3,11},{7,15},{16,24},{20,... | collective-permute-start | bytes 835592 | tf_op jit(solution)/shard_map/kv_rows/ppermute | solution.py:71
  112.4 4.7 %collective-permute-start.14 = (bf16[2,272,256]{2,1,0:T(8,128)(2,1)}, bf16[2,272,256]{2,1,0:T(8,128)(2,1)}, u32[]{:S(2)}, u32[]{:S(2)}) collective-permute-start(bf16[2,272,256]{2,1,0:T(8,128)(2,1)} %pad_maximum_fusion.5.own_ref), channel_id=1, source_target_pairs={{0,4},{4,8},{8,12},{1,5},{5,9},{9,13},{2,6},{6,10},{10,14},{3,7},{... | collective-permute-start | bytes 835592 | tf_op jit(solution)/shard_map/kv_rows/ppermute | solution.py:71
  126.5 7.7 %project_q.1.refs_2_.query_ref = bf16[512,1024]{1,0:T(8,128)(2,1)S(1)} custom-call(s32[4]{0:T(128)S(1)} %fusion.5.index_ref, bf16[4,512,1024]{2,1,0:T(8,128)(2,1)S(1)} %bitcast.21, bf16[1024,1024]{1,0:T(8,128)(2,1)S(1)} %bitcast.28, bf16[1024,1024]{1,0:T(8,128)(2,1)S(1)} %copy-done.5, bf16[1024,1024]{1,0:T(8,128)(2,1)} %collective-permute-done.1.refs_2_, ...), custom_call_target="tpu_custom_call" | custom-call | flops 1024 | bytes 1024 | tf_op jit(solution)/shard_map/project_q/pallas_call | solution.py:152
  140.8 10.3 %attend.1.mixed_ref = bf16[512,1024]{1,0:T(8,128)(2,1)S(1)} custom-call(s32[1]{0:T(128)} %bitcast.6.place_ref, bf16[512,1024]{1,0:T(8,128)(2,1)S(1)} %copy-done.7, f32[2,256,1]{2,1,0:T(8,128)S(1)} %copy-done.15, bf16[2,272,256]{2,1,0:T(8,128)(2,1)} %collective-permute-done.13.refs_1_.two_ref, bf16[2,272,256]{2,1,0:T(8,128)(2,1)} %hold.4.one_ref, ...), custom_call_target="tpu_custom_call" | custom-call | flops 1024 | bytes 1024 | tf_op jit(solution)/shard_map/attend/pallas_call | solution.py:208
  151.1 2.6 %collective-permute-done.18.back_ref = bf16[512,640]{1,0:T(8,128)(2,1)} collective-permute-done((bf16[512,640]{1,0:T(8,128)(2,1)}, bf16[512,640]{1,0:T(8,128)(2,1)}, u32[]{:S(2)}, u32[]{:S(2)}) %collective-permute-start.18) | collective-permute-done | bytes 655392 | tf_op jit(solution)/shard_map/out_hop2_0/ppermute | solution.py:66
  153.8 5.7 %spread_0.1 = (bf16[512,640]{1,0:T(8,128)(2,1)S(1)}, bf16[512,640]{1,0:T(8,128)(2,1)S(1)}, f32[512,640]{1,0:T(8,128)S(1)}, f32[512,640]{1,0:T(8,128)S(1)}) custom-call(s32[4]{0:T(128)S(1)} %and_select_fusion.1.index_ref, bf16[512,1024]{1,0:T(8,128)(2,1)S(1)} %attend.1.mixed_ref, bf16[1024,640]{1,0:T(8,128)(2,1)S(1)} %copy-done.3, ...), custom_call_target="tpu_custom_call" | custom-call | flops 1024 | bytes 1024 | tf_op jit(solution)/shard_map/spread_0/pallas_call | solution.py:247
  159.4 4.3 %collective-permute-start.20 = (bf16[512,640]{1,0:T(8,128)(2,1)S(1)}, bf16[512,640]{1,0:T(8,128)(2,1)S(1)}, u32[]{:S(2)}, u32[]{:S(2)}) collective-permute-start(bf16[512,640]{1,0:T(8,128)(2,1)S(1)} %get-tuple-element.42), channel_id=1, source_target_pairs={{0,1},{1,0},{2,3},{3,2},{4,5},{5,4},{6,7},{7,6},{8,9},{9,8},{10,11... | collective-permute-start | bytes 1966088 | tf_op jit(solution)/shard_map/core_passed_0/ppermute | solution.py:76
  167.1 15.8 %collective-permute-done.22.ahead_ref = bf16[1024,384]{1,0:T(8,128)(2,1)S(1)} collective-permute-done((bf16[1024,384]{1,0:T(8,128)(2,1)S(1)}, bf16[1024,384]{1,0:T(8,128)(2,1)S(1)}, u32[]{:S(2)}, u32[]{:S(2)}) %collective-permute-start.22) | collective-permute-done | bytes 786464 | tf_op jit(solution)/shard_map/out_hop1_1/ppermute | solution.py:66
  184.5 8.2 %collective-permute-done.23.near_ref = bf16[512,384]{1,0:T(8,128)(2,1)S(1)} collective-permute-done((bf16[512,384]{1,0:T(8,128)(2,1)S(1)}, bf16[512,384]{1,0:T(8,128)(2,1)S(1)}, u32[]{:S(2)}, u32[]{:S(2)}) %collective-permute-start.23) | collective-permute-done | bytes 393248 | tf_op jit(solution)/shard_map/out_hop2_1/ppermute | solution.py:66
  192.7 2.6 %collective-permute-done.25.back_ref = bf16[512,384]{1,0:T(8,128)(2,1)S(1)} collective-permute-done((bf16[512,384]{1,0:T(8,128)(2,1)S(1)}, bf16[512,384]{1,0:T(8,128)(2,1)S(1)}, u32[]{:S(2)}, u32[]{:S(2)}) %collective-permute-start.25) | collective-permute-done | bytes 393248 | tf_op jit(solution)/shard_map/out_hop2_1/ppermute | solution.py:66
  195.3 3.1 %spread_1.1 = (bf16[512,384]{1,0:T(8,128)(2,1)S(1)}, bf16[512,384]{1,0:T(8,128)(2,1)S(1)}, f32[512,384]{1,0:T(8,128)S(1)}, f32[512,384]{1,0:T(8,128)S(1)}) custom-call(s32[4]{0:T(128)S(1)} %and_select_fusion.1.index_ref, bf16[512,1024]{1,0:T(8,128)(2,1)S(1)} %attend.1.mixed_ref, bf16[1024,384]{1,0:T(8,128)(2,1)S(1)} %copy-done.8, ...), custom_call_target="tpu_custom_call" | custom-call | flops 1024 | bytes 1024 | tf_op jit(solution)/shard_map/spread_1/pallas_call | solution.py:247
  204.1 19.4 %collective-permute-done.28 = bf16[512,384]{1,0:T(8,128)(2,1)S(1)} collective-permute-done((bf16[512,384]{1,0:T(8,128)(2,1)S(1)}, bf16[512,384]{1,0:T(8,128)(2,1)S(1)}, u32[]{:S(2)}, u32[]{:S(2)}) %collective-permute-start.28) | collective-permute-done | bytes 393248 | tf_op jit(solution)/shard_map/z_sum_1/ppermute | solution.py:76
  (141 shorter events, 61.0 us)
Async XLA Ops:
  0.6 47.2 %collective-permute-start = (bf16[1024,1024]{1,0:T(8,128)(2,1)}, bf16[1024,1024]{1,0:T(8,128)(2,1)S(1)}, u32[]{:S(2)}, u32[]{:S(2)}) collective-permute-start(bf16[1024,1024]{1,0:T(8,128)(2,1)} %bitcast.26), channel_id=1, source_target_pairs={{4,0},{8,4},{12,8},{0,12},{5,1},{9,5},{13,9},{1,13},{6,2},{10,6},{... | collective-permute-start | bytes 6291464 | tf_op jit(solution)/shard_map/q_hop1/ppermute | solution.py:66
  3.2 47.7 %collective-permute-start.1 = (bf16[1024,1024]{1,0:T(8,128)(2,1)}, bf16[1024,1024]{1,0:T(8,128)(2,1)}, u32[]{:S(2)}, u32[]{:S(2)}) collective-permute-start(bf16[1024,1024]{1,0:T(8,128)(2,1)} %bitcast.27), channel_id=1, source_target_pairs={{12,0},{0,4},{4,8},{8,12},{13,1},{1,5},{5,9},{9,13},{14,2},{2,6},{... | collective-permute-start | bytes 6291464 | tf_op jit(solution)/shard_map/q_hop1/ppermute | solution.py:66
  5.5 48.9 %collective-permute-start.2 = (bf16[512,1024]{1,0:T(8,128)(2,1)}, bf16[512,1024]{1,0:T(8,128)(2,1)}, u32[]{:S(2)}, u32[]{:S(2)}) collective-permute-start(bf16[512,1024]{1,0:T(8,128)(2,1)} %pad_maximum_fusion), channel_id=1, source_target_pairs={{128,0},{129,1},{144,16},{145,17},{160,32},{161,33},{176,48},{177,... | collective-permute-start | bytes 3145736 | tf_op jit(solution)/shard_map/z_in/ppermute | solution.py:61
  10.6 49.3 %collective-permute-start.3 = (bf16[512,1024]{1,0:T(8,128)(2,1)}, bf16[512,1024]{1,0:T(8,128)(2,1)}, u32[]{:S(2)}, u32[]{:S(2)}) collective-permute-start(bf16[512,1024]{1,0:T(8,128)(2,1)} %pad_maximum_fusion), channel_id=1, source_target_pairs={{130,0},{131,1},{146,16},{147,17},{162,32},{163,33},{178,48},{179,... | collective-permute-start | bytes 3145736 | tf_op jit(solution)/shard_map/z_in/ppermute | solution.py:61
  50.9 15.0 %collective-permute-start.4 = (bf16[1024,256]{1,0:T(8,128)(2,1)S(1)}, bf16[1024,256]{1,0:T(8,128)(2,1)}, u32[]{:S(2)}, u32[]{:S(2)}) collective-permute-start(bf16[1024,256]{1,0:T(8,128)(2,1)S(1)} %pad_maximum_fusion.2.refs_0_), channel_id=1, source_target_pairs={{4,0},{8,4},{12,8},{0,12},{5,1},{9,5},{13,9},{1,13},{6,2},{10,6},{... | collective-permute-start | bytes 1572872 | tf_op jit(solution)/shard_map/kv_hop1/ppermute | solution.py:66
  51.2 14.7 %collective-permute-start.5 = (bf16[1024,256]{1,0:T(8,128)(2,1)S(1)}, bf16[1024,256]{1,0:T(8,128)(2,1)}, u32[]{:S(2)}, u32[]{:S(2)}) collective-permute-start(bf16[1024,256]{1,0:T(8,128)(2,1)S(1)} %pad_maximum_fusion.2.refs_0_), channel_id=1, source_target_pairs={{12,0},{0,4},{4,8},{8,12},{13,1},{1,5},{5,9},{9,13},{14,2},{2,6},{... | collective-permute-start | bytes 1572872 | tf_op jit(solution)/shard_map/kv_hop1/ppermute | solution.py:66
  65.9 32.9 %collective-permute-start.11 = (bf16[512,1024]{1,0:T(8,128)(2,1)}, bf16[512,1024]{1,0:T(8,128)(2,1)}, u32[]{:S(2)}, u32[]{:S(2)}) collective-permute-start(bf16[512,1024]{1,0:T(8,128)(2,1)} %slice.84), channel_id=1, source_target_pairs={{4,0},{8,4},{12,8},{0,12},{5,1},{9,5},{13,9},{1,13},{6,2},{10,6},{... | collective-permute-start | bytes 3145736 | tf_op jit(solution)/shard_map/q_hop2/ppermute | solution.py:66
  68.5 30.3 %collective-permute-start.12 = (bf16[512,1024]{1,0:T(8,128)(2,1)}, bf16[512,1024]{1,0:T(8,128)(2,1)}, u32[]{:S(2)}, u32[]{:S(2)}) collective-permute-start(bf16[512,1024]{1,0:T(8,128)(2,1)} %slice.85), channel_id=1, source_target_pairs={{12,0},{0,4},{4,8},{8,12},{13,1},{1,5},{5,9},{9,13},{14,2},{2,6},{... | collective-permute-start | bytes 3145736 | tf_op jit(solution)/shard_map/q_hop2/ppermute | solution.py:66
  72.4 14.1 %collective-permute-start.7 = (bf16[128,1024]{1,0:T(8,128)(2,1)S(1)}, bf16[128,1024]{1,0:T(8,128)(2,1)S(1)}, u32[]{:S(2)}, u32[]{:S(2)}) collective-permute-start(bf16[128,1024]{1,0:T(8,128)(2,1)S(1)} %slice.87), channel_id=1, source_target_pairs={{130,0},{131,1},{146,16},{147,17},{162,32},{163,33},{178,48},{179,... | collective-permute-start | bytes 786440 | tf_op jit(solution)/shard_map/far/ppermute | solution.py:61
  73.4 22.2 %collective-permute-start.9 = (bf16[512,256]{1,0:T(8,128)(2,1)S(1)}, bf16[512,256]{1,0:T(8,128)(2,1)S(1)}, u32[]{:S(2)}, u32[]{:S(2)}) collective-permute-start(bf16[512,256]{1,0:T(8,128)(2,1)S(1)} %slice.70), channel_id=1, source_target_pairs={{4,0},{8,4},{12,8},{0,12},{5,1},{9,5},{13,9},{1,13},{6,2},{10,6},{... | collective-permute-start | bytes 786440 | tf_op jit(solution)/shard_map/kv_hop2/ppermute | solution.py:66
  80.7 18.0 %collective-permute-start.10 = (bf16[512,256]{1,0:T(8,128)(2,1)S(1)}, bf16[512,256]{1,0:T(8,128)(2,1)}, u32[]{:S(2)}, u32[]{:S(2)}) collective-permute-start(bf16[512,256]{1,0:T(8,128)(2,1)S(1)} %slice.71), channel_id=1, source_target_pairs={{12,0},{0,4},{4,8},{8,12},{13,1},{1,5},{5,9},{9,13},{14,2},{2,6},{... | collective-permute-start | bytes 786440 | tf_op jit(solution)/shard_map/kv_hop2/ppermute | solution.py:66
  87.2 15.1 %collective-permute-start.8 = (bf16[1024,1024]{1,0:T(8,128)(2,1)}, bf16[1024,1024]{1,0:T(8,128)(2,1)S(1)}, u32[]{:S(2)}, u32[]{:S(2)}) collective-permute-start(bf16[1024,1024]{1,0:T(8,128)(2,1)} %constant_dynamic-update-slice_fusion), channel_id=1, source_target_pairs={{0,1},{1,0},{2,3},{3,2},{4,5},{5,4},{6,7},{7,6},{8,9},{9,8},{10,11... | collective-permute-start | bytes 6291464 | tf_op jit(solution)/shard_map/sib/ppermute | solution.py:76
  98.8 36.5 %collective-permute-start.15 = (bf16[1024,640]{1,0:T(8,128)(2,1)}, bf16[1024,640]{1,0:T(8,128)(2,1)}, u32[]{:S(2)}, u32[]{:S(2)}) collective-permute-start(bf16[1024,640]{1,0:T(8,128)(2,1)} %hold.5.own_ref), channel_id=1, source_target_pairs={{4,0},{8,4},{12,8},{0,12},{5,1},{9,5},{13,9},{1,13},{6,2},{10,6},{... | collective-permute-start | bytes 3932168 | tf_op jit(solution)/shard_map/out_hop1_0/ppermute | solution.py:66
  99.7 37.6 %collective-permute-start.17 = (bf16[1024,640]{1,0:T(8,128)(2,1)}, bf16[1024,640]{1,0:T(8,128)(2,1)}, u32[]{:S(2)}, u32[]{:S(2)}) collective-permute-start(bf16[1024,640]{1,0:T(8,128)(2,1)} %hold.5.own_ref), channel_id=1, source_target_pairs={{12,0},{0,4},{4,8},{8,12},{13,1},{1,5},{5,9},{9,13},{14,2},{2,6},{... | collective-permute-start | bytes 3932168 | tf_op jit(solution)/shard_map/out_hop1_0/ppermute | solution.py:66
  109.3 31.5 %collective-permute-start.13 = (bf16[2,272,256]{2,1,0:T(8,128)(2,1)}, bf16[2,272,256]{2,1,0:T(8,128)(2,1)}, u32[]{:S(2)}, u32[]{:S(2)}) collective-permute-start(bf16[2,272,256]{2,1,0:T(8,128)(2,1)} %pad_maximum_fusion.5.own_ref), channel_id=1, source_target_pairs={{0,8},{4,12},{1,9},{5,13},{2,10},{6,14},{3,11},{7,15},{16,24},{20,... | collective-permute-start | bytes 835592 | tf_op jit(solution)/shard_map/kv_rows/ppermute | solution.py:71
  112.4 28.3 %collective-permute-start.14 = (bf16[2,272,256]{2,1,0:T(8,128)(2,1)}, bf16[2,272,256]{2,1,0:T(8,128)(2,1)}, u32[]{:S(2)}, u32[]{:S(2)}) collective-permute-start(bf16[2,272,256]{2,1,0:T(8,128)(2,1)} %pad_maximum_fusion.5.own_ref), channel_id=1, source_target_pairs={{0,4},{4,8},{8,12},{1,5},{5,9},{9,13},{2,6},{6,10},{10,14},{3,7},{... | collective-permute-start | bytes 835592 | tf_op jit(solution)/shard_map/kv_rows/ppermute | solution.py:71
  137.3 13.8 %collective-permute-start.16 = (bf16[512,640]{1,0:T(8,128)(2,1)}, bf16[512,640]{1,0:T(8,128)(2,1)S(1)}, u32[]{:S(2)}, u32[]{:S(2)}) collective-permute-start(bf16[512,640]{1,0:T(8,128)(2,1)} %slice.92), channel_id=1, source_target_pairs={{4,0},{8,4},{12,8},{0,12},{5,1},{9,5},{13,9},{1,13},{6,2},{10,6},{... | collective-permute-start | bytes 1966088 | tf_op jit(solution)/shard_map/out_hop2_0/ppermute | solution.py:66
  139.3 14.5 %collective-permute-start.18 = (bf16[512,640]{1,0:T(8,128)(2,1)}, bf16[512,640]{1,0:T(8,128)(2,1)}, u32[]{:S(2)}, u32[]{:S(2)}) collective-permute-start(bf16[512,640]{1,0:T(8,128)(2,1)} %slice.93), channel_id=1, source_target_pairs={{12,0},{0,4},{4,8},{8,12},{13,1},{1,5},{5,9},{9,13},{14,2},{2,6},{... | collective-permute-start | bytes 1966088 | tf_op jit(solution)/shard_map/out_hop2_0/ppermute | solution.py:66
  163.7 19.1 %collective-permute-start.22 = (bf16[1024,384]{1,0:T(8,128)(2,1)S(1)}, bf16[1024,384]{1,0:T(8,128)(2,1)S(1)}, u32[]{:S(2)}, u32[]{:S(2)}) collective-permute-start(bf16[1024,384]{1,0:T(8,128)(2,1)S(1)} %copy-done.8), channel_id=1, source_target_pairs={{4,0},{8,4},{12,8},{0,12},{5,1},{9,5},{13,9},{1,13},{6,2},{10,6},{... | collective-permute-start | bytes 2359304 | tf_op jit(solution)/shard_map/out_hop1_1/ppermute | solution.py:66
  163.7 20.6 %collective-permute-start.24 = (bf16[1024,384]{1,0:T(8,128)(2,1)S(1)}, bf16[1024,384]{1,0:T(8,128)(2,1)S(1)}, u32[]{:S(2)}, u32[]{:S(2)}) collective-permute-start(bf16[1024,384]{1,0:T(8,128)(2,1)S(1)} %copy-done.8), channel_id=1, source_target_pairs={{12,0},{0,4},{4,8},{8,12},{13,1},{1,5},{5,9},{9,13},{14,2},{2,6},{... | collective-permute-start | bytes 2359304 | tf_op jit(solution)/shard_map/out_hop1_1/ppermute | solution.py:66
  165.2 33.2 %collective-permute-start.19 = (bf16[512,640]{1,0:T(8,128)(2,1)S(1)}, bf16[512,640]{1,0:T(8,128)(2,1)S(1)}, u32[]{:S(2)}, u32[]{:S(2)}) collective-permute-start(bf16[512,640]{1,0:T(8,128)(2,1)S(1)} %get-tuple-element.40), channel_id=1, source_target_pairs={{0,1},{1,0},{2,3},{3,2},{4,5},{5,4},{6,7},{7,6},{8,9},{9,8},{10,11... | collective-permute-start | bytes 1966088 | tf_op jit(solution)/shard_map/core_kept_0/ppermute | solution.py:76
  166.0 32.6 %collective-permute-start.21 = (bf16[512,640]{1,0:T(8,128)(2,1)S(1)}, bf16[512,640]{1,0:T(8,128)(2,1)S(1)}, u32[]{:S(2)}, u32[]{:S(2)}) collective-permute-start(bf16[512,640]{1,0:T(8,128)(2,1)S(1)} %add_convert_fusion.1), channel_id=1, source_target_pairs={{0,2},{1,3},{2,0},{3,1},{4,6},{5,7},{6,4},{7,5},{8,10},{9,11},{10,... | collective-permute-start | bytes 1966088 | tf_op jit(solution)/shard_map/z_sum_0/ppermute | solution.py:76
  184.4 10.9 %collective-permute-start.25 = (bf16[512,384]{1,0:T(8,128)(2,1)S(1)}, bf16[512,384]{1,0:T(8,128)(2,1)S(1)}, u32[]{:S(2)}, u32[]{:S(2)}) collective-permute-start(bf16[512,384]{1,0:T(8,128)(2,1)S(1)} %slice.95), channel_id=1, source_target_pairs={{12,0},{0,4},{4,8},{8,12},{13,1},{1,5},{5,9},{9,13},{14,2},{2,6},{... | collective-permute-start | bytes 1179656 | tf_op jit(solution)/shard_map/out_hop2_1/ppermute | solution.py:66
  202.2 21.4 %collective-permute-start.28 = (bf16[512,384]{1,0:T(8,128)(2,1)S(1)}, bf16[512,384]{1,0:T(8,128)(2,1)S(1)}, u32[]{:S(2)}, u32[]{:S(2)}) collective-permute-start(bf16[512,384]{1,0:T(8,128)(2,1)S(1)} %add_convert_fusion.3), channel_id=1, source_target_pairs={{0,2},{1,3},{2,0},{3,1},{4,6},{5,7},{6,4},{7,5},{8,10},{9,11},{10,... | collective-permute-start | bytes 1179656 | tf_op jit(solution)/shard_map/z_sum_1/ppermute | solution.py:76
  (31 other events, 224.7 us)
